TPU v7x, 512 devices: a whole 4x4x16 slice. The times are simulated.
512 devices in a mesh: view: 16 (over z_lo, y), tile: 32 (over x, z_hi, core).
Axes of the slice: x: 4, y: 4, z: 16 (z_hi: 4, z_lo: 4; z = z_hi * 4 + z_lo), core: 2. Of those that a mesh axis runs over, the one named last changes fastest.
Arguments:
- estimate: float32 [256, 256, 128], P('tile', 'view'), may hold values from 0.5 to 1.5
- images: float32 [16, 256, 256, 128], P('view', 'tile'), may hold values from 0.25 to 4
- taps_first: float32 [16, 5], P('view'), may hold values from 0.1 to 1
- taps_second: float32 [16, 7], P('view'), may hold values from 0.1 to 1
- taps_axial: float32 [16, 33], P('view'), may hold values from 0.02 to 0.2
Outputs:
- deconvolved: float32 [256, 256, 128], P('tile', 'view')
All inputs are finite; a program needn't handle non-finite values.
Results may differ from a plain program's by a relative error of at most 0.0001.
Values sent between devices are 32-bit elements; how exact they have to be, the bound alone decides.
No kernel may reach another device: no remote copies, remote signals or barrier semaphores. Data moves between devices by JAX's collectives and lax.ppermute only.
A program may use at most 64 MiB of HBM per device.

v0:
```python
import jax
import jax.numpy as jnp
from jax import lax
from jax.sharding import PartitionSpec as P

ITERS = 2


def extended(cells, sides, width):
    for axis, dim in sides:
        count = lax.axis_size(axis)
        ends = count - 1
        head = lax.slice_in_dim(cells, 0, width, axis=dim)
        tail = lax.slice_in_dim(cells, cells.shape[dim] - width, cells.shape[dim], axis=dim)
        cells = jnp.concatenate(
            [
                lax.ppermute(tail, axis, [(i, (i + 1) % count) for i in range(ends)]),
                cells,
                lax.ppermute(head, axis, [((i + 1) % count, i) for i in range(ends)]),
            ],
            axis=dim,
        )
    return cells


def toeplitz(taps, length, radius):
    index = jnp.arange(length, dtype=jnp.int32)
    offset = index[None, :] - index[:, None] + radius
    count = taps.shape[0]
    onehot = (offset[None, :, :] == jnp.arange(count, dtype=jnp.int32)[:, None, None]).astype(
        jnp.float32
    )
    return jnp.sum(onehot * taps[:, None, None], axis=0)


def along_axial(field, matrix):
    flat = field.reshape(-1, field.shape[2])
    out = jnp.dot(flat, matrix, precision=lax.Precision.HIGHEST, preferred_element_type=jnp.float32)
    return out.reshape(field.shape)


def along_second(field, taps, reverse):
    count = taps.shape[0]
    radius = (count - 1) // 2
    length = field.shape[1]
    padded = jnp.pad(field, ((0, 0), (radius, radius), (0, 0)))
    total = jnp.zeros(field.shape, jnp.float32)
    for tap in range(count):
        start = tap if reverse else 2 * radius - tap
        total = total + taps[tap] * padded[:, start : start + length, :]
    return total


def along_first(padded, taps, reverse):
    count = taps.shape[0]
    radius = (count - 1) // 2
    length = padded.shape[0] - 2 * radius
    total = jnp.zeros((length,) + padded.shape[1:], jnp.float32)
    for tap in range(count):
        start = tap if reverse else 2 * radius - tap
        total = total + taps[tap] * padded[start : start + length]
    return total


def spread(piece):
    return lax.all_gather(piece, "view", axis=1, tiled=True)


def local(estimate, images, taps_first, taps_second, taps_axial):
    first = taps_first[0]
    second = taps_second[0]
    axial = taps_axial[0]
    image = images[0]
    radius = (first.shape[0] - 1) // 2
    matrix = toeplitz(axial, estimate.shape[2], (axial.shape[0] - 1) // 2)
    views = lax.axis_size("view")
    width = estimate.shape[1]
    current = spread(estimate)
    for step in range(ITERS):
        inner = along_second(along_axial(current, matrix), second, False)
        blurred = along_first(extended(inner, (("tile", 0),), radius), first, False)
        ratio = image / blurred
        inner = along_second(along_axial(ratio, matrix.T), second, True)
        total = along_first(extended(inner, (("tile", 0),), radius), first, True)
        current = current * (lax.psum(total, "view") / views)
    own = lax.dynamic_slice_in_dim(current, lax.axis_index("view") * width, width, 1)
    return own


def solution(mesh):
    in_specs = (
        P("tile", "view", None),
        P("view", "tile", None, None),
        P("view", None),
        P("view", None),
        P("view", None),
    )
    out_specs = P("tile", "view", None)
    return jax.shard_map(local, mesh=mesh, in_specs=in_specs, out_specs=out_specs, check_vma=False)
```

profile of v0, /device:TPU:2, one launch (start us, length us, event | category | flops | bytes accessed | tf_op | source)
XLA Modules:
  0.0 563.0 jit_solution(5084498150551239331)
XLA Ops:
  9.8 90.1 %all-gather.2.cloned.1.call-done = f32[8,256,128]{2,1,0:T(8,128)} async-done(((f32[8,16,128]{2,1,0:T(8,128)}), f32[8,256,128]{2,1,0:T(8,128)}) %all-gather.2.cloned.1.call-update) | async-done | bytes 1048592 | tf_op jit(solution)/shard_map/all_gather | solution.py:66
  99.9 2.3 convolution_bitcast_fusion
  102.5 5.0 multiply_add_fusion.3
  107.7 2.1 collective-permute-start
  109.7 2.4 collective-permute-start.1
  112.8 3.1 collective-permute-done
  115.9 10.1 %collective-permute-done.1 = f32[2,256,128]{2,1,0:T(8,128)S(1)} collective-permute-done((f32[2,256,128]{2,1,0:T(8,128)S(1)}, f32[2,256,128]{2,1,0:T(8,128)S(1)}, u32[]{:S(2)}, u32[]{:S(2)}) %collective-permute-start.1) | collective-permute-done | bytes 262176 | tf_op jit(solution)/shard_map/ppermute | solution.py:17
  126.0 4.4 fusion.54
  130.5 5.0 multiply_add_fusion.2
  137.5 8.4 %collective-permute-start.3 = (f32[2,256,128]{2,1,0:T(8,128)S(1)}, f32[2,256,128]{2,1,0:T(8,128)S(1)}, u32[]{:S(2)}, u32[]{:S(2)}) collective-permute-start(f32[2,256,128]{2,1,0:T(8,128)S(1)} %get-tuple-element.10), channel_id=1, source_target_pairs={{1,0},{2,1},{3,2},{4,3},{5,4},{6,5},{7,6},{8,7},{9,8},{10,9},{11,1... | collective-permute-start | bytes 786440 | tf_op jit(solution)/shard_map/ppermute | solution.py:19
  146.0 4.2 collective-permute-done.2
  151.9 4.5 fusion.20
  156.4 171.3 %all-reduce.7.cloned.1.call-done = f32[8,256,128]{2,1,0:T(8,128)} async-done(((f32[8,256,128]{2,1,0:T(8,128)}), f32[8,256,128]{2,1,0:T(8,128)}) %all-reduce.7.cloned.1.call-update) | async-done | bytes 1048592 | tf_op jit(solution)/shard_map/psum | solution.py:85
  330.1 5.0 multiply_add_fusion.1
  337.1 2.4 collective-permute-start.5
  339.5 4.1 collective-permute-done.4
  343.6 9.3 %collective-permute-done.5 = f32[2,256,128]{2,1,0:T(8,128)S(1)} collective-permute-done((f32[2,256,128]{2,1,0:T(8,128)S(1)}, f32[2,256,128]{2,1,0:T(8,128)S(1)}, u32[]{:S(2)}, u32[]{:S(2)}) %collective-permute-start.5) | collective-permute-done | bytes 262176 | tf_op jit(solution)/shard_map/ppermute | solution.py:17
  352.9 4.4 fusion.56
  357.3 5.0 multiply_add_fusion
  364.3 8.4 %collective-permute-start.7 = (f32[2,256,128]{2,1,0:T(8,128)S(1)}, f32[2,256,128]{2,1,0:T(8,128)S(1)}, u32[]{:S(2)}, u32[]{:S(2)}) collective-permute-start(f32[2,256,128]{2,1,0:T(8,128)S(1)} %get-tuple-element.6), channel_id=1, source_target_pairs={{1,0},{2,1},{3,2},{4,3},{5,4},{6,5},{7,6},{8,7},{9,8},{10,9},{11,1... | collective-permute-start | bytes 786440 | tf_op jit(solution)/shard_map/ppermute | solution.py:19
  372.8 3.8 collective-permute-done.6
  376.6 3.8 collective-permute-done.7
  380.4 4.5 fusion.3
  384.9 170.1 %all-reduce.9.cloned.1.call-done = f32[8,256,128]{2,1,0:T(8,128)} async-done(((f32[8,256,128]{2,1,0:T(8,128)}), f32[8,256,128]{2,1,0:T(8,128)}) %all-reduce.9.cloned.1.call-update) | async-done | bytes 1048592 | tf_op jit(solution)/shard_map/psum | solution.py:85
  (28 shorter events, 15.7 us)
Async XLA Ops:
  6.5 93.4 %all-gather.2.cloned.1.call-start = ((), (), s32[]{:S(2)}) async-start(), calls=%async_computation | async-start | bytes 1114112 | tf_op jit(solution)/shard_map/all_gather | solution.py:66
  7.3 320.5 %all-reduce.7.cloned.1.call-start = ((), (), s32[]{:S(2)}) async-start(), calls=%async_computation.1 | async-start | bytes 2097152 | tf_op jit(solution)/shard_map/psum | solution.py:85
  107.6 4.5 copy-start.1
  107.6 18.4 %copy-start.2 = (f32[1,8,256,128]{3,2,1,0:T(8,128)S(1)}, f32[1,8,256,128]{3,2,1,0:T(8,128)}, u32[]{:S(2)}) copy-start(f32[1,8,256,128]{3,2,1,0:T(8,128)} %param.6) | copy-start | bytes 3145732
  107.7 8.3 %collective-permute-start = (f32[2,256,128]{2,1,0:T(8,128)S(1)}, f32[2,256,128]{2,1,0:T(8,128)S(1)}, u32[]{:S(2)}, u32[]{:S(2)}) collective-permute-start(f32[2,256,128]{2,1,0:T(8,128)S(1)} %get-tuple-element.11), channel_id=1, source_target_pairs={{1,0},{2,1},{3,2},{4,3},{5,4},{6,5},{7,6},{8,7},{9,8},{10,9},{11,1... | collective-permute-start | bytes 786440 | tf_op jit(solution)/shard_map/ppermute | solution.py:19
  109.7 16.3 %collective-permute-start.1 = (f32[2,256,128]{2,1,0:T(8,128)S(1)}, f32[2,256,128]{2,1,0:T(8,128)S(1)}, u32[]{:S(2)}, u32[]{:S(2)}) collective-permute-start(f32[2,256,128]{2,1,0:T(8,128)S(1)} %get-tuple-element.12), channel_id=1, source_target_pairs={{0,1},{1,2},{2,3},{3,4},{4,5},{5,6},{6,7},{7,8},{8,9},{9,10},{10,1... | collective-permute-start | bytes 786440 | tf_op jit(solution)/shard_map/ppermute | solution.py:17
  135.6 14.6 %collective-permute-start.2 = (f32[2,256,128]{2,1,0:T(8,128)S(1)}, f32[2,256,128]{2,1,0:T(8,128)S(1)}, u32[]{:S(2)}, u32[]{:S(2)}) collective-permute-start(f32[2,256,128]{2,1,0:T(8,128)S(1)} %get-tuple-element.9), channel_id=1, source_target_pairs={{0,1},{1,2},{2,3},{3,4},{4,5},{5,6},{6,7},{7,8},{8,9},{9,10},{10,1... | collective-permute-start | bytes 786440 | tf_op jit(solution)/shard_map/ppermute | solution.py:17
  137.5 14.4 %collective-permute-start.3 = (f32[2,256,128]{2,1,0:T(8,128)S(1)}, f32[2,256,128]{2,1,0:T(8,128)S(1)}, u32[]{:S(2)}, u32[]{:S(2)}) collective-permute-start(f32[2,256,128]{2,1,0:T(8,128)S(1)} %get-tuple-element.10), channel_id=1, source_target_pairs={{1,0},{2,1},{3,2},{4,3},{5,4},{6,5},{7,6},{8,7},{9,8},{10,9},{11,1... | collective-permute-start | bytes 786440 | tf_op jit(solution)/shard_map/ppermute | solution.py:19
  156.4 171.4 %copy-start = (f32[8,256,128]{2,1,0:T(8,128)S(1)}, f32[8,256,128]{2,1,0:T(8,128)}, u32[]{:S(2)}) copy-start(f32[8,256,128]{2,1,0:T(8,128)} %all-gather.2.cloned.1.call-done) | copy-start | bytes 3145732
  156.4 398.6 %all-reduce.9.cloned.1.call-start = ((), (), s32[]{:S(2)}) async-start(), calls=%async_computation.2 | async-start | bytes 2097152 | tf_op jit(solution)/shard_map/psum | solution.py:85
  335.2 8.4 %collective-permute-start.4 = (f32[2,256,128]{2,1,0:T(8,128)S(1)}, f32[2,256,128]{2,1,0:T(8,128)S(1)}, u32[]{:S(2)}, u32[]{:S(2)}) collective-permute-start(f32[2,256,128]{2,1,0:T(8,128)S(1)} %get-tuple-element.7), channel_id=1, source_target_pairs={{1,0},{2,1},{3,2},{4,3},{5,4},{6,5},{7,6},{8,7},{9,8},{10,9},{11,1... | collective-permute-start | bytes 786440 | tf_op jit(solution)/shard_map/ppermute | solution.py:19
  337.1 15.8 %collective-permute-start.5 = (f32[2,256,128]{2,1,0:T(8,128)S(1)}, f32[2,256,128]{2,1,0:T(8,128)S(1)}, u32[]{:S(2)}, u32[]{:S(2)}) collective-permute-start(f32[2,256,128]{2,1,0:T(8,128)S(1)} %get-tuple-element.8), channel_id=1, source_target_pairs={{0,1},{1,2},{2,3},{3,4},{4,5},{5,6},{6,7},{7,8},{8,9},{9,10},{10,1... | collective-permute-start | bytes 786440 | tf_op jit(solution)/shard_map/ppermute | solution.py:17
  362.4 14.2 %collective-permute-start.6 = (f32[2,256,128]{2,1,0:T(8,128)S(1)}, f32[2,256,128]{2,1,0:T(8,128)S(1)}, u32[]{:S(2)}, u32[]{:S(2)}) collective-permute-start(f32[2,256,128]{2,1,0:T(8,128)S(1)} %get-tuple-element.5), channel_id=1, source_target_pairs={{0,1},{1,2},{2,3},{3,4},{4,5},{5,6},{6,7},{7,8},{8,9},{9,10},{10,1... | collective-permute-start | bytes 786440 | tf_op jit(solution)/shard_map/ppermute | solution.py:17
  364.3 16.1 %collective-permute-start.7 = (f32[2,256,128]{2,1,0:T(8,128)S(1)}, f32[2,256,128]{2,1,0:T(8,128)S(1)}, u32[]{:S(2)}, u32[]{:S(2)}) collective-permute-start(f32[2,256,128]{2,1,0:T(8,128)S(1)} %get-tuple-element.6), channel_id=1, source_target_pairs={{1,0},{2,1},{3,2},{4,3},{5,4},{6,5},{7,6},{8,7},{9,8},{10,9},{11,1... | collective-permute-start | bytes 786440 | tf_op jit(solution)/shard_map/ppermute | solution.py:19
Sparse Core Ops, SparseCore 0:
  9.4 90.4 all-gather.1
  156.5 171.2 all-reduce.6
  385.0 169.9 all-reduce.8
where the time goes:
time: 564 us; the launch traced here: 563 us
  waiting for transfers between devices  472 us (84%)
  other arithmetic  32.9 us (6%)
  starting transfers between devices  29.6 us (5%)
  between operations  13.3 us (2%)
  matrix products  12.1 us (2%)
    psum x2, waiting for transfers between devices, local(): current = current * (lax.psum(total, 'view') / views)  341 us
    all_gather x1, waiting for transfers between devices, spread(): return lax.all_gather(piece, 'view', axis=1, tiled=True)  90.1 us
    ppermute x4, waiting for transfers between devices, extended(): lax.ppermute(tail, axis, [(i, (i + 1) % count) for i in range(ends)])  27.3 us
    ppermute x4, starting transfers between devices, extended(): lax.ppermute(head, axis, [((i + 1) % count, i) for i in range(ends)])  20.9 us
    add x4, other arithmetic, along_second(): total = total + taps[tap] * padded[:, start:start + length, :]  20.2 us
    ppermute x4, waiting for transfers between devices, extended(): lax.ppermute(head, axis, [((i + 1) % count, i) for i in range(ends)])  12.8 us
    dot_general x4, matrix products, along_axial(): jnp.dot(flat, matrix, precision=lax.Precision.HIGHEST, preferred_element_...  12.1 us
  transfers between devices with their start and end apart: 11, of which 11 were waited for; matrix products, arithmetic and copies ran while one was open for 1% of the time, Pallas kernels for 0%

commit v1 on v0

v1 whole, which is shorter than its diff:
```python
import functools

import jax
import jax.numpy as jnp
from jax import lax
from jax.experimental import pallas as pl
from jax.experimental.pallas import tpu as pltpu
from jax.sharding import PartitionSpec as P

ITERS = 2
LANES = 128
COLS = 24


def split(x):
    high = x.astype(jnp.bfloat16)
    low = (x - high.astype(jnp.float32)).astype(jnp.bfloat16)
    return high, low


def product(x, m_high, m_low):
    x_high, x_low = split(x)
    dot = functools.partial(jnp.dot, preferred_element_type=jnp.float32)
    return dot(x_high, m_high) + (dot(x_high, m_low) + dot(x_low, m_high))


def banded(row, radius):
    full = jnp.broadcast_to(row, (LANES, LANES))
    rolled = pltpu.roll(full, LANES - radius, 1, stride=1, stride_axis=0)
    z = lax.broadcasted_iota(jnp.int32, (LANES, LANES), 0)
    zz = lax.broadcasted_iota(jnp.int32, (LANES, LANES), 1)
    return jnp.where(jnp.abs(zz - z) <= radius, rolled, 0.0)


def edges(flag, low, high):
    even = flag == 0
    return jnp.where(even, high, low), jnp.where(even, low, high)


def views_pass(sizes, flags, est_ref, data_ref, part_ref, near_ref, far_ref, shifted, spread):
    nf, ns, rz = sizes
    rows, cols, halo_x = 8, 16, nf - 1
    wide = rows + halo_x
    views = data_ref.shape[0]
    for k in range(ns):
        shifted[k] = est_ref[:, k : k + cols, :]

    def one(v, carry):
        taps = data_ref[v, rows * cols : rows * cols + 8, :]
        first = [jnp.broadcast_to(taps[2:3, i : i + 1], (cols, LANES)) for i in range(nf)]
        second = [
            jnp.broadcast_to(taps[2:3, nf + i : nf + i + 1], (cols, LANES)) for i in range(ns)
        ]
        conv = split(banded(taps[0:1], rz))
        corr = split(banded(taps[1:2], rz))
        a = []
        for i in range(wide):
            t = second[0] * shifted[ns - 1, i]
            for k in range(1, ns):
                t = t + second[k] * shifted[ns - 1 - k, i]
            a.append(t)
        b = []
        for i in range(rows):
            t = first[0] * a[i + nf - 1]
            for k in range(1, nf):
                t = t + first[k] * a[i + nf - 1 - k]
            b.append(t)
        blurred = product(jnp.concatenate(b, axis=0), *conv)
        ratio = data_ref[v, 0 : rows * cols, :] / blurred
        back = product(ratio, *corr)
        for i in range(wide):
            t = None
            for k in range(nf):
                j = i - (nf - 1) + k
                if 0 <= j < rows:
                    u = first[k] * back[j * cols : (j + 1) * cols]
                    t = u if t is None else t + u
            spread[v, i] = t
        return carry

    lax.fori_loop(0, views, one, 0)

    part_ref[...] = jnp.zeros_like(part_ref)

    def row(i, carry):
        sums = [None] * ns
        for v in range(views):
            taps = data_ref[v, rows * cols + 2 : rows * cols + 3, :]
            g = spread[v, i]
            for k in range(ns):
                u = jnp.broadcast_to(taps[:, nf + ns - 1 - k : nf + ns - k], (cols, LANES)) * g
                sums[k] = u if sums[k] is None else sums[k] + u
        for k in range(ns):
            part_ref[i, k : k + cols, :] += sums[k]
        return carry

    lax.fori_loop(0, wide, row, 0)
    near_ref[...], far_ref[...] = edges(
        flags[0], part_ref[0:halo_x], part_ref[wide - halo_x : wide]
    )


def pass_kernel(sizes, flags, est_ref, data_ref, part_ref, near_ref, far_ref, shifted, spread):
    views_pass(sizes, flags, est_ref, data_ref, part_ref, near_ref, far_ref, shifted, spread)


def update_kernel(sizes, views, flags, est_ref, total_ref, yn_ref, yf_ref, data_ref, new_ref, part_ref, near_ref, far_ref, shifted, spread):
    even = flags[1] == 0
    low = jnp.where(even, yf_ref[...], yn_ref[...])
    high = jnp.where(even, yn_ref[...], yf_ref[...])
    new_ref[:, 0:8, :] = est_ref[:, 0:8, :] * ((total_ref[:, 0:8, :] + low) / views)
    new_ref[:, 8:16, :] = est_ref[:, 8:16, :] * (total_ref[:, 8:16, :] / views)
    new_ref[:, 16:24, :] = est_ref[:, 16:24, :] * ((total_ref[:, 16:24, :] + high) / views)
    views_pass(sizes, flags, new_ref, data_ref, part_ref, near_ref, far_ref, shifted, spread)


def rows_kernel(flags, part_ref, near_ref, far_ref, out_ref, yn_ref, yf_ref):
    wide, halo = part_ref.shape[0], near_ref.shape[0]
    even = flags[0] == 0
    near, far = near_ref[...], far_ref[...]
    out_ref[0:halo] = part_ref[0:halo] + jnp.where(even, far, near)
    out_ref[halo : wide - halo] = part_ref[halo : wide - halo]
    out_ref[wide - halo : wide] = part_ref[wide - halo : wide] + jnp.where(even, near, far)
    yn_ref[...], yf_ref[...] = edges(flags[1], out_ref[:, 0:8, :], out_ref[:, 16:24, :])


def final_kernel(views, lo_x, lo_y, flags, est_ref, total_ref, yn_ref, yf_ref, out_ref, sums):
    even = flags[1] == 0
    low = jnp.where(even, yf_ref[...], yn_ref[...])
    high = jnp.where(even, yn_ref[...], yf_ref[...])
    sums[:, 0:8, :] = est_ref[:, 0:8, :] * ((total_ref[:, 0:8, :] + low) / views)
    sums[:, 8:16, :] = est_ref[:, 8:16, :] * (total_ref[:, 8:16, :] / views)
    sums[:, 16:24, :] = est_ref[:, 16:24, :] * ((total_ref[:, 16:24, :] + high) / views)
    out_ref[...] = sums[lo_x : lo_x + 8, lo_y : lo_y + 16, :]


def pairs(count, start):
    out = []
    for i in range(start, count - 1, 2):
        out += [(i, i + 1), (i + 1, i)]
    return out


def swapped(near, far, axis):
    count = lax.axis_size(axis)
    far = lax.ppermute(far, axis, pairs(count, 1))
    near = lax.ppermute(near, axis, pairs(count, 0))
    return near, far


VMEM = pl.BlockSpec(memory_space=pltpu.VMEM)
SMEM = pl.BlockSpec(memory_space=pltpu.SMEM)


def call(kernel, ins, shapes, scratch=(), cost=None):
    return pl.pallas_call(
        kernel,
        in_specs=[SMEM] + [VMEM] * (len(ins) - 1),
        out_specs=[VMEM] * len(shapes),
        out_shape=[jax.ShapeDtypeStruct(s, jnp.float32) for s in shapes],
        scratch_shapes=list(scratch),
        cost_estimate=cost,
    )(*ins)


def local(estimate, images, taps_first, taps_second, taps_axial):
    nf, ns, nz = taps_first.shape[1], taps_second.shape[1], taps_axial.shape[1]
    sizes = (nf, ns, (nz - 1) // 2)
    views = lax.axis_size("view")
    rows, cols, lanes = estimate.shape
    wide = rows + nf - 1
    halo = nf - 1
    flags = jnp.stack(
        [lax.axis_index("tile") % 2, lax.axis_index("view") % 2]
    ).astype(jnp.int32)

    own = jnp.pad(estimate, ((nf // 2, nf // 2), (ns // 2, COLS - cols - ns // 2), (0, 0)))
    near, far = edges(flags[0], own[0:halo], own[wide - halo :])
    near, far = swapped(near, far, "tile")

    pieces = images[0].reshape(rows, views, cols, lanes).transpose(1, 0, 2, 3)
    pieces = pieces.reshape(views, rows * cols, lanes)
    pad = lambda x: jnp.pad(x, ((0, 0), (0, lanes - x.shape[1])))
    taps = jnp.concatenate(
        [
            pad(taps_axial),
            pad(taps_axial[:, ::-1]),
            pad(jnp.concatenate([taps_first, taps_second], axis=1)),
            jnp.zeros((5, lanes), jnp.float32),
        ],
        axis=0,
    )
    data = jnp.concatenate([pieces, jnp.broadcast_to(taps[None], (views, 8, lanes))], axis=1)
    data = lax.all_to_all(data, "view", 0, 0, tiled=True)

    block, strip, side = (wide, COLS, lanes), (halo, COLS, lanes), (wide, 8, lanes)
    scratch = [
        pltpu.VMEM((ns, wide, cols, lanes), jnp.float32),
        pltpu.VMEM((views, wide, cols, lanes), jnp.float32),
    ]

    def joined(part, near, far):
        total, yn, yf = call(rows_kernel, (flags, part, near, far), (block, side, side))
        yn, yf = swapped(yn, yf, "view")
        return total, yn, yf

    total, yn, yf = joined(own, near, far)
    even = flags[1] == 0
    low, high = jnp.where(even, yf, yn), jnp.where(even, yn, yf)
    current = jnp.concatenate(
        [total[:, 0:8] + low, total[:, 8:16], total[:, 16:24] + high], axis=1
    )
    part, near, far = call(
        functools.partial(pass_kernel, sizes), (flags, current, data), (block, strip, strip), scratch
    )
    for step in range(1, ITERS):
        near, far = swapped(near, far, "tile")
        total, yn, yf = joined(part, near, far)
        current, part, near, far = call(
            functools.partial(update_kernel, sizes, views),
            (flags, current, total, yn, yf, data),
            (block, block, strip, strip),
            scratch,
        )
    near, far = swapped(near, far, "tile")
    total, yn, yf = joined(part, near, far)
    (out,) = call(
        functools.partial(final_kernel, views, nf // 2, ns // 2),
        (flags, current, total, yn, yf),
        ((rows, cols, lanes),),
        [pltpu.VMEM(block, jnp.float32)],
    )
    return out


def solution(mesh):
    in_specs = (
        P("tile", "view", None),
        P("view", "tile", None, None),
        P("view", None),
        P("view", None),
        P("view", None),
    )
    out_specs = P("tile", "view", None)
    return jax.shard_map(local, mesh=mesh, in_specs=in_specs, out_specs=out_specs, check_vma=False)
```

time: 564 us -> 144 us (0.26)
  the two profiles are of different devices: /device:TPU:2 before, /device:TPU:70 now
where the time goes in v1:
time: 144 us; the launch traced here: 143 us
  starting transfers between devices  58.6 us (41%)
  waiting for transfers between devices  39.5 us (27%)
  Pallas kernels  33.9 us (24%)
  local copies, waits for them, and re-layouts  7.6 us (5%)
  other arithmetic  3.36 us (2%)
    ppermute x6, starting transfers between devices, swapped(): far = lax.ppermute(far, axis, pairs(count, 1))  38.2 us
    pallas_call x6, Pallas kernels, call(): pl.pallas_call(kernel, in_specs=[SMEM] + [VMEM] * (len(ins) - 1), out_spe...  33.9 us
    ppermute x6, waiting for transfers between devices, swapped(): far = lax.ppermute(far, axis, pairs(count, 1))  32.9 us
    ppermute x6, starting transfers between devices, swapped(): near = lax.ppermute(near, axis, pairs(count, 0))  12 us
    all_to_all x1, starting transfers between devices, local(): data = lax.all_to_all(data, 'view', 0, 0, tiled=True)  8.33 us
    ppermute x6, waiting for transfers between devices, swapped(): near = lax.ppermute(near, axis, pairs(count, 0))  6.6 us
    unnamed x30, local copies, waits for them, and re-layouts  4.72 us
  transfers between devices with their start and end apart: 13, of which 9 were waited for; matrix products, arithmetic and copies ran while one was open for 2% of the time, Pallas kernels for 1%

profile of v1, /device:TPU:70, one launch (start us, length us, event | category | flops | bytes accessed | tf_op | source)
XLA Modules:
  0.0 143.2 jit_solution(14938627828536600480)
XLA Ops:
  3.5 8.3 %all-to-all-start = ((f32[16,136,128]{2,1,0:T(8,128)}), f32[16,136,128]{2,1,0:T(8,128)S(1)}, u32[]{:S(2)}, u32[]{:S(2)}) async-start(f32[16,136,128]{2,1,0:T(8,128)} %pad_maximum_fusion), calls=%async_computation | async-start | bytes 2228224 | tf_op jit(solution)/shard_map/all_to_all | solution.py:194
  11.9 9.2 %collective-permute-start.1 = (f32[4,24,128]{2,1,0:T(8,128)S(1)}, f32[4,24,128]{2,1,0:T(8,128)S(1)}, u32[]{:S(2)}, u32[]{:S(2)}) collective-permute-start(f32[4,24,128]{2,1,0:T(8,128)S(1)} %get-tuple-element.40), channel_id=1, source_target_pairs={{1,2},{2,1},{3,4},{4,3},{5,6},{6,5},{7,8},{8,7},{9,10},{10,9},{11,... | collective-permute-start | bytes 147464 | tf_op jit(solution)/shard_map/ppermute | solution.py:146
  21.0 1.9 %collective-permute-start = (f32[4,24,128]{2,1,0:T(8,128)S(1)}, f32[4,24,128]{2,1,0:T(8,128)S(1)}, u32[]{:S(2)}, u32[]{:S(2)}) collective-permute-start(f32[4,24,128]{2,1,0:T(8,128)S(1)} %get-tuple-element.41), channel_id=1, source_target_pairs={{0,1},{1,0},{2,3},{3,2},{4,5},{5,4},{6,7},{7,6},{8,9},{9,8},{10,11... | collective-permute-start | bytes 147464 | tf_op jit(solution)/shard_map/ppermute | solution.py:147
  24.2 13.5 %collective-permute-done.1.far_ref = f32[4,24,128]{2,1,0:T(8,128)S(1)} collective-permute-done((f32[4,24,128]{2,1,0:T(8,128)S(1)}, f32[4,24,128]{2,1,0:T(8,128)S(1)}, u32[]{:S(2)}, u32[]{:S(2)}) %collective-permute-start.1) | collective-permute-done | bytes 49184 | tf_op jit(solution)/shard_map/ppermute | solution.py:146
  39.0 1.7 %shard_map.55 = (f32[12,24,128]{2,1,0:T(8,128)}, f32[12,8,128]{2,1,0:T(8,128)}, f32[12,8,128]{2,1,0:T(8,128)}) custom-call(s32[2]{0:T(128)} %pad_add_fusion.flags, f32[12,24,128]{2,1,0:T(8,128)} %pad.15.part_ref, f32[4,24,128]{2,1,0:T(8,128)} %copy-done.5, f32[4,24,128]{2,1,0:T(8,128)} %copy-done.4), custom_call_target="tpu_custom_call" | custom-call | tf_op jit(solution)/shard_map/pallas_call | solution.py:156
  40.6 13.1 %collective-permute-start.2 = (f32[12,8,128]{2,1,0:T(8,128)}, f32[12,8,128]{2,1,0:T(8,128)S(1)}, u32[]{:S(2)}, u32[]{:S(2)}) collective-permute-start(f32[12,8,128]{2,1,0:T(8,128)} %get-tuple-element.22), channel_id=1, source_target_pairs={{32,64},{64,32},{96,128},{128,96},{160,192},{192,160},{224,256},{2... | collective-permute-start | bytes 147464 | tf_op jit(solution)/shard_map/ppermute | solution.py:146
  53.7 1.9 %collective-permute-start.3 = (f32[12,8,128]{2,1,0:T(8,128)}, f32[12,8,128]{2,1,0:T(8,128)S(1)}, u32[]{:S(2)}, u32[]{:S(2)}) collective-permute-start(f32[12,8,128]{2,1,0:T(8,128)} %get-tuple-element.23), channel_id=1, source_target_pairs={{0,32},{32,0},{64,96},{96,64},{128,160},{160,128},{192,224},{224,1... | collective-permute-start | bytes 147464 | tf_op jit(solution)/shard_map/ppermute | solution.py:147
  56.0 3.9 %collective-permute-done.3 = f32[12,8,128]{2,1,0:T(8,128)S(1)} collective-permute-done((f32[12,8,128]{2,1,0:T(8,128)}, f32[12,8,128]{2,1,0:T(8,128)S(1)}, u32[]{:S(2)}, u32[]{:S(2)}) %collective-permute-start.3) | collective-permute-done | bytes 49184 | tf_op jit(solution)/shard_map/ppermute | solution.py:147
  62.5 13.5 %shard_map.56 = (f32[12,24,128]{2,1,0:T(8,128)}, f32[4,24,128]{2,1,0:T(8,128)}, f32[4,24,128]{2,1,0:T(8,128)}) custom-call(s32[2]{0:T(128)} %pad_add_fusion.flags, f32[12,24,128]{2,1,0:T(8,128)} %pad_maximum_fusion.1.est_ref, f32[16,136,128]{2,1,0:T(8,128)} %copy-done), custom_call_target="tpu_custom_call" | custom-call | tf_op jit(solution)/shard_map/pallas_call | solution.py:156
  76.0 1.9 %collective-permute-start.4 = (f32[4,24,128]{2,1,0:T(8,128)}, f32[4,24,128]{2,1,0:T(8,128)S(1)}, u32[]{:S(2)}, u32[]{:S(2)}) collective-permute-start(f32[4,24,128]{2,1,0:T(8,128)} %get-tuple-element.25), channel_id=1, source_target_pairs={{0,1},{1,0},{2,3},{3,2},{4,5},{5,4},{6,7},{7,6},{8,9},{9,8},{10,11... | collective-permute-start | bytes 147464 | tf_op jit(solution)/shard_map/ppermute | solution.py:147
  77.9 5.6 %collective-permute-start.5 = (f32[4,24,128]{2,1,0:T(8,128)}, f32[4,24,128]{2,1,0:T(8,128)S(1)}, u32[]{:S(2)}, u32[]{:S(2)}) collective-permute-start(f32[4,24,128]{2,1,0:T(8,128)} %get-tuple-element.26), channel_id=1, source_target_pairs={{1,2},{2,1},{3,4},{4,3},{5,6},{6,5},{7,8},{8,7},{9,10},{10,9},{11,... | collective-permute-start | bytes 147464 | tf_op jit(solution)/shard_map/ppermute | solution.py:146
  83.5 4.8 %collective-permute-done.5.far_ref = f32[4,24,128]{2,1,0:T(8,128)S(1)} collective-permute-done((f32[4,24,128]{2,1,0:T(8,128)}, f32[4,24,128]{2,1,0:T(8,128)S(1)}, u32[]{:S(2)}, u32[]{:S(2)}) %collective-permute-start.5) | collective-permute-done | bytes 49184 | tf_op jit(solution)/shard_map/ppermute | solution.py:146
  90.6 2.4 %collective-permute-start.6 = (f32[12,8,128]{2,1,0:T(8,128)}, f32[12,8,128]{2,1,0:T(8,128)S(1)}, u32[]{:S(2)}, u32[]{:S(2)}) collective-permute-start(f32[12,8,128]{2,1,0:T(8,128)} %get-tuple-element.28), channel_id=1, source_target_pairs={{0,32},{32,0},{64,96},{96,64},{128,160},{160,128},{192,224},{224,1... | collective-permute-start | bytes 147464 | tf_op jit(solution)/shard_map/ppermute | solution.py:147
  93.0 2.8 %collective-permute-start.7 = (f32[12,8,128]{2,1,0:T(8,128)}, f32[12,8,128]{2,1,0:T(8,128)S(1)}, u32[]{:S(2)}, u32[]{:S(2)}) collective-permute-start(f32[12,8,128]{2,1,0:T(8,128)} %get-tuple-element.29), channel_id=1, source_target_pairs={{32,64},{64,32},{96,128},{128,96},{160,192},{192,160},{224,256},{2... | collective-permute-start | bytes 147464 | tf_op jit(solution)/shard_map/ppermute | solution.py:146
  96.8 4.6 %collective-permute-done.7.yf_ref = f32[12,8,128]{2,1,0:T(8,128)S(1)} collective-permute-done((f32[12,8,128]{2,1,0:T(8,128)}, f32[12,8,128]{2,1,0:T(8,128)S(1)}, u32[]{:S(2)}, u32[]{:S(2)}) %collective-permute-start.7) | collective-permute-done | bytes 49184 | tf_op jit(solution)/shard_map/ppermute | solution.py:146
  102.0 13.8 %shard_map.58 = (f32[12,24,128]{2,1,0:T(8,128)}, f32[12,24,128]{2,1,0:T(8,128)}, f32[4,24,128]{2,1,0:T(8,128)}, f32[4,24,128]{2,1,0:T(8,128)}) custom-call(s32[2]{0:T(128)} %pad_add_fusion.flags, f32[12,24,128]{2,1,0:T(8,128)} %pad_maximum_fusion.1.est_ref, f32[12,24,128]{2,1,0:T(8,128)} %get-tuple-element.27.total_ref, f32[12,8,128]{2,1,0:T(8,128)} %copy-done.2, ...), custom_call_target="tpu_custom_call" | custom-call | tf_op jit(solution)/shard_map/pallas_call | solution.py:156
  115.7 1.9 %collective-permute-start.8 = (f32[4,24,128]{2,1,0:T(8,128)}, f32[4,24,128]{2,1,0:T(8,128)S(1)}, u32[]{:S(2)}, u32[]{:S(2)}) collective-permute-start(f32[4,24,128]{2,1,0:T(8,128)} %get-tuple-element.32), channel_id=1, source_target_pairs={{0,1},{1,0},{2,3},{3,2},{4,5},{5,4},{6,7},{7,6},{8,9},{9,8},{10,11... | collective-permute-start | bytes 147464 | tf_op jit(solution)/shard_map/ppermute | solution.py:147
  117.6 5.1 %collective-permute-start.9 = (f32[4,24,128]{2,1,0:T(8,128)}, f32[4,24,128]{2,1,0:T(8,128)S(1)}, u32[]{:S(2)}, u32[]{:S(2)}) collective-permute-start(f32[4,24,128]{2,1,0:T(8,128)} %get-tuple-element.33), channel_id=1, source_target_pairs={{1,2},{2,1},{3,4},{4,3},{5,6},{6,5},{7,8},{8,7},{9,10},{10,9},{11,... | collective-permute-start | bytes 147464 | tf_op jit(solution)/shard_map/ppermute | solution.py:146
  122.8 5.6 %collective-permute-done.9.far_ref = f32[4,24,128]{2,1,0:T(8,128)S(1)} collective-permute-done((f32[4,24,128]{2,1,0:T(8,128)}, f32[4,24,128]{2,1,0:T(8,128)S(1)}, u32[]{:S(2)}, u32[]{:S(2)}) %collective-permute-start.9) | collective-permute-done | bytes 49184 | tf_op jit(solution)/shard_map/ppermute | solution.py:146
  129.0 1.7 %shard_map.59 = (f32[12,24,128]{2,1,0:T(8,128)}, f32[12,8,128]{2,1,0:T(8,128)}, f32[12,8,128]{2,1,0:T(8,128)}) custom-call(s32[2]{0:T(128)} %pad_add_fusion.flags, f32[12,24,128]{2,1,0:T(8,128)} %get-tuple-element.31.part_ref, f32[4,24,128]{2,1,0:T(8,128)} %copy-done.8, f32[4,24,128]{2,1,0:T(8,128)} %copy-done.11), custom_call_target="tpu_custom_call" | custom-call | tf_op jit(solution)/shard_map/pallas_call | solution.py:156
  130.7 1.9 %collective-permute-start.10 = (f32[12,8,128]{2,1,0:T(8,128)}, f32[12,8,128]{2,1,0:T(8,128)S(1)}, u32[]{:S(2)}, u32[]{:S(2)}) collective-permute-start(f32[12,8,128]{2,1,0:T(8,128)} %get-tuple-element.35), channel_id=1, source_target_pairs={{0,32},{32,0},{64,96},{96,64},{128,160},{160,128},{192,224},{224,1... | collective-permute-start | bytes 147464 | tf_op jit(solution)/shard_map/ppermute | solution.py:147
  132.6 2.6 %collective-permute-start.11 = (f32[12,8,128]{2,1,0:T(8,128)}, f32[12,8,128]{2,1,0:T(8,128)S(1)}, u32[]{:S(2)}, u32[]{:S(2)}) collective-permute-start(f32[12,8,128]{2,1,0:T(8,128)} %get-tuple-element.36), channel_id=1, source_target_pairs={{32,64},{64,32},{96,128},{128,96},{160,192},{192,160},{224,256},{2... | collective-permute-start | bytes 147464 | tf_op jit(solution)/shard_map/ppermute | solution.py:146
  135.2 1.7 %collective-permute-done.10.yn_ref = f32[12,8,128]{2,1,0:T(8,128)S(1)} collective-permute-done((f32[12,8,128]{2,1,0:T(8,128)}, f32[12,8,128]{2,1,0:T(8,128)S(1)}, u32[]{:S(2)}, u32[]{:S(2)}) %collective-permute-start.10) | collective-permute-done | bytes 49184 | tf_op jit(solution)/shard_map/ppermute | solution.py:147
  136.9 4.0 %collective-permute-done.11.yf_ref = f32[12,8,128]{2,1,0:T(8,128)S(1)} collective-permute-done((f32[12,8,128]{2,1,0:T(8,128)}, f32[12,8,128]{2,1,0:T(8,128)S(1)}, u32[]{:S(2)}, u32[]{:S(2)}) %collective-permute-start.11) | collective-permute-done | bytes 49184 | tf_op jit(solution)/shard_map/ppermute | solution.py:146
  (51 shorter events, 15.6 us)
Async XLA Ops:
  0.0 2.3 %copy-start.12 = (f32[1,33]{1,0:T(1,128)S(1)}, f32[1,33]{1,0:T(1,128)}, u32[]{:S(2)}) copy-start(f32[1,33]{1,0:T(1,128)} %param.9) | copy-start | bytes 400
  0.0 2.2 %copy-start.13 = (f32[1,7]{1,0:T(1,128)S(1)}, f32[1,7]{1,0:T(1,128)}, u32[]{:S(2)}) copy-start(f32[1,7]{1,0:T(1,128)} %param.8) | copy-start | bytes 88
  0.0 2.2 %copy-start.14 = (f32[1,5]{1,0:T(1,128)S(1)}, f32[1,5]{1,0:T(1,128)}, u32[]{:S(2)}) copy-start(f32[1,5]{1,0:T(1,128)} %param.7) | copy-start | bytes 64
  3.5 8.3 %copy-start.1 = (f32[8,16,128]{2,1,0:T(8,128)S(1)}, f32[8,16,128]{2,1,0:T(8,128)}, u32[]{:S(2)}) copy-start(f32[8,16,128]{2,1,0:T(8,128)} %param.5) | copy-start | bytes 196612
  3.5 58.0 %all-to-all-start = ((f32[16,136,128]{2,1,0:T(8,128)}), f32[16,136,128]{2,1,0:T(8,128)S(1)}, u32[]{:S(2)}, u32[]{:S(2)}) async-start(f32[16,136,128]{2,1,0:T(8,128)} %pad_maximum_fusion), calls=%async_computation | async-start | bytes 2228224 | tf_op jit(solution)/shard_map/all_to_all | solution.py:194
  11.9 25.9 %collective-permute-start.1 = (f32[4,24,128]{2,1,0:T(8,128)S(1)}, f32[4,24,128]{2,1,0:T(8,128)S(1)}, u32[]{:S(2)}, u32[]{:S(2)}) collective-permute-start(f32[4,24,128]{2,1,0:T(8,128)S(1)} %get-tuple-element.40), channel_id=1, source_target_pairs={{1,2},{2,1},{3,4},{4,3},{5,6},{6,5},{7,8},{8,7},{9,10},{10,9},{11,... | collective-permute-start | bytes 147464 | tf_op jit(solution)/shard_map/ppermute | solution.py:146
  21.0 16.7 %collective-permute-start = (f32[4,24,128]{2,1,0:T(8,128)S(1)}, f32[4,24,128]{2,1,0:T(8,128)S(1)}, u32[]{:S(2)}, u32[]{:S(2)}) collective-permute-start(f32[4,24,128]{2,1,0:T(8,128)S(1)} %get-tuple-element.41), channel_id=1, source_target_pairs={{0,1},{1,0},{2,3},{3,2},{4,5},{5,4},{6,7},{7,6},{8,9},{9,8},{10,11... | collective-permute-start | bytes 147464 | tf_op jit(solution)/shard_map/ppermute | solution.py:147
  38.3 0.6 copy-start.5
  40.6 15.3 %collective-permute-start.2 = (f32[12,8,128]{2,1,0:T(8,128)}, f32[12,8,128]{2,1,0:T(8,128)S(1)}, u32[]{:S(2)}, u32[]{:S(2)}) collective-permute-start(f32[12,8,128]{2,1,0:T(8,128)} %get-tuple-element.22), channel_id=1, source_target_pairs={{32,64},{64,32},{96,128},{128,96},{160,192},{192,160},{224,256},{2... | collective-permute-start | bytes 147464 | tf_op jit(solution)/shard_map/ppermute | solution.py:146
  53.7 6.2 %collective-permute-start.3 = (f32[12,8,128]{2,1,0:T(8,128)}, f32[12,8,128]{2,1,0:T(8,128)S(1)}, u32[]{:S(2)}, u32[]{:S(2)}) collective-permute-start(f32[12,8,128]{2,1,0:T(8,128)} %get-tuple-element.23), channel_id=1, source_target_pairs={{0,32},{32,0},{64,96},{96,64},{128,160},{160,128},{192,224},{224,1... | collective-permute-start | bytes 147464 | tf_op jit(solution)/shard_map/ppermute | solution.py:147
  61.5 1.0 copy-start
  76.0 7.5 %collective-permute-start.4 = (f32[4,24,128]{2,1,0:T(8,128)}, f32[4,24,128]{2,1,0:T(8,128)S(1)}, u32[]{:S(2)}, u32[]{:S(2)}) collective-permute-start(f32[4,24,128]{2,1,0:T(8,128)} %get-tuple-element.25), channel_id=1, source_target_pairs={{0,1},{1,0},{2,3},{3,2},{4,5},{5,4},{6,7},{7,6},{8,9},{9,8},{10,11... | collective-permute-start | bytes 147464 | tf_op jit(solution)/shard_map/ppermute | solution.py:147
  77.9 10.4 %collective-permute-start.5 = (f32[4,24,128]{2,1,0:T(8,128)}, f32[4,24,128]{2,1,0:T(8,128)S(1)}, u32[]{:S(2)}, u32[]{:S(2)}) collective-permute-start(f32[4,24,128]{2,1,0:T(8,128)} %get-tuple-element.26), channel_id=1, source_target_pairs={{1,2},{2,1},{3,4},{4,3},{5,6},{6,5},{7,8},{8,7},{9,10},{10,9},{11,... | collective-permute-start | bytes 147464 | tf_op jit(solution)/shard_map/ppermute | solution.py:146
  83.5 4.9 %copy-start.6 = (f32[4,24,128]{2,1,0:T(8,128)}, f32[4,24,128]{2,1,0:T(8,128)S(1)}, u32[]{:S(2)}) copy-start(f32[4,24,128]{2,1,0:T(8,128)S(1)} %collective-permute-done.4.near_ref) | copy-start | bytes 147460
  90.6 6.2 %collective-permute-start.6 = (f32[12,8,128]{2,1,0:T(8,128)}, f32[12,8,128]{2,1,0:T(8,128)S(1)}, u32[]{:S(2)}, u32[]{:S(2)}) collective-permute-start(f32[12,8,128]{2,1,0:T(8,128)} %get-tuple-element.28), channel_id=1, source_target_pairs={{0,32},{32,0},{64,96},{96,64},{128,160},{160,128},{192,224},{224,1... | collective-permute-start | bytes 147464 | tf_op jit(solution)/shard_map/ppermute | solution.py:147
  93.0 8.3 %collective-permute-start.7 = (f32[12,8,128]{2,1,0:T(8,128)}, f32[12,8,128]{2,1,0:T(8,128)S(1)}, u32[]{:S(2)}, u32[]{:S(2)}) collective-permute-start(f32[12,8,128]{2,1,0:T(8,128)} %get-tuple-element.29), channel_id=1, source_target_pairs={{32,64},{64,32},{96,128},{128,96},{160,192},{192,160},{224,256},{2... | collective-permute-start | bytes 147464 | tf_op jit(solution)/shard_map/ppermute | solution.py:146
  96.8 4.6 %copy-start.2 = (f32[12,8,128]{2,1,0:T(8,128)}, f32[12,8,128]{2,1,0:T(8,128)S(1)}, u32[]{:S(2)}) copy-start(f32[12,8,128]{2,1,0:T(8,128)S(1)} %collective-permute-done.6.yn_ref) | copy-start | bytes 147460
  101.3 0.6 copy-start.3
  115.7 7.0 %collective-permute-start.8 = (f32[4,24,128]{2,1,0:T(8,128)}, f32[4,24,128]{2,1,0:T(8,128)S(1)}, u32[]{:S(2)}, u32[]{:S(2)}) collective-permute-start(f32[4,24,128]{2,1,0:T(8,128)} %get-tuple-element.32), channel_id=1, source_target_pairs={{0,1},{1,0},{2,3},{3,2},{4,5},{5,4},{6,7},{7,6},{8,9},{9,8},{10,11... | collective-permute-start | bytes 147464 | tf_op jit(solution)/shard_map/ppermute | solution.py:147
  117.6 10.8 %collective-permute-start.9 = (f32[4,24,128]{2,1,0:T(8,128)}, f32[4,24,128]{2,1,0:T(8,128)S(1)}, u32[]{:S(2)}, u32[]{:S(2)}) collective-permute-start(f32[4,24,128]{2,1,0:T(8,128)} %get-tuple-element.33), channel_id=1, source_target_pairs={{1,2},{2,1},{3,4},{4,3},{5,6},{6,5},{7,8},{8,7},{9,10},{10,9},{11,... | collective-permute-start | bytes 147464 | tf_op jit(solution)/shard_map/ppermute | solution.py:146
  122.7 5.7 %copy-start.8 = (f32[4,24,128]{2,1,0:T(8,128)}, f32[4,24,128]{2,1,0:T(8,128)S(1)}, u32[]{:S(2)}) copy-start(f32[4,24,128]{2,1,0:T(8,128)S(1)} %collective-permute-done.8.near_ref) | copy-start | bytes 147460
  130.7 6.2 %collective-permute-start.10 = (f32[12,8,128]{2,1,0:T(8,128)}, f32[12,8,128]{2,1,0:T(8,128)S(1)}, u32[]{:S(2)}, u32[]{:S(2)}) collective-permute-start(f32[12,8,128]{2,1,0:T(8,128)} %get-tuple-element.35), channel_id=1, source_target_pairs={{0,32},{32,0},{64,96},{96,64},{128,160},{160,128},{192,224},{224,1... | collective-permute-start | bytes 147464 | tf_op jit(solution)/shard_map/ppermute | solution.py:147
  132.6 8.3 %collective-permute-start.11 = (f32[12,8,128]{2,1,0:T(8,128)}, f32[12,8,128]{2,1,0:T(8,128)S(1)}, u32[]{:S(2)}, u32[]{:S(2)}) collective-permute-start(f32[12,8,128]{2,1,0:T(8,128)} %get-tuple-element.36), channel_id=1, source_target_pairs={{32,64},{64,32},{96,128},{128,96},{160,192},{192,160},{224,256},{2... | collective-permute-start | bytes 147464 | tf_op jit(solution)/shard_map/ppermute | solution.py:146
  136.9 4.0 %copy-start.7 = (f32[12,8,128]{2,1,0:T(8,128)}, f32[12,8,128]{2,1,0:T(8,128)S(1)}, u32[]{:S(2)}) copy-start(f32[12,8,128]{2,1,0:T(8,128)S(1)} %collective-permute-done.10.yn_ref) | copy-start | bytes 147460
  (4 other events, 2.5 us)

commit v2 on v1

v2 whole, which is shorter than its diff:
```python
import functools

import jax
import jax.numpy as jnp
from jax import lax
from jax.experimental import pallas as pl
from jax.experimental.pallas import tpu as pltpu
from jax.sharding import PartitionSpec as P

ITERS = 2
LANES = 128
COLS = 24
ROWS, WIDTH = 8, 16


def split(x):
    high = x.astype(jnp.bfloat16)
    low = (x - high.astype(jnp.float32)).astype(jnp.bfloat16)
    return high, low


def stacked(x):
    high, low = split(x)
    return jnp.concatenate([high, low, high], axis=1)


def banded(row, radius):
    full = jnp.broadcast_to(row, (LANES, LANES))
    rolled = pltpu.roll(full, LANES - radius, 1, stride=1, stride_axis=0)
    z = lax.broadcasted_iota(jnp.int32, (LANES, LANES), 0)
    zz = lax.broadcasted_iota(jnp.int32, (LANES, LANES), 1)
    return jnp.where(jnp.abs(zz - z) <= radius, rolled, 0.0)


def edges(flag, low, high):
    even = flag == 0
    return jnp.where(even, high, low), jnp.where(even, low, high)


def tables_kernel(radius, count, flags, taps_ref, conv_ref, corr_ref, table_ref):
    lane = lax.broadcasted_iota(jnp.int32, (16, LANES), 1)
    sub = lax.broadcasted_iota(jnp.int32, (16, LANES), 0)

    def one(v, carry):
        taps = taps_ref[pl.ds(8 * v, 8), :]
        for row, ref in ((0, conv_ref), (1, corr_ref)):
            high, low = split(banded(taps[row : row + 1], radius))
            ref[v, 0:LANES] = high
            ref[v, LANES : 2 * LANES] = high
            ref[v, 2 * LANES : 3 * LANES] = low
        picked = jnp.where(lane == sub, jnp.broadcast_to(taps[2:3], (16, LANES)), 0.0)
        column = jnp.broadcast_to(jnp.sum(picked, axis=1, keepdims=True), (16, LANES))
        for k in range(count):
            table_ref[v, k] = jnp.broadcast_to(column[k : k + 1], (8, LANES))
        return carry

    lax.fori_loop(0, table_ref.shape[0], one, 0)


def conv_part(sizes, est_ref, conv_ref, table_ref, spread, finish):
    nf, ns = sizes
    wide, views = est_ref.shape[0], conv_ref.shape[0]

    def row(i, carry):
        shifted = [
            [est_ref[i, k + 8 * h : k + 8 * h + 8, :] for h in range(2)] for k in range(ns)
        ]
        for v in range(views):
            taps = [table_ref[v, nf + ns - 1 - k] for k in range(ns)]
            for h in range(2):
                t = taps[0] * shifted[0][h]
                for k in range(1, ns):
                    t = t + taps[k] * shifted[k][h]
                spread[v, i, 8 * h : 8 * h + 8, :] = t
        return carry

    lax.fori_loop(0, wide, row, 0)

    def one(v, carry):
        first = [table_ref[v, k] for k in range(nf)]
        out = []
        for i in range(ROWS):
            for h in range(2):
                t = first[0] * spread[v, i + nf - 1, 8 * h : 8 * h + 8, :]
                for k in range(1, nf):
                    t = t + first[k] * spread[v, i + nf - 1 - k, 8 * h : 8 * h + 8, :]
                out.append(t)
        x = stacked(jnp.concatenate(out, axis=0))
        finish(v, jnp.dot(x, conv_ref[v], preferred_element_type=jnp.float32))
        return carry

    lax.fori_loop(0, views, one, 0, unroll=2)


def corr_part(sizes, flags, ratio_of, corr_ref, table_ref, spread, part_ref, near_ref, far_ref):
    nf, ns = sizes
    wide, views = spread.shape[1], spread.shape[0]

    def one(v, carry):
        first = [table_ref[v, k] for k in range(nf)]
        back = jnp.dot(stacked(ratio_of(v)), corr_ref[v], preferred_element_type=jnp.float32)
        for i in range(wide):
            for h in range(2):
                t = None
                for k in range(nf):
                    j = i - (nf - 1) + k
                    if 0 <= j < ROWS:
                        at = j * WIDTH + 8 * h
                        u = first[k] * back[at : at + 8]
                        t = u if t is None else t + u
                spread[v, i, 8 * h : 8 * h + 8, :] = t
        return carry

    lax.fori_loop(0, views, one, 0, unroll=2)

    def row(i, carry):
        sums = [[None, None] for _ in range(ns)]
        for v in range(views):
            g = [spread[v, i, 8 * h : 8 * h + 8, :] for h in range(2)]
            for k in range(ns):
                tap = table_ref[v, nf + ns - 1 - k]
                for h in range(2):
                    u = tap * g[h]
                    sums[k][h] = u if sums[k][h] is None else sums[k][h] + u
        total = None
        for k in range(ns):
            t = jnp.concatenate(sums[k] + [jnp.zeros((8, LANES), jnp.float32)], axis=0)
            t = pltpu.roll(t, k, 0) if k else t
            total = t if total is None else total + t
        part_ref[i] = total
        return carry

    lax.fori_loop(0, wide, row, 0)
    halo = nf - 1
    near_ref[...], far_ref[...] = edges(
        flags[0], part_ref[0:halo], part_ref[wide - halo : wide]
    )


def sides(flags, yn_ref, yf_ref):
    even = flags[1] == 0
    yn, yf = yn_ref[...], yf_ref[...]
    return jnp.where(even, yf, yn), jnp.where(even, yn, yf)


def first_conv_kernel(sizes, flags, total_ref, yn_ref, yf_ref, conv_ref, table_ref, est_ref, blurred_ref, spread):
    low, high = sides(flags, yn_ref, yf_ref)
    est_ref[:, 0:8, :] = total_ref[:, 0:8, :] + low
    est_ref[:, 8:16, :] = total_ref[:, 8:16, :]
    est_ref[:, 16:24, :] = total_ref[:, 16:24, :] + high

    def finish(v, blurred):
        blurred_ref[v] = blurred

    conv_part(sizes, est_ref, conv_ref, table_ref, spread, finish)


def first_corr_kernel(sizes, flags, data_ref, blurred_ref, corr_ref, table_ref, part_ref, near_ref, far_ref, spread):
    corr_part(
        sizes, flags, lambda v: data_ref[v] / blurred_ref[v],
        corr_ref, table_ref, spread, part_ref, near_ref, far_ref,
    )


def updated(views, flags, est_ref, total_ref, yn_ref, yf_ref, new_ref):
    low, high = sides(flags, yn_ref, yf_ref)
    new_ref[:, 0:8, :] = est_ref[:, 0:8, :] * ((total_ref[:, 0:8, :] + low) / views)
    new_ref[:, 8:16, :] = est_ref[:, 8:16, :] * (total_ref[:, 8:16, :] / views)
    new_ref[:, 16:24, :] = est_ref[:, 16:24, :] * ((total_ref[:, 16:24, :] + high) / views)


def pass_kernel(sizes, views, flags, est_ref, total_ref, yn_ref, yf_ref, data_ref, conv_ref, corr_ref, table_ref, new_ref, part_ref, near_ref, far_ref, spread, ratio):
    updated(views, flags, est_ref, total_ref, yn_ref, yf_ref, new_ref)

    def finish(v, blurred):
        ratio[v] = data_ref[v] / blurred

    conv_part(sizes, new_ref, conv_ref, table_ref, spread, finish)
    corr_part(
        sizes, flags, lambda v: ratio[v],
        corr_ref, table_ref, spread, part_ref, near_ref, far_ref,
    )


def rows_kernel(flags, part_ref, near_ref, far_ref, out_ref, yn_ref, yf_ref):
    wide, halo = part_ref.shape[0], near_ref.shape[0]
    even = flags[0] == 0
    near, far = near_ref[...], far_ref[...]
    out_ref[0:halo] = part_ref[0:halo] + jnp.where(even, far, near)
    out_ref[halo : wide - halo] = part_ref[halo : wide - halo]
    out_ref[wide - halo : wide] = part_ref[wide - halo : wide] + jnp.where(even, near, far)
    yn_ref[...], yf_ref[...] = edges(flags[1], out_ref[:, 0:8, :], out_ref[:, 16:24, :])


def final_kernel(views, lo_x, lo_y, flags, est_ref, total_ref, yn_ref, yf_ref, out_ref, new):
    updated(views, flags, est_ref, total_ref, yn_ref, yf_ref, new)
    out_ref[...] = new[lo_x : lo_x + ROWS, lo_y : lo_y + WIDTH, :]


def pairs(count, start):
    out = []
    for i in range(start, count - 1, 2):
        out += [(i, i + 1), (i + 1, i)]
    return out


def swapped(near, far, axis):
    count = lax.axis_size(axis)
    far = lax.ppermute(far, axis, pairs(count, 1))
    near = lax.ppermute(near, axis, pairs(count, 0))
    return near, far


VMEM = pl.BlockSpec(memory_space=pltpu.VMEM)
SMEM = pl.BlockSpec(memory_space=pltpu.SMEM)


def call(kernel, ins, shapes, scratch=(), limit=2 << 20):
    shapes = [s if isinstance(s, jax.ShapeDtypeStruct) else jax.ShapeDtypeStruct(s, jnp.float32) for s in shapes]
    return pl.pallas_call(
        kernel,
        in_specs=[SMEM] + [VMEM] * (len(ins) - 1),
        out_specs=[VMEM] * len(shapes),
        out_shape=shapes,
        scratch_shapes=list(scratch),
        compiler_params=pltpu.CompilerParams(vmem_limit_bytes=limit),
    )(*ins)


def local(estimate, images, taps_first, taps_second, taps_axial):
    nf, ns, nz = taps_first.shape[1], taps_second.shape[1], taps_axial.shape[1]
    sizes = (nf, ns)
    views = lax.axis_size("view")
    rows, cols, lanes = estimate.shape
    halo = nf - 1
    wide = rows + halo
    flags = jnp.stack(
        [lax.axis_index("tile") % 2, lax.axis_index("view") % 2]
    ).astype(jnp.int32)

    own = jnp.pad(estimate, ((nf // 2, nf // 2), (ns // 2, COLS - cols - ns // 2), (0, 0)))
    near, far = edges(flags[0], own[0:halo], own[wide - halo :])
    near, far = swapped(near, far, "tile")

    pieces = images[0].reshape(rows, views, cols, lanes).transpose(1, 0, 2, 3)
    pieces = pieces.reshape(views, rows * cols, lanes)
    data = lax.all_to_all(pieces, "view", 0, 0, tiled=True)

    pad = lambda x: jnp.pad(x, ((0, 0), (0, lanes - x.shape[1])))
    taps = jnp.concatenate(
        [
            pad(taps_axial),
            pad(taps_axial[:, ::-1]),
            pad(jnp.concatenate([taps_first, taps_second], axis=1)),
            jnp.zeros((5, lanes), jnp.float32),
        ],
        axis=0,
    )
    taps = lax.all_gather(taps, "view", axis=0, tiled=True)
    matrices = jax.ShapeDtypeStruct((views, 3 * lanes, lanes), jnp.bfloat16)
    conv, corr, table = call(
        functools.partial(tables_kernel, (nz - 1) // 2, nf + ns),
        (flags, taps),
        (matrices, matrices, (views, nf + ns, 8, lanes)),
        limit=8 << 20,
    )

    block, strip, side = (wide, COLS, lanes), (halo, COLS, lanes), (wide, 8, lanes)
    images_shape = (views, rows * cols, lanes)
    spread = pltpu.VMEM((views, wide, cols, lanes), jnp.float32)

    def joined(part, near, far):
        total, yn, yf = call(rows_kernel, (flags, part, near, far), (block, side, side))
        yn, yf = swapped(yn, yf, "view")
        return total, yn, yf

    total, yn, yf = joined(own, near, far)
    current, blurred = call(
        functools.partial(first_conv_kernel, sizes),
        (flags, total, yn, yf, conv, table),
        (block, images_shape),
        [spread],
        limit=8 << 20,
    )
    part, near, far = call(
        functools.partial(first_corr_kernel, sizes),
        (flags, data, blurred, corr, table),
        (block, strip, strip),
        [spread],
        limit=10 << 20,
    )
    for _ in range(1, ITERS):
        near, far = swapped(near, far, "tile")
        total, yn, yf = joined(part, near, far)
        current, part, near, far = call(
            functools.partial(pass_kernel, sizes, views),
            (flags, current, total, yn, yf, data, conv, corr, table),
            (block, block, strip, strip),
            [spread, pltpu.VMEM(images_shape, jnp.float32)],
            limit=12 << 20,
        )
    near, far = swapped(near, far, "tile")
    total, yn, yf = joined(part, near, far)
    (out,) = call(
        functools.partial(final_kernel, views, nf // 2, ns // 2),
        (flags, current, total, yn, yf),
        ((rows, cols, lanes),),
        [pltpu.VMEM(block, jnp.float32)],
    )
    return out


def solution(mesh):
    in_specs = (
        P("tile", "view", None),
        P("view", "tile", None, None),
        P("view", None),
        P("view", None),
        P("view", None),
    )
    out_specs = P("tile", "view", None)
    return jax.shard_map(local, mesh=mesh, in_specs=in_specs, out_specs=out_specs, check_vma=False)
```

time: 144 us -> 151 us (1.049)
  the two profiles are of different devices: /device:TPU:70 before, /device:TPU:30 now
where the time goes in v2:
time: 151 us; the launch traced here: 150 us
  starting transfers between devices  62.3 us (41%)
  waiting for transfers between devices  33.5 us (22%)
  blocking collectives  29.6 us (20%)
  Pallas kernels  17.4 us (12%)
  local copies, waits for them, and re-layouts  7.22 us (5%)
    ppermute x6, starting transfers between devices, swapped(): far = lax.ppermute(far, axis, pairs(count, 1))  37.3 us
    ppermute x6, waiting for transfers between devices, swapped(): far = lax.ppermute(far, axis, pairs(count, 1))  33.4 us
    all_gather x1, blocking collectives, local(): taps = lax.all_gather(taps, 'view', axis=0, tiled=True)  29.6 us
    pallas_call x8, Pallas kernels, call(): pl.pallas_call(kernel, in_specs=[SMEM] + [VMEM] * (len(ins) - 1), out_spe...  17.4 us
    ppermute x6, starting transfers between devices, swapped(): near = lax.ppermute(near, axis, pairs(count, 0))  16.1 us
    all_to_all x1, starting transfers between devices, local(): data = lax.all_to_all(pieces, 'view', 0, 0, tiled=True)  8.91 us
    unnamed x24, local copies, waits for them, and re-layouts  4.71 us
  transfers between devices with their start and end apart: 13, of which 5 were waited for; matrix products, arithmetic and copies ran while one was open for 0% of the time, Pallas kernels for 4%

profile of v2, /device:TPU:30, one launch (start us, length us, event | category | flops | bytes accessed | tf_op | source)
XLA Modules:
  0.0 150.4 jit_solution(5316126510957232177)
XLA Ops:
  0.0 2.3 %copy.6 = f32[8,16,16,128]{3,2,0,1:T(8,128)} copy(f32[8,16,16,128]{3,2,1,0:T(8,128)} %bitcast.6) | data formatting | bytes 2097152 | tf_op jit(solution)/shard_map/reshape;squeeze | solution.py:245
  2.3 8.9 %all-to-all-start = ((f32[16,128,128]{2,1,0:T(8,128)}), f32[16,128,128]{2,1,0:T(8,128)S(1)}, u32[]{:S(2)}, u32[]{:S(2)}) async-start(f32[16,128,128]{2,1,0:T(8,128)} %bitcast.4), calls=%async_computation | async-start | bytes 2097152 | tf_op jit(solution)/shard_map/all_to_all | solution.py:247
  11.3 9.2 %collective-permute-start.1 = (f32[4,24,128]{2,1,0:T(8,128)S(1)}, f32[4,24,128]{2,1,0:T(8,128)S(1)}, u32[]{:S(2)}, u32[]{:S(2)}) collective-permute-start(f32[4,24,128]{2,1,0:T(8,128)S(1)} %get-tuple-element.47), channel_id=1, source_target_pairs={{1,2},{2,1},{3,4},{4,3},{5,6},{6,5},{7,8},{8,7},{9,10},{10,9},{11,... | collective-permute-start | bytes 147464 | tf_op jit(solution)/shard_map/ppermute | solution.py:209
  20.5 1.9 %collective-permute-start = (f32[4,24,128]{2,1,0:T(8,128)S(1)}, f32[4,24,128]{2,1,0:T(8,128)S(1)}, u32[]{:S(2)}, u32[]{:S(2)}) collective-permute-start(f32[4,24,128]{2,1,0:T(8,128)S(1)} %get-tuple-element.48), channel_id=1, source_target_pairs={{0,1},{1,0},{2,3},{3,2},{4,5},{5,4},{6,7},{7,6},{8,9},{9,8},{10,11... | collective-permute-start | bytes 147464 | tf_op jit(solution)/shard_map/ppermute | solution.py:210
  22.8 14.7 %collective-permute-done.1.far_ref = f32[4,24,128]{2,1,0:T(8,128)S(1)} collective-permute-done((f32[4,24,128]{2,1,0:T(8,128)S(1)}, f32[4,24,128]{2,1,0:T(8,128)S(1)}, u32[]{:S(2)}, u32[]{:S(2)}) %collective-permute-start.1) | collective-permute-done | bytes 49184 | tf_op jit(solution)/shard_map/ppermute | solution.py:209
  38.1 2.8 %collective-permute-start.2 = (f32[12,8,128]{2,1,0:T(8,128)S(1)}, f32[12,8,128]{2,1,0:T(8,128)S(1)}, u32[]{:S(2)}, u32[]{:S(2)}) collective-permute-start(f32[12,8,128]{2,1,0:T(8,128)S(1)} %get-tuple-element.27), channel_id=1, source_target_pairs={{0,32},{32,0},{64,96},{96,64},{128,160},{160,128},{192,224},{224,1... | collective-permute-start | bytes 147464 | tf_op jit(solution)/shard_map/ppermute | solution.py:210
  40.9 10.1 %collective-permute-start.3 = (f32[12,8,128]{2,1,0:T(8,128)S(1)}, f32[12,8,128]{2,1,0:T(8,128)S(1)}, u32[]{:S(2)}, u32[]{:S(2)}) collective-permute-start(f32[12,8,128]{2,1,0:T(8,128)S(1)} %get-tuple-element.28), channel_id=1, source_target_pairs={{32,64},{64,32},{96,128},{128,96},{160,192},{192,160},{224,256},{2... | collective-permute-start | bytes 147464 | tf_op jit(solution)/shard_map/ppermute | solution.py:209
  51.1 29.6 %all_gather.3.taps_ref = f32[128,128]{1,0:T(8,128)S(1)} all-gather(f32[8,128]{1,0:T(8,128)S(1)} %fusion.3), channel_id=1, replica_groups=mesh['view'=16,'tile'=32] {'view'}, dimensions={0}, use_global_device_ids=true | all-gather | bytes 69632 | tf_op jit(solution)/shard_map/all_gather | solution.py:259
  80.7 2.6 %shard_map.56 = (bf16[16,384,128]{2,1,0:T(8,128)(2,1)S(1)}, bf16[16,384,128]{2,1,0:T(8,128)(2,1)S(1)}, f32[16,12,8,128]{3,2,1,0:T(8,128)S(1)}) custom-call(s32[2]{0:T(128)S(1)} %pad_add_fusion.flags, f32[128,128]{1,0:T(8,128)S(1)} %all_gather.3.taps_ref), custom_call_target="tpu_custom_call" | custom-call | tf_op jit(solution)/shard_map/pallas_call | solution.py:220
  83.9 3.0 %shard_map.57 = (f32[12,24,128]{2,1,0:T(8,128)S(1)}, f32[16,128,128]{2,1,0:T(8,128)S(1)}) custom-call(s32[2]{0:T(128)S(1)} %copy-done.5, f32[12,24,128]{2,1,0:T(8,128)S(1)} %get-tuple-element.26.total_ref, f32[12,8,128]{2,1,0:T(8,128)S(1)} %collective-permute-done.2.yn_ref, f32[12,8,128]{2,1,0:T(8,128)S(1)} %collective-permute-done.3.yf_ref, ...), custom_call_target="tpu_custom_call" | custom-call | tf_op jit(solution)/shard_map/pallas_call | solution.py:220
  91.0 3.2 %shard_map.58 = (f32[12,24,128]{2,1,0:T(8,128)S(1)}, f32[4,24,128]{2,1,0:T(8,128)S(1)}, f32[4,24,128]{2,1,0:T(8,128)S(1)}) custom-call(s32[2]{0:T(128)S(1)} %copy-done.6, f32[16,128,128]{2,1,0:T(8,128)S(1)} %all-to-all-done.data_ref, f32[16,128,128]{2,1,0:T(8,128)S(1)} %copy-done.3, bf16[16,384,128]{2,1,0:T(8,128)(2,1)S(1)} %get-tuple-element.33.corr_ref, ...), custom_call_target="tpu_custom_call" | custom-call | tf_op jit(solution)/shard_map/pallas_call | solution.py:220
  94.2 1.9 %collective-permute-start.4 = (f32[4,24,128]{2,1,0:T(8,128)S(1)}, f32[4,24,128]{2,1,0:T(8,128)S(1)}, u32[]{:S(2)}, u32[]{:S(2)}) collective-permute-start(f32[4,24,128]{2,1,0:T(8,128)S(1)} %get-tuple-element.35), channel_id=1, source_target_pairs={{0,1},{1,0},{2,3},{3,2},{4,5},{5,4},{6,7},{7,6},{8,9},{9,8},{10,11... | collective-permute-start | bytes 147464 | tf_op jit(solution)/shard_map/ppermute | solution.py:210
  96.1 5.6 %collective-permute-start.5 = (f32[4,24,128]{2,1,0:T(8,128)S(1)}, f32[4,24,128]{2,1,0:T(8,128)S(1)}, u32[]{:S(2)}, u32[]{:S(2)}) collective-permute-start(f32[4,24,128]{2,1,0:T(8,128)S(1)} %get-tuple-element.36), channel_id=1, source_target_pairs={{1,2},{2,1},{3,4},{4,3},{5,6},{6,5},{7,8},{8,7},{9,10},{10,9},{11,... | collective-permute-start | bytes 147464 | tf_op jit(solution)/shard_map/ppermute | solution.py:209
  101.7 4.7 %collective-permute-done.5.far_ref = f32[4,24,128]{2,1,0:T(8,128)S(1)} collective-permute-done((f32[4,24,128]{2,1,0:T(8,128)S(1)}, f32[4,24,128]{2,1,0:T(8,128)S(1)}, u32[]{:S(2)}, u32[]{:S(2)}) %collective-permute-start.5) | collective-permute-done | bytes 49184 | tf_op jit(solution)/shard_map/ppermute | solution.py:209
  107.0 3.8 %collective-permute-start.6 = (f32[12,8,128]{2,1,0:T(8,128)S(1)}, f32[12,8,128]{2,1,0:T(8,128)S(1)}, u32[]{:S(2)}, u32[]{:S(2)}) collective-permute-start(f32[12,8,128]{2,1,0:T(8,128)S(1)} %get-tuple-element.38), channel_id=1, source_target_pairs={{0,32},{32,0},{64,96},{96,64},{128,160},{160,128},{192,224},{224,1... | collective-permute-start | bytes 147464 | tf_op jit(solution)/shard_map/ppermute | solution.py:210
  110.8 4.4 %collective-permute-start.7 = (f32[12,8,128]{2,1,0:T(8,128)S(1)}, f32[12,8,128]{2,1,0:T(8,128)S(1)}, u32[]{:S(2)}, u32[]{:S(2)}) collective-permute-start(f32[12,8,128]{2,1,0:T(8,128)S(1)} %get-tuple-element.39), channel_id=1, source_target_pairs={{32,64},{64,32},{96,128},{128,96},{160,192},{192,160},{224,256},{2... | collective-permute-start | bytes 147464 | tf_op jit(solution)/shard_map/ppermute | solution.py:209
  115.2 3.7 %collective-permute-done.7.yf_ref = f32[12,8,128]{2,1,0:T(8,128)S(1)} collective-permute-done((f32[12,8,128]{2,1,0:T(8,128)S(1)}, f32[12,8,128]{2,1,0:T(8,128)S(1)}, u32[]{:S(2)}, u32[]{:S(2)}) %collective-permute-start.7) | collective-permute-done | bytes 49184 | tf_op jit(solution)/shard_map/ppermute | solution.py:209
  118.9 5.7 %shard_map.60 = (f32[12,24,128]{2,1,0:T(8,128)S(1)}, f32[12,24,128]{2,1,0:T(8,128)S(1)}, f32[4,24,128]{2,1,0:T(8,128)S(1)}, f32[4,24,128]{2,1,0:T(8,128)S(1)}) custom-call(s32[2]{0:T(128)S(1)} %copy-done.7, f32[12,24,128]{2,1,0:T(8,128)S(1)} %get-tuple-element.31.est_ref, f32[12,24,128]{2,1,0:T(8,128)S(1)} %get-tuple-element.37.total_ref, ...), custom_call_target="tpu_custom_call" | custom-call | tf_op jit(solution)/shard_map/pallas_call | solution.py:220
  124.6 1.9 %collective-permute-start.8 = (f32[4,24,128]{2,1,0:T(8,128)S(1)}, f32[4,24,128]{2,1,0:T(8,128)S(1)}, u32[]{:S(2)}, u32[]{:S(2)}) collective-permute-start(f32[4,24,128]{2,1,0:T(8,128)S(1)} %get-tuple-element.42), channel_id=1, source_target_pairs={{0,1},{1,0},{2,3},{3,2},{4,5},{5,4},{6,7},{7,6},{8,9},{9,8},{10,11... | collective-permute-start | bytes 147464 | tf_op jit(solution)/shard_map/ppermute | solution.py:210
  126.5 5.0 %collective-permute-start.9 = (f32[4,24,128]{2,1,0:T(8,128)S(1)}, f32[4,24,128]{2,1,0:T(8,128)S(1)}, u32[]{:S(2)}, u32[]{:S(2)}) collective-permute-start(f32[4,24,128]{2,1,0:T(8,128)S(1)} %get-tuple-element.43), channel_id=1, source_target_pairs={{1,2},{2,1},{3,4},{4,3},{5,6},{6,5},{7,8},{8,7},{9,10},{10,9},{11,... | collective-permute-start | bytes 147464 | tf_op jit(solution)/shard_map/ppermute | solution.py:209
  131.5 5.3 %collective-permute-done.9.far_ref = f32[4,24,128]{2,1,0:T(8,128)S(1)} collective-permute-done((f32[4,24,128]{2,1,0:T(8,128)S(1)}, f32[4,24,128]{2,1,0:T(8,128)S(1)}, u32[]{:S(2)}, u32[]{:S(2)}) %collective-permute-start.9) | collective-permute-done | bytes 49184 | tf_op jit(solution)/shard_map/ppermute | solution.py:209
  137.3 3.8 %collective-permute-start.10 = (f32[12,8,128]{2,1,0:T(8,128)S(1)}, f32[12,8,128]{2,1,0:T(8,128)S(1)}, u32[]{:S(2)}, u32[]{:S(2)}) collective-permute-start(f32[12,8,128]{2,1,0:T(8,128)S(1)} %get-tuple-element.45), channel_id=1, source_target_pairs={{0,32},{32,0},{64,96},{96,64},{128,160},{160,128},{192,224},{224,1... | collective-permute-start | bytes 147464 | tf_op jit(solution)/shard_map/ppermute | solution.py:210
  141.1 3.0 %collective-permute-start.11 = (f32[12,8,128]{2,1,0:T(8,128)S(1)}, f32[12,8,128]{2,1,0:T(8,128)S(1)}, u32[]{:S(2)}, u32[]{:S(2)}) collective-permute-start(f32[12,8,128]{2,1,0:T(8,128)S(1)} %get-tuple-element.46), channel_id=1, source_target_pairs={{32,64},{64,32},{96,128},{128,96},{160,192},{192,160},{224,256},{2... | collective-permute-start | bytes 147464 | tf_op jit(solution)/shard_map/ppermute | solution.py:209
  144.2 5.1 %collective-permute-done.11.yf_ref = f32[12,8,128]{2,1,0:T(8,128)S(1)} collective-permute-done((f32[12,8,128]{2,1,0:T(8,128)S(1)}, f32[12,8,128]{2,1,0:T(8,128)S(1)}, u32[]{:S(2)}, u32[]{:S(2)}) %collective-permute-start.11) | collective-permute-done | bytes 49184 | tf_op jit(solution)/shard_map/ppermute | solution.py:209
  (44 shorter events, 8.0 us)
Async XLA Ops:
  2.3 8.9 %copy-start.8 = (f32[8,16,128]{2,1,0:T(8,128)S(1)}, f32[8,16,128]{2,1,0:T(8,128)}, u32[]{:S(2)}) copy-start(f32[8,16,128]{2,1,0:T(8,128)} %param.5) | copy-start | bytes 196612
  2.3 20.2 %copy-start.10 = (f32[1,7]{1,0:T(1,128)S(1)}, f32[1,7]{1,0:T(1,128)}, u32[]{:S(2)}) copy-start(f32[1,7]{1,0:T(1,128)} %param.8) | copy-start | bytes 88
  2.3 20.2 %copy-start.11 = (f32[1,5]{1,0:T(1,128)S(1)}, f32[1,5]{1,0:T(1,128)}, u32[]{:S(2)}) copy-start(f32[1,5]{1,0:T(1,128)} %param.7) | copy-start | bytes 64
  2.3 20.2 %copy-start.9 = (f32[1,33]{1,0:T(1,128)S(1)}, f32[1,33]{1,0:T(1,128)}, u32[]{:S(2)}) copy-start(f32[1,33]{1,0:T(1,128)} %param.9) | copy-start | bytes 400
  2.3 86.8 %all-to-all-start = ((f32[16,128,128]{2,1,0:T(8,128)}), f32[16,128,128]{2,1,0:T(8,128)S(1)}, u32[]{:S(2)}, u32[]{:S(2)}) async-start(f32[16,128,128]{2,1,0:T(8,128)} %bitcast.4), calls=%async_computation | async-start | bytes 2097152 | tf_op jit(solution)/shard_map/all_to_all | solution.py:247
  11.3 26.2 %collective-permute-start.1 = (f32[4,24,128]{2,1,0:T(8,128)S(1)}, f32[4,24,128]{2,1,0:T(8,128)S(1)}, u32[]{:S(2)}, u32[]{:S(2)}) collective-permute-start(f32[4,24,128]{2,1,0:T(8,128)S(1)} %get-tuple-element.47), channel_id=1, source_target_pairs={{1,2},{2,1},{3,4},{4,3},{5,6},{6,5},{7,8},{8,7},{9,10},{10,9},{11,... | collective-permute-start | bytes 147464 | tf_op jit(solution)/shard_map/ppermute | solution.py:209
  20.5 17.1 %collective-permute-start = (f32[4,24,128]{2,1,0:T(8,128)S(1)}, f32[4,24,128]{2,1,0:T(8,128)S(1)}, u32[]{:S(2)}, u32[]{:S(2)}) collective-permute-start(f32[4,24,128]{2,1,0:T(8,128)S(1)} %get-tuple-element.48), channel_id=1, source_target_pairs={{0,1},{1,0},{2,3},{3,2},{4,5},{5,4},{6,7},{7,6},{8,9},{9,8},{10,11... | collective-permute-start | bytes 147464 | tf_op jit(solution)/shard_map/ppermute | solution.py:210
  22.5 60.8 %copy-start.4 = (s32[2]{0:T(128)}, s32[2]{0:T(128)S(1)}, u32[]{:S(2)}) copy-start(s32[2]{0:T(128)S(1)} %pad_add_fusion.flags) | copy-start | bytes 28
  38.1 45.2 %collective-permute-start.2 = (f32[12,8,128]{2,1,0:T(8,128)S(1)}, f32[12,8,128]{2,1,0:T(8,128)S(1)}, u32[]{:S(2)}, u32[]{:S(2)}) collective-permute-start(f32[12,8,128]{2,1,0:T(8,128)S(1)} %get-tuple-element.27), channel_id=1, source_target_pairs={{0,32},{32,0},{64,96},{96,64},{128,160},{160,128},{192,224},{224,1... | collective-permute-start | bytes 147464 | tf_op jit(solution)/shard_map/ppermute | solution.py:210
  40.9 42.4 %collective-permute-start.3 = (f32[12,8,128]{2,1,0:T(8,128)S(1)}, f32[12,8,128]{2,1,0:T(8,128)S(1)}, u32[]{:S(2)}, u32[]{:S(2)}) collective-permute-start(f32[12,8,128]{2,1,0:T(8,128)S(1)} %get-tuple-element.28), channel_id=1, source_target_pairs={{32,64},{64,32},{96,128},{128,96},{160,192},{192,160},{224,256},{2... | collective-permute-start | bytes 147464 | tf_op jit(solution)/shard_map/ppermute | solution.py:209
  83.3 0.7 copy-start.5
  86.9 1.2 copy-start
  88.1 1.0 copy-start.2
  89.1 1.2 copy-start.3
  91.0 27.9 %copy-start.1 = (bf16[16,384,128]{2,1,0:T(8,128)(2,1)S(1)}, bf16[16,384,128]{2,1,0:T(8,128)(2,1)}, u32[]{:S(2)}) copy-start(bf16[16,384,128]{2,1,0:T(8,128)(2,1)} %copy-done) | copy-start | bytes 4718596
  91.0 27.9 %copy-start.7 = (s32[2]{0:T(128)S(1)}, s32[2]{0:T(128)}, u32[]{:S(2)}) copy-start(s32[2]{0:T(128)} %copy-done.4) | copy-start | bytes 28
  94.2 7.5 %collective-permute-start.4 = (f32[4,24,128]{2,1,0:T(8,128)S(1)}, f32[4,24,128]{2,1,0:T(8,128)S(1)}, u32[]{:S(2)}, u32[]{:S(2)}) collective-permute-start(f32[4,24,128]{2,1,0:T(8,128)S(1)} %get-tuple-element.35), channel_id=1, source_target_pairs={{0,1},{1,0},{2,3},{3,2},{4,5},{5,4},{6,7},{7,6},{8,9},{9,8},{10,11... | collective-permute-start | bytes 147464 | tf_op jit(solution)/shard_map/ppermute | solution.py:210
  96.1 10.3 %collective-permute-start.5 = (f32[4,24,128]{2,1,0:T(8,128)S(1)}, f32[4,24,128]{2,1,0:T(8,128)S(1)}, u32[]{:S(2)}, u32[]{:S(2)}) collective-permute-start(f32[4,24,128]{2,1,0:T(8,128)S(1)} %get-tuple-element.36), channel_id=1, source_target_pairs={{1,2},{2,1},{3,4},{4,3},{5,6},{6,5},{7,8},{8,7},{9,10},{10,9},{11,... | collective-permute-start | bytes 147464 | tf_op jit(solution)/shard_map/ppermute | solution.py:209
  107.0 8.2 %collective-permute-start.6 = (f32[12,8,128]{2,1,0:T(8,128)S(1)}, f32[12,8,128]{2,1,0:T(8,128)S(1)}, u32[]{:S(2)}, u32[]{:S(2)}) collective-permute-start(f32[12,8,128]{2,1,0:T(8,128)S(1)} %get-tuple-element.38), channel_id=1, source_target_pairs={{0,32},{32,0},{64,96},{96,64},{128,160},{160,128},{192,224},{224,1... | collective-permute-start | bytes 147464 | tf_op jit(solution)/shard_map/ppermute | solution.py:210
  110.8 8.1 %collective-permute-start.7 = (f32[12,8,128]{2,1,0:T(8,128)S(1)}, f32[12,8,128]{2,1,0:T(8,128)S(1)}, u32[]{:S(2)}, u32[]{:S(2)}) collective-permute-start(f32[12,8,128]{2,1,0:T(8,128)S(1)} %get-tuple-element.39), channel_id=1, source_target_pairs={{32,64},{64,32},{96,128},{128,96},{160,192},{192,160},{224,256},{2... | collective-permute-start | bytes 147464 | tf_op jit(solution)/shard_map/ppermute | solution.py:209
  124.6 6.9 %collective-permute-start.8 = (f32[4,24,128]{2,1,0:T(8,128)S(1)}, f32[4,24,128]{2,1,0:T(8,128)S(1)}, u32[]{:S(2)}, u32[]{:S(2)}) collective-permute-start(f32[4,24,128]{2,1,0:T(8,128)S(1)} %get-tuple-element.42), channel_id=1, source_target_pairs={{0,1},{1,0},{2,3},{3,2},{4,5},{5,4},{6,7},{7,6},{8,9},{9,8},{10,11... | collective-permute-start | bytes 147464 | tf_op jit(solution)/shard_map/ppermute | solution.py:210
  126.5 10.3 %collective-permute-start.9 = (f32[4,24,128]{2,1,0:T(8,128)S(1)}, f32[4,24,128]{2,1,0:T(8,128)S(1)}, u32[]{:S(2)}, u32[]{:S(2)}) collective-permute-start(f32[4,24,128]{2,1,0:T(8,128)S(1)} %get-tuple-element.43), channel_id=1, source_target_pairs={{1,2},{2,1},{3,4},{4,3},{5,6},{6,5},{7,8},{8,7},{9,10},{10,9},{11,... | collective-permute-start | bytes 147464 | tf_op jit(solution)/shard_map/ppermute | solution.py:209
  137.3 6.8 %collective-permute-start.10 = (f32[12,8,128]{2,1,0:T(8,128)S(1)}, f32[12,8,128]{2,1,0:T(8,128)S(1)}, u32[]{:S(2)}, u32[]{:S(2)}) collective-permute-start(f32[12,8,128]{2,1,0:T(8,128)S(1)} %get-tuple-element.45), channel_id=1, source_target_pairs={{0,32},{32,0},{64,96},{96,64},{128,160},{160,128},{192,224},{224,1... | collective-permute-start | bytes 147464 | tf_op jit(solution)/shard_map/ppermute | solution.py:210
  141.1 8.1 %collective-permute-start.11 = (f32[12,8,128]{2,1,0:T(8,128)S(1)}, f32[12,8,128]{2,1,0:T(8,128)S(1)}, u32[]{:S(2)}, u32[]{:S(2)}) collective-permute-start(f32[12,8,128]{2,1,0:T(8,128)S(1)} %get-tuple-element.46), channel_id=1, source_target_pairs={{32,64},{64,32},{96,128},{128,96},{160,192},{192,160},{224,256},{2... | collective-permute-start | bytes 147464 | tf_op jit(solution)/shard_map/ppermute | solution.py:209
  (1 other events, 0.7 us)

commit v3 on v2

--- a/solution.py
+++ b/solution.py
@@ -11,6 +11,7 @@
 LANES = 128
 COLS = 24
 ROWS, WIDTH = 8, 16
+BLOCK = ROWS * WIDTH
 
 
 def split(x):
@@ -37,28 +38,51 @@
     return jnp.where(even, high, low), jnp.where(even, low, high)
 
 
-def tables_kernel(radius, count, flags, taps_ref, conv_ref, corr_ref, table_ref):
-    lane = lax.broadcasted_iota(jnp.int32, (16, LANES), 1)
-    sub = lax.broadcasted_iota(jnp.int32, (16, LANES), 0)
+def pieces_kernel(images_ref, first_ref, second_ref, axial_ref, out_ref, taps):
+    taps[...] = jnp.zeros_like(taps)
+    for row, ref in enumerate((axial_ref, first_ref, second_ref)):
+        taps[row : row + 1, 0 : ref.shape[1]] = ref[...]
+    for w in range(out_ref.shape[0]):
+        for i in range(ROWS):
+            out_ref[w, WIDTH * i : WIDTH * (i + 1), :] = images_ref[0, i, WIDTH * w : WIDTH * (w + 1), :]
+        out_ref[w, BLOCK:, :] = taps[...]
+
+
+def make_tables(sizes, data_ref, conv_ref, corr_ref, table_ref, axial):
+    nf, ns, nz = sizes
+    views = data_ref.shape[0]
+    lane = lax.broadcasted_iota(jnp.int32, (8, LANES), 1)
+    sub = lax.broadcasted_iota(jnp.int32, (8, LANES), 0)
+    for v in range(views):
+        axial[v : v + 1, :] = data_ref[v, BLOCK : BLOCK + 1, :]
+    z = lax.broadcasted_iota(jnp.int32, (LANES, LANES), 0)
+    zz = lax.broadcasted_iota(jnp.int32, (LANES, LANES), 1)
+    reverse = jnp.where(z + zz == nz - 1, 1.0, 0.0).astype(jnp.float32)
+    axial[views:, :] = jnp.dot(
+        axial[0:views, :], reverse, precision=lax.Precision.HIGHEST, preferred_element_type=jnp.float32
+    )
 
     def one(v, carry):
-        taps = taps_ref[pl.ds(8 * v, 8), :]
-        for row, ref in ((0, conv_ref), (1, corr_ref)):
-            high, low = split(banded(taps[row : row + 1], radius))
+        for at, ref in ((0, conv_ref), (views, corr_ref)):
+            high, low = split(banded(axial[pl.ds(at + v, 1), :], nz // 2))
             ref[v, 0:LANES] = high
             ref[v, LANES : 2 * LANES] = high
             ref[v, 2 * LANES : 3 * LANES] = low
-        picked = jnp.where(lane == sub, jnp.broadcast_to(taps[2:3], (16, LANES)), 0.0)
-        column = jnp.broadcast_to(jnp.sum(picked, axis=1, keepdims=True), (16, LANES))
-        for k in range(count):
-            table_ref[v, k] = jnp.broadcast_to(column[k : k + 1], (8, LANES))
-        return carry
-
-    lax.fori_loop(0, table_ref.shape[0], one, 0)
+        start = 0
+        for row, count in ((1, nf), (2, ns)):
+            taps = jnp.broadcast_to(data_ref[v, BLOCK + row : BLOCK + row + 1, :], (8, LANES))
+            column = jnp.sum(jnp.where(lane == sub, taps, 0.0), axis=1, keepdims=True)
+            column = jnp.broadcast_to(column, (8, LANES))
+            for k in range(count):
+                table_ref[v, start + k] = jnp.broadcast_to(column[k : k + 1], (8, LANES))
+            start += count
+        return carry
+
+    lax.fori_loop(0, views, one, 0, unroll=2)
 
 
 def conv_part(sizes, est_ref, conv_ref, table_ref, spread, finish):
-    nf, ns = sizes
+    nf, ns, _ = sizes
     wide, views = est_ref.shape[0], conv_ref.shape[0]
 
     def row(i, carry):
@@ -93,7 +117,7 @@
 
 
 def corr_part(sizes, flags, ratio_of, corr_ref, table_ref, spread, part_ref, near_ref, far_ref):
-    nf, ns = sizes
+    nf, ns, _ = sizes
     wide, views = spread.shape[1], spread.shape[0]
 
     def one(v, carry):
@@ -143,21 +167,22 @@
     return jnp.where(even, yf, yn), jnp.where(even, yn, yf)
 
 
-def first_conv_kernel(sizes, flags, total_ref, yn_ref, yf_ref, conv_ref, table_ref, est_ref, blurred_ref, spread):
+def first_kernel(sizes, flags, total_ref, yn_ref, yf_ref, data_ref, est_ref, part_ref, near_ref, far_ref, conv_ref, corr_ref, table_ref, spread, ratio, axial):
+    make_tables(sizes, data_ref, conv_ref, corr_ref, table_ref, axial)
     low, high = sides(flags, yn_ref, yf_ref)
     est_ref[:, 0:8, :] = total_ref[:, 0:8, :] + low
     est_ref[:, 8:16, :] = total_ref[:, 8:16, :]
     est_ref[:, 16:24, :] = total_ref[:, 16:24, :] + high
-
+    both_parts(sizes, flags, est_ref, data_ref, conv_ref, corr_ref, table_ref, part_ref, near_ref, far_ref, spread, ratio)
+
+
+def both_parts(sizes, flags, est_ref, data_ref, conv_ref, corr_ref, table_ref, part_ref, near_ref, far_ref, spread, ratio):
     def finish(v, blurred):
-        blurred_ref[v] = blurred
+        ratio[v] = data_ref[v, 0:BLOCK, :] / blurred
 
     conv_part(sizes, est_ref, conv_ref, table_ref, spread, finish)
-
-
-def first_corr_kernel(sizes, flags, data_ref, blurred_ref, corr_ref, table_ref, part_ref, near_ref, far_ref, spread):
     corr_part(
-        sizes, flags, lambda v: data_ref[v] / blurred_ref[v],
+        sizes, flags, lambda v: ratio[v],
         corr_ref, table_ref, spread, part_ref, near_ref, far_ref,
     )
 
@@ -171,15 +196,7 @@
 
 def pass_kernel(sizes, views, flags, est_ref, total_ref, yn_ref, yf_ref, data_ref, conv_ref, corr_ref, table_ref, new_ref, part_ref, near_ref, far_ref, spread, ratio):
     updated(views, flags, est_ref, total_ref, yn_ref, yf_ref, new_ref)
-
-    def finish(v, blurred):
-        ratio[v] = data_ref[v] / blurred
-
-    conv_part(sizes, new_ref, conv_ref, table_ref, spread, finish)
-    corr_part(
-        sizes, flags, lambda v: ratio[v],
-        corr_ref, table_ref, spread, part_ref, near_ref, far_ref,
-    )
+    both_parts(sizes, flags, new_ref, data_ref, conv_ref, corr_ref, table_ref, part_ref, near_ref, far_ref, spread, ratio)
 
 
 def rows_kernel(flags, part_ref, near_ref, far_ref, out_ref, yn_ref, yf_ref):
@@ -229,7 +246,7 @@
 
 def local(estimate, images, taps_first, taps_second, taps_axial):
     nf, ns, nz = taps_first.shape[1], taps_second.shape[1], taps_axial.shape[1]
-    sizes = (nf, ns)
+    sizes = (nf, ns, nz)
     views = lax.axis_size("view")
     rows, cols, lanes = estimate.shape
     halo = nf - 1
@@ -242,32 +259,23 @@
     near, far = edges(flags[0], own[0:halo], own[wide - halo :])
     near, far = swapped(near, far, "tile")
 
-    pieces = images[0].reshape(rows, views, cols, lanes).transpose(1, 0, 2, 3)
-    pieces = pieces.reshape(views, rows * cols, lanes)
-    data = lax.all_to_all(pieces, "view", 0, 0, tiled=True)
-
-    pad = lambda x: jnp.pad(x, ((0, 0), (0, lanes - x.shape[1])))
-    taps = jnp.concatenate(
-        [
-            pad(taps_axial),
-            pad(taps_axial[:, ::-1]),
-            pad(jnp.concatenate([taps_first, taps_second], axis=1)),
-            jnp.zeros((5, lanes), jnp.float32),
-        ],
-        axis=0,
-    )
-    taps = lax.all_gather(taps, "view", axis=0, tiled=True)
+    data_shape = (views, rows * cols + 8, lanes)
+    data = pl.pallas_call(
+        pieces_kernel,
+        in_specs=[VMEM] * 4,
+        out_specs=VMEM,
+        out_shape=jax.ShapeDtypeStruct(data_shape, jnp.float32),
+        scratch_shapes=[pltpu.VMEM((8, lanes), jnp.float32)],
+        compiler_params=pltpu.CompilerParams(vmem_limit_bytes=4 << 20),
+    )(images, taps_first, taps_second, taps_axial)
+    data = lax.all_to_all(data, "view", 0, 0, tiled=True)
     matrices = jax.ShapeDtypeStruct((views, 3 * lanes, lanes), jnp.bfloat16)
-    conv, corr, table = call(
-        functools.partial(tables_kernel, (nz - 1) // 2, nf + ns),
-        (flags, taps),
-        (matrices, matrices, (views, nf + ns, 8, lanes)),
-        limit=8 << 20,
-    )
 
     block, strip, side = (wide, COLS, lanes), (halo, COLS, lanes), (wide, 8, lanes)
-    images_shape = (views, rows * cols, lanes)
-    spread = pltpu.VMEM((views, wide, cols, lanes), jnp.float32)
+    scratch = [
+        pltpu.VMEM((views, wide, cols, lanes), jnp.float32),
+        pltpu.VMEM((views, rows * cols, lanes), jnp.float32),
+    ]
 
     def joined(part, near, far):
         total, yn, yf = call(rows_kernel, (flags, part, near, far), (block, side, side))
@@ -275,19 +283,12 @@
         return total, yn, yf
 
     total, yn, yf = joined(own, near, far)
-    current, blurred = call(
-        functools.partial(first_conv_kernel, sizes),
-        (flags, total, yn, yf, conv, table),
-        (block, images_shape),
-        [spread],
-        limit=8 << 20,
-    )
-    part, near, far = call(
-        functools.partial(first_corr_kernel, sizes),
-        (flags, data, blurred, corr, table),
-        (block, strip, strip),
-        [spread],
-        limit=10 << 20,
+    current, part, near, far, conv, corr, table = call(
+        functools.partial(first_kernel, sizes),
+        (flags, total, yn, yf, data),
+        (block, block, strip, strip, matrices, matrices, (views, nf + ns, 8, lanes)),
+        scratch + [pltpu.VMEM((2 * views, lanes), jnp.float32)],
+        limit=16 << 20,
     )
     for _ in range(1, ITERS):
         near, far = swapped(near, far, "tile")
@@ -296,7 +297,7 @@
             functools.partial(pass_kernel, sizes, views),
             (flags, current, total, yn, yf, data, conv, corr, table),
             (block, block, strip, strip),
-            [spread, pltpu.VMEM(images_shape, jnp.float32)],
+            scratch,
             limit=12 << 20,
         )
     near, far = swapped(near, far, "tile")

time: 151 us -> 120 us (0.79)
  the two profiles are of different devices: /device:TPU:30 before, /device:TPU:38 now
where the time goes in v3:
time: 120 us; the launch traced here: 119 us
  waiting for transfers between devices  51.6 us (43%)
  starting transfers between devices  47.1 us (39%)
  Pallas kernels  17.2 us (14%)
  local copies, waits for them, and re-layouts  3.2 us (3%)
    ppermute x6, waiting for transfers between devices, swapped(): far = lax.ppermute(far, axis, pairs(count, 1))  46.7 us
    ppermute x6, starting transfers between devices, swapped(): far = lax.ppermute(far, axis, pairs(count, 1))  25.3 us
    pallas_call x6, Pallas kernels, call(): pl.pallas_call(kernel, in_specs=[SMEM] + [VMEM] * (len(ins) - 1), out_spe...  16.1 us
    ppermute x6, starting transfers between devices, swapped(): near = lax.ppermute(near, axis, pairs(count, 0))  13 us
    all_to_all x1, starting transfers between devices, local(): data = lax.all_to_all(data, 'view', 0, 0, tiled=True)  8.78 us
    ppermute x6, waiting for transfers between devices, swapped(): near = lax.ppermute(near, axis, pairs(count, 0))  4.9 us
    unnamed x10, local copies, waits for them, and re-layouts  3.19 us
  transfers between devices with their start and end apart: 13, of which 9 were waited for; matrix products, arithmetic and copies ran while one was open for 0% of the time, Pallas kernels for 0%

profile of v3, /device:TPU:38, one launch (start us, length us, event | category | flops | bytes accessed | tf_op | source)
XLA Modules:
  0.0 119.4 jit_solution(14293055288296718142)
XLA Ops:
  0.0 1.2 %copy-done = f32[1,8,256,128]{3,2,1,0:T(8,128)S(1)} copy-done((f32[1,8,256,128]{3,2,1,0:T(8,128)S(1)}, f32[1,8,256,128]{3,2,1,0:T(8,128)}, u32[]{:S(2)}) %copy-start) | copy-done | bytes 1048600
  4.3 8.8 %all-to-all-start = ((f32[16,136,128]{2,1,0:T(8,128)}), f32[16,136,128]{2,1,0:T(8,128)S(1)}, u32[]{:S(2)}, u32[]{:S(2)}) async-start(f32[16,136,128]{2,1,0:T(8,128)} %shard_map.56), calls=%async_computation | async-start | bytes 2228224 | tf_op jit(solution)/shard_map/all_to_all | solution.py:271
  13.1 9.2 %collective-permute-start.1 = (f32[4,24,128]{2,1,0:T(8,128)S(1)}, f32[4,24,128]{2,1,0:T(8,128)S(1)}, u32[]{:S(2)}, u32[]{:S(2)}) collective-permute-start(f32[4,24,128]{2,1,0:T(8,128)S(1)} %get-tuple-element.45), channel_id=1, source_target_pairs={{1,2},{2,1},{3,4},{4,3},{5,6},{6,5},{7,8},{8,7},{9,10},{10,9},{11,... | collective-permute-start | bytes 147464 | tf_op jit(solution)/shard_map/ppermute | solution.py:226
  22.3 1.9 %collective-permute-start = (f32[4,24,128]{2,1,0:T(8,128)S(1)}, f32[4,24,128]{2,1,0:T(8,128)S(1)}, u32[]{:S(2)}, u32[]{:S(2)}) collective-permute-start(f32[4,24,128]{2,1,0:T(8,128)S(1)} %get-tuple-element.46), channel_id=1, source_target_pairs={{0,1},{1,0},{2,3},{3,2},{4,5},{5,4},{6,7},{7,6},{8,9},{9,8},{10,11... | collective-permute-start | bytes 147464 | tf_op jit(solution)/shard_map/ppermute | solution.py:227
  24.3 22.6 %collective-permute-done.1.far_ref = f32[4,24,128]{2,1,0:T(8,128)S(1)} collective-permute-done((f32[4,24,128]{2,1,0:T(8,128)S(1)}, f32[4,24,128]{2,1,0:T(8,128)S(1)}, u32[]{:S(2)}, u32[]{:S(2)}) %collective-permute-start.1) | collective-permute-done | bytes 49184 | tf_op jit(solution)/shard_map/ppermute | solution.py:226
  47.5 3.4 %collective-permute-start.2 = (f32[12,8,128]{2,1,0:T(8,128)S(1)}, f32[12,8,128]{2,1,0:T(8,128)S(1)}, u32[]{:S(2)}, u32[]{:S(2)}) collective-permute-start(f32[12,8,128]{2,1,0:T(8,128)S(1)} %get-tuple-element.26), channel_id=1, source_target_pairs={{0,32},{32,0},{64,96},{96,64},{128,160},{160,128},{192,224},{224,1... | collective-permute-start | bytes 147464 | tf_op jit(solution)/shard_map/ppermute | solution.py:227
  50.9 1.9 %collective-permute-start.3 = (f32[12,8,128]{2,1,0:T(8,128)S(1)}, f32[12,8,128]{2,1,0:T(8,128)S(1)}, u32[]{:S(2)}, u32[]{:S(2)}) collective-permute-start(f32[12,8,128]{2,1,0:T(8,128)S(1)} %get-tuple-element.27), channel_id=1, source_target_pairs={{32,64},{64,32},{96,128},{128,96},{160,192},{192,160},{224,256},{2... | collective-permute-start | bytes 147464 | tf_op jit(solution)/shard_map/ppermute | solution.py:226
  53.5 5.5 %collective-permute-done.3.yf_ref = f32[12,8,128]{2,1,0:T(8,128)S(1)} collective-permute-done((f32[12,8,128]{2,1,0:T(8,128)S(1)}, f32[12,8,128]{2,1,0:T(8,128)S(1)}, u32[]{:S(2)}, u32[]{:S(2)}) %collective-permute-start.3) | collective-permute-done | bytes 49184 | tf_op jit(solution)/shard_map/ppermute | solution.py:226
  58.9 7.4 %shard_map.57 = (f32[12,24,128]{2,1,0:T(8,128)S(1)}, f32[12,24,128]{2,1,0:T(8,128)S(1)}, f32[4,24,128]{2,1,0:T(8,128)S(1)}, f32[4,24,128]{2,1,0:T(8,128)S(1)}, b...) custom-call(s32[2]{0:T(128)S(1)} %pad_add_fusion.flags, ...), custom_call_target="tpu_custom_call" | custom-call | tf_op jit(solution)/shard_map/pallas_call | solution.py:237
  66.4 1.9 %collective-permute-start.4 = (f32[4,24,128]{2,1,0:T(8,128)S(1)}, f32[4,24,128]{2,1,0:T(8,128)S(1)}, u32[]{:S(2)}, u32[]{:S(2)}) collective-permute-start(f32[4,24,128]{2,1,0:T(8,128)S(1)} %get-tuple-element.30), channel_id=1, source_target_pairs={{0,1},{1,0},{2,3},{3,2},{4,5},{5,4},{6,7},{7,6},{8,9},{9,8},{10,11... | collective-permute-start | bytes 147464 | tf_op jit(solution)/shard_map/ppermute | solution.py:227
  68.3 5.6 %collective-permute-start.5 = (f32[4,24,128]{2,1,0:T(8,128)S(1)}, f32[4,24,128]{2,1,0:T(8,128)S(1)}, u32[]{:S(2)}, u32[]{:S(2)}) collective-permute-start(f32[4,24,128]{2,1,0:T(8,128)S(1)} %get-tuple-element.31), channel_id=1, source_target_pairs={{1,2},{2,1},{3,4},{4,3},{5,6},{6,5},{7,8},{8,7},{9,10},{10,9},{11,... | collective-permute-start | bytes 147464 | tf_op jit(solution)/shard_map/ppermute | solution.py:226
  73.9 4.6 %collective-permute-done.5.far_ref = f32[4,24,128]{2,1,0:T(8,128)S(1)} collective-permute-done((f32[4,24,128]{2,1,0:T(8,128)S(1)}, f32[4,24,128]{2,1,0:T(8,128)S(1)}, u32[]{:S(2)}, u32[]{:S(2)}) %collective-permute-start.5) | collective-permute-done | bytes 49184 | tf_op jit(solution)/shard_map/ppermute | solution.py:226
  79.1 1.9 %collective-permute-start.6 = (f32[12,8,128]{2,1,0:T(8,128)S(1)}, f32[12,8,128]{2,1,0:T(8,128)S(1)}, u32[]{:S(2)}, u32[]{:S(2)}) collective-permute-start(f32[12,8,128]{2,1,0:T(8,128)S(1)} %get-tuple-element.33), channel_id=1, source_target_pairs={{0,32},{32,0},{64,96},{96,64},{128,160},{160,128},{192,224},{224,1... | collective-permute-start | bytes 147464 | tf_op jit(solution)/shard_map/ppermute | solution.py:227
  81.0 2.0 %collective-permute-start.7 = (f32[12,8,128]{2,1,0:T(8,128)S(1)}, f32[12,8,128]{2,1,0:T(8,128)S(1)}, u32[]{:S(2)}, u32[]{:S(2)}) collective-permute-start(f32[12,8,128]{2,1,0:T(8,128)S(1)} %get-tuple-element.34), channel_id=1, source_target_pairs={{32,64},{64,32},{96,128},{128,96},{160,192},{192,160},{224,256},{2... | collective-permute-start | bytes 147464 | tf_op jit(solution)/shard_map/ppermute | solution.py:226
  83.0 2.1 %collective-permute-done.6.yn_ref = f32[12,8,128]{2,1,0:T(8,128)S(1)} collective-permute-done((f32[12,8,128]{2,1,0:T(8,128)S(1)}, f32[12,8,128]{2,1,0:T(8,128)S(1)}, u32[]{:S(2)}, u32[]{:S(2)}) %collective-permute-start.6) | collective-permute-done | bytes 49184 | tf_op jit(solution)/shard_map/ppermute | solution.py:227
  85.1 4.0 %collective-permute-done.7.yf_ref = f32[12,8,128]{2,1,0:T(8,128)S(1)} collective-permute-done((f32[12,8,128]{2,1,0:T(8,128)S(1)}, f32[12,8,128]{2,1,0:T(8,128)S(1)}, u32[]{:S(2)}, u32[]{:S(2)}) %collective-permute-start.7) | collective-permute-done | bytes 49184 | tf_op jit(solution)/shard_map/ppermute | solution.py:226
  89.1 5.8 %shard_map.59 = (f32[12,24,128]{2,1,0:T(8,128)S(1)}, f32[12,24,128]{2,1,0:T(8,128)S(1)}, f32[4,24,128]{2,1,0:T(8,128)S(1)}, f32[4,24,128]{2,1,0:T(8,128)S(1)}) custom-call(s32[2]{0:T(128)S(1)} %pad_add_fusion.flags, f32[12,24,128]{2,1,0:T(8,128)S(1)} %get-tuple-element.28.est_ref, f32[12,24,128]{2,1,0:T(8,128)S(1)} %get-tuple-element.32.total_ref, ...), custom_call_target="tpu_custom_call" | custom-call | tf_op jit(solution)/shard_map/pallas_call | solution.py:237
  94.9 1.9 %collective-permute-start.8 = (f32[4,24,128]{2,1,0:T(8,128)S(1)}, f32[4,24,128]{2,1,0:T(8,128)S(1)}, u32[]{:S(2)}, u32[]{:S(2)}) collective-permute-start(f32[4,24,128]{2,1,0:T(8,128)S(1)} %get-tuple-element.40), channel_id=1, source_target_pairs={{0,1},{1,0},{2,3},{3,2},{4,5},{5,4},{6,7},{7,6},{8,9},{9,8},{10,11... | collective-permute-start | bytes 147464 | tf_op jit(solution)/shard_map/ppermute | solution.py:227
  96.8 4.8 %collective-permute-start.9 = (f32[4,24,128]{2,1,0:T(8,128)S(1)}, f32[4,24,128]{2,1,0:T(8,128)S(1)}, u32[]{:S(2)}, u32[]{:S(2)}) collective-permute-start(f32[4,24,128]{2,1,0:T(8,128)S(1)} %get-tuple-element.41), channel_id=1, source_target_pairs={{1,2},{2,1},{3,4},{4,3},{5,6},{6,5},{7,8},{8,7},{9,10},{10,9},{11,... | collective-permute-start | bytes 147464 | tf_op jit(solution)/shard_map/ppermute | solution.py:226
  101.6 6.0 %collective-permute-done.9.far_ref = f32[4,24,128]{2,1,0:T(8,128)S(1)} collective-permute-done((f32[4,24,128]{2,1,0:T(8,128)S(1)}, f32[4,24,128]{2,1,0:T(8,128)S(1)}, u32[]{:S(2)}, u32[]{:S(2)}) %collective-permute-start.9) | collective-permute-done | bytes 49184 | tf_op jit(solution)/shard_map/ppermute | solution.py:226
  108.1 1.9 %collective-permute-start.10 = (f32[12,8,128]{2,1,0:T(8,128)S(1)}, f32[12,8,128]{2,1,0:T(8,128)S(1)}, u32[]{:S(2)}, u32[]{:S(2)}) collective-permute-start(f32[12,8,128]{2,1,0:T(8,128)S(1)} %get-tuple-element.43), channel_id=1, source_target_pairs={{0,32},{32,0},{64,96},{96,64},{128,160},{160,128},{192,224},{224,1... | collective-permute-start | bytes 147464 | tf_op jit(solution)/shard_map/ppermute | solution.py:227
  110.1 1.9 %collective-permute-start.11 = (f32[12,8,128]{2,1,0:T(8,128)S(1)}, f32[12,8,128]{2,1,0:T(8,128)S(1)}, u32[]{:S(2)}, u32[]{:S(2)}) collective-permute-start(f32[12,8,128]{2,1,0:T(8,128)S(1)} %get-tuple-element.44), channel_id=1, source_target_pairs={{32,64},{64,32},{96,128},{128,96},{160,192},{192,160},{224,256},{2... | collective-permute-start | bytes 147464 | tf_op jit(solution)/shard_map/ppermute | solution.py:226
  112.0 2.1 %collective-permute-done.10.yn_ref = f32[12,8,128]{2,1,0:T(8,128)S(1)} collective-permute-done((f32[12,8,128]{2,1,0:T(8,128)S(1)}, f32[12,8,128]{2,1,0:T(8,128)S(1)}, u32[]{:S(2)}, u32[]{:S(2)}) %collective-permute-start.10) | collective-permute-done | bytes 49184 | tf_op jit(solution)/shard_map/ppermute | solution.py:227
  114.1 4.0 %collective-permute-done.11.yf_ref = f32[12,8,128]{2,1,0:T(8,128)S(1)} collective-permute-done((f32[12,8,128]{2,1,0:T(8,128)S(1)}, f32[12,8,128]{2,1,0:T(8,128)S(1)}, u32[]{:S(2)}, u32[]{:S(2)}) %collective-permute-start.11) | collective-permute-done | bytes 49184 | tf_op jit(solution)/shard_map/ppermute | solution.py:226
  (22 shorter events, 6.7 us)
Async XLA Ops:
  0.0 1.2 %copy-start = (f32[1,8,256,128]{3,2,1,0:T(8,128)S(1)}, f32[1,8,256,128]{3,2,1,0:T(8,128)}, u32[]{:S(2)}) copy-start(f32[1,8,256,128]{3,2,1,0:T(8,128)} %images_ref.1) | copy-start | bytes 3145732
  1.2 0.7 copy-start.1
  1.9 0.7 copy-start.2
  2.5 0.7 copy-start.3
  4.3 8.8 %copy-start.4 = (f32[8,16,128]{2,1,0:T(8,128)S(1)}, f32[8,16,128]{2,1,0:T(8,128)}, u32[]{:S(2)}) copy-start(f32[8,16,128]{2,1,0:T(8,128)} %param.5) | copy-start | bytes 196612
  4.3 54.6 %all-to-all-start = ((f32[16,136,128]{2,1,0:T(8,128)}), f32[16,136,128]{2,1,0:T(8,128)S(1)}, u32[]{:S(2)}, u32[]{:S(2)}) async-start(f32[16,136,128]{2,1,0:T(8,128)} %shard_map.56), calls=%async_computation | async-start | bytes 2228224 | tf_op jit(solution)/shard_map/all_to_all | solution.py:271
  13.1 33.8 %collective-permute-start.1 = (f32[4,24,128]{2,1,0:T(8,128)S(1)}, f32[4,24,128]{2,1,0:T(8,128)S(1)}, u32[]{:S(2)}, u32[]{:S(2)}) collective-permute-start(f32[4,24,128]{2,1,0:T(8,128)S(1)} %get-tuple-element.45), channel_id=1, source_target_pairs={{1,2},{2,1},{3,4},{4,3},{5,6},{6,5},{7,8},{8,7},{9,10},{10,9},{11,... | collective-permute-start | bytes 147464 | tf_op jit(solution)/shard_map/ppermute | solution.py:226
  22.3 24.6 %collective-permute-start = (f32[4,24,128]{2,1,0:T(8,128)S(1)}, f32[4,24,128]{2,1,0:T(8,128)S(1)}, u32[]{:S(2)}, u32[]{:S(2)}) collective-permute-start(f32[4,24,128]{2,1,0:T(8,128)S(1)} %get-tuple-element.46), channel_id=1, source_target_pairs={{0,1},{1,0},{2,3},{3,2},{4,5},{5,4},{6,7},{7,6},{8,9},{9,8},{10,11... | collective-permute-start | bytes 147464 | tf_op jit(solution)/shard_map/ppermute | solution.py:227
  47.5 6.0 %collective-permute-start.2 = (f32[12,8,128]{2,1,0:T(8,128)S(1)}, f32[12,8,128]{2,1,0:T(8,128)S(1)}, u32[]{:S(2)}, u32[]{:S(2)}) collective-permute-start(f32[12,8,128]{2,1,0:T(8,128)S(1)} %get-tuple-element.26), channel_id=1, source_target_pairs={{0,32},{32,0},{64,96},{96,64},{128,160},{160,128},{192,224},{224,1... | collective-permute-start | bytes 147464 | tf_op jit(solution)/shard_map/ppermute | solution.py:227
  50.9 8.1 %collective-permute-start.3 = (f32[12,8,128]{2,1,0:T(8,128)S(1)}, f32[12,8,128]{2,1,0:T(8,128)S(1)}, u32[]{:S(2)}, u32[]{:S(2)}) collective-permute-start(f32[12,8,128]{2,1,0:T(8,128)S(1)} %get-tuple-element.27), channel_id=1, source_target_pairs={{32,64},{64,32},{96,128},{128,96},{160,192},{192,160},{224,256},{2... | collective-permute-start | bytes 147464 | tf_op jit(solution)/shard_map/ppermute | solution.py:226
  66.4 7.5 %collective-permute-start.4 = (f32[4,24,128]{2,1,0:T(8,128)S(1)}, f32[4,24,128]{2,1,0:T(8,128)S(1)}, u32[]{:S(2)}, u32[]{:S(2)}) collective-permute-start(f32[4,24,128]{2,1,0:T(8,128)S(1)} %get-tuple-element.30), channel_id=1, source_target_pairs={{0,1},{1,0},{2,3},{3,2},{4,5},{5,4},{6,7},{7,6},{8,9},{9,8},{10,11... | collective-permute-start | bytes 147464 | tf_op jit(solution)/shard_map/ppermute | solution.py:227
  68.3 10.2 %collective-permute-start.5 = (f32[4,24,128]{2,1,0:T(8,128)S(1)}, f32[4,24,128]{2,1,0:T(8,128)S(1)}, u32[]{:S(2)}, u32[]{:S(2)}) collective-permute-start(f32[4,24,128]{2,1,0:T(8,128)S(1)} %get-tuple-element.31), channel_id=1, source_target_pairs={{1,2},{2,1},{3,4},{4,3},{5,6},{6,5},{7,8},{8,7},{9,10},{10,9},{11,... | collective-permute-start | bytes 147464 | tf_op jit(solution)/shard_map/ppermute | solution.py:226
  79.1 6.0 %collective-permute-start.6 = (f32[12,8,128]{2,1,0:T(8,128)S(1)}, f32[12,8,128]{2,1,0:T(8,128)S(1)}, u32[]{:S(2)}, u32[]{:S(2)}) collective-permute-start(f32[12,8,128]{2,1,0:T(8,128)S(1)} %get-tuple-element.33), channel_id=1, source_target_pairs={{0,32},{32,0},{64,96},{96,64},{128,160},{160,128},{192,224},{224,1... | collective-permute-start | bytes 147464 | tf_op jit(solution)/shard_map/ppermute | solution.py:227
  81.0 8.1 %collective-permute-start.7 = (f32[12,8,128]{2,1,0:T(8,128)S(1)}, f32[12,8,128]{2,1,0:T(8,128)S(1)}, u32[]{:S(2)}, u32[]{:S(2)}) collective-permute-start(f32[12,8,128]{2,1,0:T(8,128)S(1)} %get-tuple-element.34), channel_id=1, source_target_pairs={{32,64},{64,32},{96,128},{128,96},{160,192},{192,160},{224,256},{2... | collective-permute-start | bytes 147464 | tf_op jit(solution)/shard_map/ppermute | solution.py:226
  94.9 6.7 %collective-permute-start.8 = (f32[4,24,128]{2,1,0:T(8,128)S(1)}, f32[4,24,128]{2,1,0:T(8,128)S(1)}, u32[]{:S(2)}, u32[]{:S(2)}) collective-permute-start(f32[4,24,128]{2,1,0:T(8,128)S(1)} %get-tuple-element.40), channel_id=1, source_target_pairs={{0,1},{1,0},{2,3},{3,2},{4,5},{5,4},{6,7},{7,6},{8,9},{9,8},{10,11... | collective-permute-start | bytes 147464 | tf_op jit(solution)/shard_map/ppermute | solution.py:227
  96.8 10.7 %collective-permute-start.9 = (f32[4,24,128]{2,1,0:T(8,128)S(1)}, f32[4,24,128]{2,1,0:T(8,128)S(1)}, u32[]{:S(2)}, u32[]{:S(2)}) collective-permute-start(f32[4,24,128]{2,1,0:T(8,128)S(1)} %get-tuple-element.41), channel_id=1, source_target_pairs={{1,2},{2,1},{3,4},{4,3},{5,6},{6,5},{7,8},{8,7},{9,10},{10,9},{11,... | collective-permute-start | bytes 147464 | tf_op jit(solution)/shard_map/ppermute | solution.py:226
  108.1 6.0 %collective-permute-start.10 = (f32[12,8,128]{2,1,0:T(8,128)S(1)}, f32[12,8,128]{2,1,0:T(8,128)S(1)}, u32[]{:S(2)}, u32[]{:S(2)}) collective-permute-start(f32[12,8,128]{2,1,0:T(8,128)S(1)} %get-tuple-element.43), channel_id=1, source_target_pairs={{0,32},{32,0},{64,96},{96,64},{128,160},{160,128},{192,224},{224,1... | collective-permute-start | bytes 147464 | tf_op jit(solution)/shard_map/ppermute | solution.py:227
  110.1 8.1 %collective-permute-start.11 = (f32[12,8,128]{2,1,0:T(8,128)S(1)}, f32[12,8,128]{2,1,0:T(8,128)S(1)}, u32[]{:S(2)}, u32[]{:S(2)}) collective-permute-start(f32[12,8,128]{2,1,0:T(8,128)S(1)} %get-tuple-element.44), channel_id=1, source_target_pairs={{32,64},{64,32},{96,128},{128,96},{160,192},{192,160},{224,256},{2... | collective-permute-start | bytes 147464 | tf_op jit(solution)/shard_map/ppermute | solution.py:226

commit v4 on v3

--- a/solution.py
+++ b/solution.py
@@ -20,9 +20,11 @@
     return high, low
 
 
-def stacked(x):
-    high, low = split(x)
-    return jnp.concatenate([high, low, high], axis=1)
+def product(x, matrix):
+    left = jnp.concatenate(split(x), axis=1)
+    right = jnp.concatenate([matrix, matrix], axis=0)
+    both = jnp.dot(left, right, preferred_element_type=jnp.float32)
+    return both[:, 0:LANES] + both[:, LANES:]
 
 
 def banded(row, radius):
@@ -38,18 +40,42 @@
     return jnp.where(even, high, low), jnp.where(even, low, high)
 
 
-def pieces_kernel(images_ref, first_ref, second_ref, axial_ref, out_ref, taps):
+def pieces_kernel(images_ref, axial_ref, first_ref, second_ref, out_ref, rows, taps, axial, taps_1, taps_2, taps_sems, in_sems, out_sems):
+    small = [
+        pltpu.make_async_copy(src, dst, taps_sems.at[k])
+        for k, (src, dst) in enumerate(
+            ((axial_ref, axial), (first_ref, taps_1), (second_ref, taps_2))
+        )
+    ]
+    ins = [
+        pltpu.make_async_copy(images_ref.at[i], rows.at[i], in_sems.at[i]) for i in range(ROWS)
+    ]
+    outs = [
+        pltpu.make_async_copy(
+            rows.at[i], out_ref.at[:, pl.ds(WIDTH * i, WIDTH), :], out_sems.at[i]
+        )
+        for i in range(ROWS)
+    ]
+    outs.append(pltpu.make_async_copy(taps, out_ref.at[:, pl.ds(BLOCK, 8), :], out_sems.at[ROWS]))
+    for copy in small + ins:
+        copy.start()
     taps[...] = jnp.zeros_like(taps)
-    for row, ref in enumerate((axial_ref, first_ref, second_ref)):
-        taps[row : row + 1, 0 : ref.shape[1]] = ref[...]
-    for w in range(out_ref.shape[0]):
-        for i in range(ROWS):
-            out_ref[w, WIDTH * i : WIDTH * (i + 1), :] = images_ref[0, i, WIDTH * w : WIDTH * (w + 1), :]
-        out_ref[w, BLOCK:, :] = taps[...]
+    for copy in small:
+        copy.wait()
+    for row, ref in enumerate((axial, taps_1, taps_2)):
+        taps[:, row : row + 1, 0 : ref.shape[1]] = jnp.broadcast_to(
+            ref[...][None], (taps.shape[0], 1, ref.shape[1])
+        )
+    outs[ROWS].start()
+    for i in range(ROWS):
+        ins[i].wait()
+        outs[i].start()
+    for copy in outs:
+        copy.wait()
 
 
 def make_tables(sizes, data_ref, conv_ref, corr_ref, table_ref, axial):
-    nf, ns, nz = sizes
+    _, _, nz = sizes
     views = data_ref.shape[0]
     lane = lax.broadcasted_iota(jnp.int32, (8, LANES), 1)
     sub = lax.broadcasted_iota(jnp.int32, (8, LANES), 0)
@@ -65,20 +91,21 @@
     def one(v, carry):
         for at, ref in ((0, conv_ref), (views, corr_ref)):
             high, low = split(banded(axial[pl.ds(at + v, 1), :], nz // 2))
-            ref[v, 0:LANES] = high
-            ref[v, LANES : 2 * LANES] = high
-            ref[v, 2 * LANES : 3 * LANES] = low
+            ref[v, :, 0:LANES] = high
+            ref[v, :, LANES:] = low
         start = 0
-        for row, count in ((1, nf), (2, ns)):
+        for row in (1, 2):
             taps = jnp.broadcast_to(data_ref[v, BLOCK + row : BLOCK + row + 1, :], (8, LANES))
             column = jnp.sum(jnp.where(lane == sub, taps, 0.0), axis=1, keepdims=True)
-            column = jnp.broadcast_to(column, (8, LANES))
-            for k in range(count):
-                table_ref[v, start + k] = jnp.broadcast_to(column[k : k + 1], (8, LANES))
-            start += count
+            table_ref[v, start : start + 8, :] = jnp.broadcast_to(column, (8, LANES))
+            start += 8
         return carry
 
     lax.fori_loop(0, views, one, 0, unroll=2)
+
+
+def tap(table_ref, v, k):
+    return jnp.broadcast_to(table_ref[v, pl.ds(k, 1), :], (8, LANES))
 
 
 def conv_part(sizes, est_ref, conv_ref, table_ref, spread, finish):
@@ -90,7 +117,7 @@
             [est_ref[i, k + 8 * h : k + 8 * h + 8, :] for h in range(2)] for k in range(ns)
         ]
         for v in range(views):
-            taps = [table_ref[v, nf + ns - 1 - k] for k in range(ns)]
+            taps = [tap(table_ref, v, 8 + ns - 1 - k) for k in range(ns)]
             for h in range(2):
                 t = taps[0] * shifted[0][h]
                 for k in range(1, ns):
@@ -101,7 +128,7 @@
     lax.fori_loop(0, wide, row, 0)
 
     def one(v, carry):
-        first = [table_ref[v, k] for k in range(nf)]
+        first = [tap(table_ref, v, k) for k in range(nf)]
         out = []
         for i in range(ROWS):
             for h in range(2):
@@ -109,8 +136,7 @@
                 for k in range(1, nf):
                     t = t + first[k] * spread[v, i + nf - 1 - k, 8 * h : 8 * h + 8, :]
                 out.append(t)
-        x = stacked(jnp.concatenate(out, axis=0))
-        finish(v, jnp.dot(x, conv_ref[v], preferred_element_type=jnp.float32))
+        finish(v, product(jnp.concatenate(out, axis=0), conv_ref[v]))
         return carry
 
     lax.fori_loop(0, views, one, 0, unroll=2)
@@ -121,8 +147,8 @@
     wide, views = spread.shape[1], spread.shape[0]
 
     def one(v, carry):
-        first = [table_ref[v, k] for k in range(nf)]
-        back = jnp.dot(stacked(ratio_of(v)), corr_ref[v], preferred_element_type=jnp.float32)
+        first = [tap(table_ref, v, k) for k in range(nf)]
+        back = product(ratio_of(v), corr_ref[v])
         for i in range(wide):
             for h in range(2):
                 t = None
@@ -135,16 +161,16 @@
                 spread[v, i, 8 * h : 8 * h + 8, :] = t
         return carry
 
-    lax.fori_loop(0, views, one, 0, unroll=2)
+    lax.fori_loop(0, views, one, 0, unroll=4)
 
     def row(i, carry):
         sums = [[None, None] for _ in range(ns)]
         for v in range(views):
             g = [spread[v, i, 8 * h : 8 * h + 8, :] for h in range(2)]
             for k in range(ns):
-                tap = table_ref[v, nf + ns - 1 - k]
+                t = tap(table_ref, v, 8 + ns - 1 - k)
                 for h in range(2):
-                    u = tap * g[h]
+                    u = t * g[h]
                     sums[k][h] = u if sums[k][h] is None else sums[k][h] + u
         total = None
         for k in range(ns):
@@ -167,6 +193,17 @@
     return jnp.where(even, yf, yn), jnp.where(even, yn, yf)
 
 
+def both_parts(sizes, flags, est_ref, data_ref, conv_ref, corr_ref, table_ref, part_ref, near_ref, far_ref, spread, ratio):
+    def finish(v, blurred):
+        ratio[v] = data_ref[v, 0:BLOCK, :] / blurred
+
+    conv_part(sizes, est_ref, conv_ref, table_ref, spread, finish)
+    corr_part(
+        sizes, flags, lambda v: ratio[v],
+        corr_ref, table_ref, spread, part_ref, near_ref, far_ref,
+    )
+
+
 def first_kernel(sizes, flags, total_ref, yn_ref, yf_ref, data_ref, est_ref, part_ref, near_ref, far_ref, conv_ref, corr_ref, table_ref, spread, ratio, axial):
     make_tables(sizes, data_ref, conv_ref, corr_ref, table_ref, axial)
     low, high = sides(flags, yn_ref, yf_ref)
@@ -174,17 +211,6 @@
     est_ref[:, 8:16, :] = total_ref[:, 8:16, :]
     est_ref[:, 16:24, :] = total_ref[:, 16:24, :] + high
     both_parts(sizes, flags, est_ref, data_ref, conv_ref, corr_ref, table_ref, part_ref, near_ref, far_ref, spread, ratio)
-
-
-def both_parts(sizes, flags, est_ref, data_ref, conv_ref, corr_ref, table_ref, part_ref, near_ref, far_ref, spread, ratio):
-    def finish(v, blurred):
-        ratio[v] = data_ref[v, 0:BLOCK, :] / blurred
-
-    conv_part(sizes, est_ref, conv_ref, table_ref, spread, finish)
-    corr_part(
-        sizes, flags, lambda v: ratio[v],
-        corr_ref, table_ref, spread, part_ref, near_ref, far_ref,
-    )
 
 
 def updated(views, flags, est_ref, total_ref, yn_ref, yf_ref, new_ref):
@@ -259,17 +285,25 @@
     near, far = edges(flags[0], own[0:halo], own[wide - halo :])
     near, far = swapped(near, far, "tile")
 
-    data_shape = (views, rows * cols + 8, lanes)
+    hbm = pl.BlockSpec(memory_space=pltpu.HBM)
+    small = (taps_axial, taps_first, taps_second)
     data = pl.pallas_call(
         pieces_kernel,
-        in_specs=[VMEM] * 4,
-        out_specs=VMEM,
-        out_shape=jax.ShapeDtypeStruct(data_shape, jnp.float32),
-        scratch_shapes=[pltpu.VMEM((8, lanes), jnp.float32)],
-        compiler_params=pltpu.CompilerParams(vmem_limit_bytes=4 << 20),
-    )(images, taps_first, taps_second, taps_axial)
+        in_specs=[hbm] * 4,
+        out_specs=hbm,
+        out_shape=jax.ShapeDtypeStruct((views, rows * cols + 8, lanes), jnp.float32),
+        scratch_shapes=[
+            pltpu.VMEM((rows, views, cols, lanes), jnp.float32),
+            pltpu.VMEM((views, 8, lanes), jnp.float32),
+            *(pltpu.VMEM(x.shape, jnp.float32) for x in small),
+            pltpu.SemaphoreType.DMA((3,)),
+            pltpu.SemaphoreType.DMA((rows,)),
+            pltpu.SemaphoreType.DMA((rows + 1,)),
+        ],
+        compiler_params=pltpu.CompilerParams(vmem_limit_bytes=60 << 20),
+    )(images.reshape(rows, views, cols, lanes), *small)
     data = lax.all_to_all(data, "view", 0, 0, tiled=True)
-    matrices = jax.ShapeDtypeStruct((views, 3 * lanes, lanes), jnp.bfloat16)
+    matrices = jax.ShapeDtypeStruct((views, lanes, 2 * lanes), jnp.bfloat16)
 
     block, strip, side = (wide, COLS, lanes), (halo, COLS, lanes), (wide, 8, lanes)
     scratch = [
@@ -286,7 +320,7 @@
     current, part, near, far, conv, corr, table = call(
         functools.partial(first_kernel, sizes),
         (flags, total, yn, yf, data),
-        (block, block, strip, strip, matrices, matrices, (views, nf + ns, 8, lanes)),
+        (block, block, strip, strip, matrices, matrices, (views, 16, lanes)),
         scratch + [pltpu.VMEM((2 * views, lanes), jnp.float32)],
         limit=16 << 20,
     )

time: 120 us -> 116 us (0.967)
  local copies, waits for them, and re-layouts: 3.2 us -> 0.02 us
    unnamed x10 -> x2, local copies, waits for them, and re-layouts: 3.19 us -> 0.01 us
    pallas_call x6, Pallas kernels: 16.1 us -> 14.5 us  [call(): pl.pallas_call(kernel, in_specs=[SMEM] + [VMEM] * (len(ins) - 1), out_spe...]
where the time goes in v4:
time: 116 us
  waiting for transfers between devices  51.6 us (44%)
  starting transfers between devices  47.1 us (41%)
  Pallas kernels  16.8 us (14%)
    ppermute x6, waiting for transfers between devices, swapped(): far = lax.ppermute(far, axis, pairs(count, 1))  46.7 us
    ppermute x6, starting transfers between devices, swapped(): far = lax.ppermute(far, axis, pairs(count, 1))  25.3 us
    pallas_call x6, Pallas kernels, call(): pl.pallas_call(kernel, in_specs=[SMEM] + [VMEM] * (len(ins) - 1), out_spe...  14.5 us
    ppermute x6, starting transfers between devices, swapped(): near = lax.ppermute(near, axis, pairs(count, 0))  13 us
    all_to_all x1, starting transfers between devices, local(): data = lax.all_to_all(data, 'view', 0, 0, tiled=True)  8.8 us
    ppermute x6, waiting for transfers between devices, swapped(): near = lax.ppermute(near, axis, pairs(count, 0))  4.9 us
  transfers between devices with their start and end apart: 13, of which 9 were waited for; matrix products, arithmetic and copies ran while one was open for 0% of the time, Pallas kernels for 0%

profile of v4, /device:TPU:38, one launch (start us, length us, event | category | flops | bytes accessed | tf_op | source)
XLA Modules:
  0.0 115.8 jit_solution(10279970301048839677)
XLA Ops:
  0.0 2.3 %shard_map.56 = f32[16,136,128]{2,1,0:T(8,128)} custom-call(f32[8,16,16,128]{3,2,1,0:T(8,128)} %bitcast.3, f32[1,33]{1,0:T(1,128)} %axial_ref.1, f32[1,5]{1,0:T(1,128)} %first_ref.1, f32[1,7]{1,0:T(1,128)} %second_ref.1), custom_call_target="tpu_custom_call" | custom-call | tf_op jit(solution)/shard_map/pallas_call | solution.py:290
  2.3 8.8 %all-to-all-start = ((f32[16,136,128]{2,1,0:T(8,128)}), f32[16,136,128]{2,1,0:T(8,128)S(1)}, u32[]{:S(2)}, u32[]{:S(2)}) async-start(f32[16,136,128]{2,1,0:T(8,128)} %shard_map.56), calls=%async_computation | async-start | bytes 2228224 | tf_op jit(solution)/shard_map/all_to_all | solution.py:305
  11.1 9.2 %collective-permute-start.1 = (f32[4,24,128]{2,1,0:T(8,128)S(1)}, f32[4,24,128]{2,1,0:T(8,128)S(1)}, u32[]{:S(2)}, u32[]{:S(2)}) collective-permute-start(f32[4,24,128]{2,1,0:T(8,128)S(1)} %get-tuple-element.45), channel_id=1, source_target_pairs={{1,2},{2,1},{3,4},{4,3},{5,6},{6,5},{7,8},{8,7},{9,10},{10,9},{11,... | collective-permute-start | bytes 147464 | tf_op jit(solution)/shard_map/ppermute | solution.py:252
  20.3 1.9 %collective-permute-start = (f32[4,24,128]{2,1,0:T(8,128)S(1)}, f32[4,24,128]{2,1,0:T(8,128)S(1)}, u32[]{:S(2)}, u32[]{:S(2)}) collective-permute-start(f32[4,24,128]{2,1,0:T(8,128)S(1)} %get-tuple-element.46), channel_id=1, source_target_pairs={{0,1},{1,0},{2,3},{3,2},{4,5},{5,4},{6,7},{7,6},{8,9},{9,8},{10,11... | collective-permute-start | bytes 147464 | tf_op jit(solution)/shard_map/ppermute | solution.py:253
  22.3 22.6 %collective-permute-done.1.far_ref = f32[4,24,128]{2,1,0:T(8,128)S(1)} collective-permute-done((f32[4,24,128]{2,1,0:T(8,128)S(1)}, f32[4,24,128]{2,1,0:T(8,128)S(1)}, u32[]{:S(2)}, u32[]{:S(2)}) %collective-permute-start.1) | collective-permute-done | bytes 49184 | tf_op jit(solution)/shard_map/ppermute | solution.py:252
  45.5 3.4 %collective-permute-start.2 = (f32[12,8,128]{2,1,0:T(8,128)S(1)}, f32[12,8,128]{2,1,0:T(8,128)S(1)}, u32[]{:S(2)}, u32[]{:S(2)}) collective-permute-start(f32[12,8,128]{2,1,0:T(8,128)S(1)} %get-tuple-element.26), channel_id=1, source_target_pairs={{0,32},{32,0},{64,96},{96,64},{128,160},{160,128},{192,224},{224,1... | collective-permute-start | bytes 147464 | tf_op jit(solution)/shard_map/ppermute | solution.py:253
  48.8 1.9 %collective-permute-start.3 = (f32[12,8,128]{2,1,0:T(8,128)S(1)}, f32[12,8,128]{2,1,0:T(8,128)S(1)}, u32[]{:S(2)}, u32[]{:S(2)}) collective-permute-start(f32[12,8,128]{2,1,0:T(8,128)S(1)} %get-tuple-element.27), channel_id=1, source_target_pairs={{32,64},{64,32},{96,128},{128,96},{160,192},{192,160},{224,256},{2... | collective-permute-start | bytes 147464 | tf_op jit(solution)/shard_map/ppermute | solution.py:252
  51.5 5.5 %collective-permute-done.3.yf_ref = f32[12,8,128]{2,1,0:T(8,128)S(1)} collective-permute-done((f32[12,8,128]{2,1,0:T(8,128)S(1)}, f32[12,8,128]{2,1,0:T(8,128)S(1)}, u32[]{:S(2)}, u32[]{:S(2)}) %collective-permute-start.3) | collective-permute-done | bytes 49184 | tf_op jit(solution)/shard_map/ppermute | solution.py:252
  56.9 6.6 %shard_map.57 = (f32[12,24,128]{2,1,0:T(8,128)S(1)}, f32[12,24,128]{2,1,0:T(8,128)S(1)}, f32[4,24,128]{2,1,0:T(8,128)S(1)}, f32[4,24,128]{2,1,0:T(8,128)S(1)}, b...) custom-call(s32[2]{0:T(128)S(1)} %pad_add_fusion.flags, ...), custom_call_target="tpu_custom_call" | custom-call | tf_op jit(solution)/shard_map/pallas_call | solution.py:263
  63.6 1.9 %collective-permute-start.4 = (f32[4,24,128]{2,1,0:T(8,128)S(1)}, f32[4,24,128]{2,1,0:T(8,128)S(1)}, u32[]{:S(2)}, u32[]{:S(2)}) collective-permute-start(f32[4,24,128]{2,1,0:T(8,128)S(1)} %get-tuple-element.30), channel_id=1, source_target_pairs={{0,1},{1,0},{2,3},{3,2},{4,5},{5,4},{6,7},{7,6},{8,9},{9,8},{10,11... | collective-permute-start | bytes 147464 | tf_op jit(solution)/shard_map/ppermute | solution.py:253
  65.5 5.6 %collective-permute-start.5 = (f32[4,24,128]{2,1,0:T(8,128)S(1)}, f32[4,24,128]{2,1,0:T(8,128)S(1)}, u32[]{:S(2)}, u32[]{:S(2)}) collective-permute-start(f32[4,24,128]{2,1,0:T(8,128)S(1)} %get-tuple-element.31), channel_id=1, source_target_pairs={{1,2},{2,1},{3,4},{4,3},{5,6},{6,5},{7,8},{8,7},{9,10},{10,9},{11,... | collective-permute-start | bytes 147464 | tf_op jit(solution)/shard_map/ppermute | solution.py:252
  71.1 4.6 %collective-permute-done.5.far_ref = f32[4,24,128]{2,1,0:T(8,128)S(1)} collective-permute-done((f32[4,24,128]{2,1,0:T(8,128)S(1)}, f32[4,24,128]{2,1,0:T(8,128)S(1)}, u32[]{:S(2)}, u32[]{:S(2)}) %collective-permute-start.5) | collective-permute-done | bytes 49184 | tf_op jit(solution)/shard_map/ppermute | solution.py:252
  76.3 1.9 %collective-permute-start.6 = (f32[12,8,128]{2,1,0:T(8,128)S(1)}, f32[12,8,128]{2,1,0:T(8,128)S(1)}, u32[]{:S(2)}, u32[]{:S(2)}) collective-permute-start(f32[12,8,128]{2,1,0:T(8,128)S(1)} %get-tuple-element.33), channel_id=1, source_target_pairs={{0,32},{32,0},{64,96},{96,64},{128,160},{160,128},{192,224},{224,1... | collective-permute-start | bytes 147464 | tf_op jit(solution)/shard_map/ppermute | solution.py:253
  78.2 2.0 %collective-permute-start.7 = (f32[12,8,128]{2,1,0:T(8,128)S(1)}, f32[12,8,128]{2,1,0:T(8,128)S(1)}, u32[]{:S(2)}, u32[]{:S(2)}) collective-permute-start(f32[12,8,128]{2,1,0:T(8,128)S(1)} %get-tuple-element.34), channel_id=1, source_target_pairs={{32,64},{64,32},{96,128},{128,96},{160,192},{192,160},{224,256},{2... | collective-permute-start | bytes 147464 | tf_op jit(solution)/shard_map/ppermute | solution.py:252
  80.2 2.1 %collective-permute-done.6.yn_ref = f32[12,8,128]{2,1,0:T(8,128)S(1)} collective-permute-done((f32[12,8,128]{2,1,0:T(8,128)S(1)}, f32[12,8,128]{2,1,0:T(8,128)S(1)}, u32[]{:S(2)}, u32[]{:S(2)}) %collective-permute-start.6) | collective-permute-done | bytes 49184 | tf_op jit(solution)/shard_map/ppermute | solution.py:253
  82.3 4.0 %collective-permute-done.7.yf_ref = f32[12,8,128]{2,1,0:T(8,128)S(1)} collective-permute-done((f32[12,8,128]{2,1,0:T(8,128)S(1)}, f32[12,8,128]{2,1,0:T(8,128)S(1)}, u32[]{:S(2)}, u32[]{:S(2)}) %collective-permute-start.7) | collective-permute-done | bytes 49184 | tf_op jit(solution)/shard_map/ppermute | solution.py:252
  86.3 5.0 %shard_map.59 = (f32[12,24,128]{2,1,0:T(8,128)S(1)}, f32[12,24,128]{2,1,0:T(8,128)S(1)}, f32[4,24,128]{2,1,0:T(8,128)S(1)}, f32[4,24,128]{2,1,0:T(8,128)S(1)}) custom-call(s32[2]{0:T(128)S(1)} %pad_add_fusion.flags, f32[12,24,128]{2,1,0:T(8,128)S(1)} %get-tuple-element.28.est_ref, f32[12,24,128]{2,1,0:T(8,128)S(1)} %get-tuple-element.32.total_ref, ...), custom_call_target="tpu_custom_call" | custom-call | tf_op jit(solution)/shard_map/pallas_call | solution.py:263
  91.3 1.9 %collective-permute-start.8 = (f32[4,24,128]{2,1,0:T(8,128)S(1)}, f32[4,24,128]{2,1,0:T(8,128)S(1)}, u32[]{:S(2)}, u32[]{:S(2)}) collective-permute-start(f32[4,24,128]{2,1,0:T(8,128)S(1)} %get-tuple-element.40), channel_id=1, source_target_pairs={{0,1},{1,0},{2,3},{3,2},{4,5},{5,4},{6,7},{7,6},{8,9},{9,8},{10,11... | collective-permute-start | bytes 147464 | tf_op jit(solution)/shard_map/ppermute | solution.py:253
  93.2 4.8 %collective-permute-start.9 = (f32[4,24,128]{2,1,0:T(8,128)S(1)}, f32[4,24,128]{2,1,0:T(8,128)S(1)}, u32[]{:S(2)}, u32[]{:S(2)}) collective-permute-start(f32[4,24,128]{2,1,0:T(8,128)S(1)} %get-tuple-element.41), channel_id=1, source_target_pairs={{1,2},{2,1},{3,4},{4,3},{5,6},{6,5},{7,8},{8,7},{9,10},{10,9},{11,... | collective-permute-start | bytes 147464 | tf_op jit(solution)/shard_map/ppermute | solution.py:252
  98.0 6.0 %collective-permute-done.9.far_ref = f32[4,24,128]{2,1,0:T(8,128)S(1)} collective-permute-done((f32[4,24,128]{2,1,0:T(8,128)S(1)}, f32[4,24,128]{2,1,0:T(8,128)S(1)}, u32[]{:S(2)}, u32[]{:S(2)}) %collective-permute-start.9) | collective-permute-done | bytes 49184 | tf_op jit(solution)/shard_map/ppermute | solution.py:252
  104.5 1.9 %collective-permute-start.10 = (f32[12,8,128]{2,1,0:T(8,128)S(1)}, f32[12,8,128]{2,1,0:T(8,128)S(1)}, u32[]{:S(2)}, u32[]{:S(2)}) collective-permute-start(f32[12,8,128]{2,1,0:T(8,128)S(1)} %get-tuple-element.43), channel_id=1, source_target_pairs={{0,32},{32,0},{64,96},{96,64},{128,160},{160,128},{192,224},{224,1... | collective-permute-start | bytes 147464 | tf_op jit(solution)/shard_map/ppermute | solution.py:253
  106.5 1.9 %collective-permute-start.11 = (f32[12,8,128]{2,1,0:T(8,128)S(1)}, f32[12,8,128]{2,1,0:T(8,128)S(1)}, u32[]{:S(2)}, u32[]{:S(2)}) collective-permute-start(f32[12,8,128]{2,1,0:T(8,128)S(1)} %get-tuple-element.44), channel_id=1, source_target_pairs={{32,64},{64,32},{96,128},{128,96},{160,192},{192,160},{224,256},{2... | collective-permute-start | bytes 147464 | tf_op jit(solution)/shard_map/ppermute | solution.py:252
  108.4 2.1 %collective-permute-done.10.yn_ref = f32[12,8,128]{2,1,0:T(8,128)S(1)} collective-permute-done((f32[12,8,128]{2,1,0:T(8,128)S(1)}, f32[12,8,128]{2,1,0:T(8,128)S(1)}, u32[]{:S(2)}, u32[]{:S(2)}) %collective-permute-start.10) | collective-permute-done | bytes 49184 | tf_op jit(solution)/shard_map/ppermute | solution.py:253
  110.5 4.0 %collective-permute-done.11.yf_ref = f32[12,8,128]{2,1,0:T(8,128)S(1)} collective-permute-done((f32[12,8,128]{2,1,0:T(8,128)S(1)}, f32[12,8,128]{2,1,0:T(8,128)S(1)}, u32[]{:S(2)}, u32[]{:S(2)}) %collective-permute-start.11) | collective-permute-done | bytes 49184 | tf_op jit(solution)/shard_map/ppermute | solution.py:252
  (14 shorter events, 3.7 us)
Async XLA Ops:
  2.3 8.8 %copy-start = (f32[8,16,128]{2,1,0:T(8,128)S(1)}, f32[8,16,128]{2,1,0:T(8,128)}, u32[]{:S(2)}) copy-start(f32[8,16,128]{2,1,0:T(8,128)} %param.5) | copy-start | bytes 196612
  2.3 54.7 %all-to-all-start = ((f32[16,136,128]{2,1,0:T(8,128)}), f32[16,136,128]{2,1,0:T(8,128)S(1)}, u32[]{:S(2)}, u32[]{:S(2)}) async-start(f32[16,136,128]{2,1,0:T(8,128)} %shard_map.56), calls=%async_computation | async-start | bytes 2228224 | tf_op jit(solution)/shard_map/all_to_all | solution.py:305
  11.1 33.8 %collective-permute-start.1 = (f32[4,24,128]{2,1,0:T(8,128)S(1)}, f32[4,24,128]{2,1,0:T(8,128)S(1)}, u32[]{:S(2)}, u32[]{:S(2)}) collective-permute-start(f32[4,24,128]{2,1,0:T(8,128)S(1)} %get-tuple-element.45), channel_id=1, source_target_pairs={{1,2},{2,1},{3,4},{4,3},{5,6},{6,5},{7,8},{8,7},{9,10},{10,9},{11,... | collective-permute-start | bytes 147464 | tf_op jit(solution)/shard_map/ppermute | solution.py:252
  20.3 24.6 %collective-permute-start = (f32[4,24,128]{2,1,0:T(8,128)S(1)}, f32[4,24,128]{2,1,0:T(8,128)S(1)}, u32[]{:S(2)}, u32[]{:S(2)}) collective-permute-start(f32[4,24,128]{2,1,0:T(8,128)S(1)} %get-tuple-element.46), channel_id=1, source_target_pairs={{0,1},{1,0},{2,3},{3,2},{4,5},{5,4},{6,7},{7,6},{8,9},{9,8},{10,11... | collective-permute-start | bytes 147464 | tf_op jit(solution)/shard_map/ppermute | solution.py:253
  45.5 6.0 %collective-permute-start.2 = (f32[12,8,128]{2,1,0:T(8,128)S(1)}, f32[12,8,128]{2,1,0:T(8,128)S(1)}, u32[]{:S(2)}, u32[]{:S(2)}) collective-permute-start(f32[12,8,128]{2,1,0:T(8,128)S(1)} %get-tuple-element.26), channel_id=1, source_target_pairs={{0,32},{32,0},{64,96},{96,64},{128,160},{160,128},{192,224},{224,1... | collective-permute-start | bytes 147464 | tf_op jit(solution)/shard_map/ppermute | solution.py:253
  48.8 8.1 %collective-permute-start.3 = (f32[12,8,128]{2,1,0:T(8,128)S(1)}, f32[12,8,128]{2,1,0:T(8,128)S(1)}, u32[]{:S(2)}, u32[]{:S(2)}) collective-permute-start(f32[12,8,128]{2,1,0:T(8,128)S(1)} %get-tuple-element.27), channel_id=1, source_target_pairs={{32,64},{64,32},{96,128},{128,96},{160,192},{192,160},{224,256},{2... | collective-permute-start | bytes 147464 | tf_op jit(solution)/shard_map/ppermute | solution.py:252
  63.6 7.5 %collective-permute-start.4 = (f32[4,24,128]{2,1,0:T(8,128)S(1)}, f32[4,24,128]{2,1,0:T(8,128)S(1)}, u32[]{:S(2)}, u32[]{:S(2)}) collective-permute-start(f32[4,24,128]{2,1,0:T(8,128)S(1)} %get-tuple-element.30), channel_id=1, source_target_pairs={{0,1},{1,0},{2,3},{3,2},{4,5},{5,4},{6,7},{7,6},{8,9},{9,8},{10,11... | collective-permute-start | bytes 147464 | tf_op jit(solution)/shard_map/ppermute | solution.py:253
  65.5 10.2 %collective-permute-start.5 = (f32[4,24,128]{2,1,0:T(8,128)S(1)}, f32[4,24,128]{2,1,0:T(8,128)S(1)}, u32[]{:S(2)}, u32[]{:S(2)}) collective-permute-start(f32[4,24,128]{2,1,0:T(8,128)S(1)} %get-tuple-element.31), channel_id=1, source_target_pairs={{1,2},{2,1},{3,4},{4,3},{5,6},{6,5},{7,8},{8,7},{9,10},{10,9},{11,... | collective-permute-start | bytes 147464 | tf_op jit(solution)/shard_map/ppermute | solution.py:252
  76.3 6.0 %collective-permute-start.6 = (f32[12,8,128]{2,1,0:T(8,128)S(1)}, f32[12,8,128]{2,1,0:T(8,128)S(1)}, u32[]{:S(2)}, u32[]{:S(2)}) collective-permute-start(f32[12,8,128]{2,1,0:T(8,128)S(1)} %get-tuple-element.33), channel_id=1, source_target_pairs={{0,32},{32,0},{64,96},{96,64},{128,160},{160,128},{192,224},{224,1... | collective-permute-start | bytes 147464 | tf_op jit(solution)/shard_map/ppermute | solution.py:253
  78.2 8.1 %collective-permute-start.7 = (f32[12,8,128]{2,1,0:T(8,128)S(1)}, f32[12,8,128]{2,1,0:T(8,128)S(1)}, u32[]{:S(2)}, u32[]{:S(2)}) collective-permute-start(f32[12,8,128]{2,1,0:T(8,128)S(1)} %get-tuple-element.34), channel_id=1, source_target_pairs={{32,64},{64,32},{96,128},{128,96},{160,192},{192,160},{224,256},{2... | collective-permute-start | bytes 147464 | tf_op jit(solution)/shard_map/ppermute | solution.py:252
  91.3 6.7 %collective-permute-start.8 = (f32[4,24,128]{2,1,0:T(8,128)S(1)}, f32[4,24,128]{2,1,0:T(8,128)S(1)}, u32[]{:S(2)}, u32[]{:S(2)}) collective-permute-start(f32[4,24,128]{2,1,0:T(8,128)S(1)} %get-tuple-element.40), channel_id=1, source_target_pairs={{0,1},{1,0},{2,3},{3,2},{4,5},{5,4},{6,7},{7,6},{8,9},{9,8},{10,11... | collective-permute-start | bytes 147464 | tf_op jit(solution)/shard_map/ppermute | solution.py:253
  93.2 10.7 %collective-permute-start.9 = (f32[4,24,128]{2,1,0:T(8,128)S(1)}, f32[4,24,128]{2,1,0:T(8,128)S(1)}, u32[]{:S(2)}, u32[]{:S(2)}) collective-permute-start(f32[4,24,128]{2,1,0:T(8,128)S(1)} %get-tuple-element.41), channel_id=1, source_target_pairs={{1,2},{2,1},{3,4},{4,3},{5,6},{6,5},{7,8},{8,7},{9,10},{10,9},{11,... | collective-permute-start | bytes 147464 | tf_op jit(solution)/shard_map/ppermute | solution.py:252
  104.5 6.0 %collective-permute-start.10 = (f32[12,8,128]{2,1,0:T(8,128)S(1)}, f32[12,8,128]{2,1,0:T(8,128)S(1)}, u32[]{:S(2)}, u32[]{:S(2)}) collective-permute-start(f32[12,8,128]{2,1,0:T(8,128)S(1)} %get-tuple-element.43), channel_id=1, source_target_pairs={{0,32},{32,0},{64,96},{96,64},{128,160},{160,128},{192,224},{224,1... | collective-permute-start | bytes 147464 | tf_op jit(solution)/shard_map/ppermute | solution.py:253
  106.5 8.1 %collective-permute-start.11 = (f32[12,8,128]{2,1,0:T(8,128)S(1)}, f32[12,8,128]{2,1,0:T(8,128)S(1)}, u32[]{:S(2)}, u32[]{:S(2)}) collective-permute-start(f32[12,8,128]{2,1,0:T(8,128)S(1)} %get-tuple-element.44), channel_id=1, source_target_pairs={{32,64},{64,32},{96,128},{128,96},{160,192},{192,160},{224,256},{2... | collective-permute-start | bytes 147464 | tf_op jit(solution)/shard_map/ppermute | solution.py:252

commit v5 on v4

--- a/solution.py
+++ b/solution.py
@@ -27,12 +27,18 @@
     return both[:, 0:LANES] + both[:, LANES:]
 
 
-def banded(row, radius):
-    full = jnp.broadcast_to(row, (LANES, LANES))
-    rolled = pltpu.roll(full, LANES - radius, 1, stride=1, stride_axis=0)
-    z = lax.broadcasted_iota(jnp.int32, (LANES, LANES), 0)
-    zz = lax.broadcasted_iota(jnp.int32, (LANES, LANES), 1)
-    return jnp.where(jnp.abs(zz - z) <= radius, rolled, 0.0)
+def banded(row, radius, ref):
+    full = jnp.broadcast_to(row, (16, LANES))
+    first = pltpu.roll(full, LANES - radius, 1, stride=1, stride_axis=0)
+    z = lax.broadcasted_iota(jnp.int32, (16, LANES), 0)
+    zz = lax.broadcasted_iota(jnp.int32, (16, LANES), 1)
+    for j in range(LANES // 16):
+        rows = pltpu.roll(first, 16 * j, 1) if j else first
+        if j in (0, LANES // 16 - 1):
+            rows = jnp.where(jnp.abs(zz - z - 16 * j) <= radius, rows, 0.0)
+        high, low = split(rows)
+        ref[16 * j : 16 * j + 16, 0:LANES] = high
+        ref[16 * j : 16 * j + 16, LANES:] = low
 
 
 def edges(flag, low, high):
@@ -90,9 +96,7 @@
 
     def one(v, carry):
         for at, ref in ((0, conv_ref), (views, corr_ref)):
-            high, low = split(banded(axial[pl.ds(at + v, 1), :], nz // 2))
-            ref[v, :, 0:LANES] = high
-            ref[v, :, LANES:] = low
+            banded(axial[pl.ds(at + v, 1), :], nz // 2, ref.at[v])
         start = 0
         for row in (1, 2):
             taps = jnp.broadcast_to(data_ref[v, BLOCK + row : BLOCK + row + 1, :], (8, LANES))
@@ -181,9 +185,9 @@
         return carry
 
     lax.fori_loop(0, wide, row, 0)
-    halo = nf - 1
+    strip = near_ref.shape[0]
     near_ref[...], far_ref[...] = edges(
-        flags[0], part_ref[0:halo], part_ref[wide - halo : wide]
+        flags[0], part_ref[0:strip], part_ref[wide - strip : wide]
     )
 
 
@@ -226,18 +230,23 @@
 
 
 def rows_kernel(flags, part_ref, near_ref, far_ref, out_ref, yn_ref, yf_ref):
-    wide, halo = part_ref.shape[0], near_ref.shape[0]
+    strip, rows = near_ref.shape[0], out_ref.shape[0]
+    skip = (part_ref.shape[0] - rows) // 2
     even = flags[0] == 0
     near, far = near_ref[...], far_ref[...]
-    out_ref[0:halo] = part_ref[0:halo] + jnp.where(even, far, near)
-    out_ref[halo : wide - halo] = part_ref[halo : wide - halo]
-    out_ref[wide - halo : wide] = part_ref[wide - halo : wide] + jnp.where(even, near, far)
+    out_ref[0:strip] = part_ref[skip : skip + strip] + jnp.where(even, far, near)
+    out_ref[strip : rows - strip] = part_ref[skip + strip : skip + rows - strip]
+    out_ref[rows - strip :] = part_ref[skip + rows - strip : skip + rows] + jnp.where(even, near, far)
     yn_ref[...], yf_ref[...] = edges(flags[1], out_ref[:, 0:8, :], out_ref[:, 16:24, :])
 
 
-def final_kernel(views, lo_x, lo_y, flags, est_ref, total_ref, yn_ref, yf_ref, out_ref, new):
-    updated(views, flags, est_ref, total_ref, yn_ref, yf_ref, new)
-    out_ref[...] = new[lo_x : lo_x + ROWS, lo_y : lo_y + WIDTH, :]
+def final_kernel(views, lo_x, lo_y, flags, est_ref, total_ref, yn_ref, yf_ref, out_ref, total):
+    low, high = sides(flags, yn_ref, yf_ref)
+    total[:, 0:8, :] = total_ref[:, 0:8, :] + low
+    total[:, 8:16, :] = total_ref[:, 8:16, :]
+    total[:, 16:24, :] = total_ref[:, 16:24, :] + high
+    own = pl.ds(lo_y, WIDTH)
+    out_ref[...] = est_ref[pl.ds(lo_x, ROWS), own, :] * (total[:, own, :] / views)
 
 
 def pairs(count, start):
@@ -305,42 +314,44 @@
     data = lax.all_to_all(data, "view", 0, 0, tiled=True)
     matrices = jax.ShapeDtypeStruct((views, lanes, 2 * lanes), jnp.bfloat16)
 
-    block, strip, side = (wide, COLS, lanes), (halo, COLS, lanes), (wide, 8, lanes)
+    block = (wide, COLS, lanes)
+    strips = [(halo, COLS, lanes)] * (ITERS - 1) + [(halo // 2, COLS, lanes)]
     scratch = [
         pltpu.VMEM((views, wide, cols, lanes), jnp.float32),
         pltpu.VMEM((views, rows * cols, lanes), jnp.float32),
     ]
 
-    def joined(part, near, far):
-        total, yn, yf = call(rows_kernel, (flags, part, near, far), (block, side, side))
+    def joined(part, near, far, count):
+        shapes = [(count, width, lanes) for width in (COLS, 8, 8)]
+        total, yn, yf = call(rows_kernel, (flags, part, near, far), shapes)
         yn, yf = swapped(yn, yf, "view")
         return total, yn, yf
 
-    total, yn, yf = joined(own, near, far)
+    total, yn, yf = joined(own, near, far, wide)
     current, part, near, far, conv, corr, table = call(
         functools.partial(first_kernel, sizes),
         (flags, total, yn, yf, data),
-        (block, block, strip, strip, matrices, matrices, (views, 16, lanes)),
+        (block, block, strips[0], strips[0], matrices, matrices, (views, 16, lanes)),
         scratch + [pltpu.VMEM((2 * views, lanes), jnp.float32)],
         limit=16 << 20,
     )
-    for _ in range(1, ITERS):
+    for step in range(1, ITERS):
         near, far = swapped(near, far, "tile")
-        total, yn, yf = joined(part, near, far)
+        total, yn, yf = joined(part, near, far, wide)
         current, part, near, far = call(
             functools.partial(pass_kernel, sizes, views),
             (flags, current, total, yn, yf, data, conv, corr, table),
-            (block, block, strip, strip),
+            (block, block, strips[step], strips[step]),
             scratch,
             limit=12 << 20,
         )
     near, far = swapped(near, far, "tile")
-    total, yn, yf = joined(part, near, far)
+    total, yn, yf = joined(part, near, far, rows)
     (out,) = call(
         functools.partial(final_kernel, views, nf // 2, ns // 2),
         (flags, current, total, yn, yf),
         ((rows, cols, lanes),),
-        [pltpu.VMEM(block, jnp.float32)],
+        [pltpu.VMEM((rows, COLS, lanes), jnp.float32)],
     )
     return out
 

time: 116 us -> 116 us (level)
  no operation moved by 1% of the time
where the time goes in v5:
time: 116 us; the launch traced here: 115 us
  waiting for transfers between devices  50.6 us (44%)
  starting transfers between devices  47.1 us (41%)
  Pallas kernels  17 us (15%)
    ppermute x6, waiting for transfers between devices, swapped(): far = lax.ppermute(far, axis, pairs(count, 1))  45.9 us
    ppermute x6, starting transfers between devices, swapped(): far = lax.ppermute(far, axis, pairs(count, 1))  25.3 us
    pallas_call x6, Pallas kernels, call(): pl.pallas_call(kernel, in_specs=[SMEM] + [VMEM] * (len(ins) - 1), out_spe...  14.8 us
    ppermute x6, starting transfers between devices, swapped(): near = lax.ppermute(near, axis, pairs(count, 0))  13 us
    all_to_all x1, starting transfers between devices, local(): data = lax.all_to_all(data, 'view', 0, 0, tiled=True)  8.8 us
    ppermute x6, waiting for transfers between devices, swapped(): near = lax.ppermute(near, axis, pairs(count, 0))  4.69 us
  transfers between devices with their start and end apart: 13, of which 9 were waited for; matrix products, arithmetic and copies ran while one was open for 0% of the time, Pallas kernels for 0%

profile of v5, /device:TPU:38, one launch (start us, length us, event | category | flops | bytes accessed | tf_op | source)
XLA Modules:
  0.0 115.1 jit_solution(986057709301194521)
XLA Ops:
  0.0 2.3 %shard_map.56 = f32[16,136,128]{2,1,0:T(8,128)} custom-call(f32[8,16,16,128]{3,2,1,0:T(8,128)} %bitcast.3, f32[1,33]{1,0:T(1,128)} %axial_ref.1, f32[1,5]{1,0:T(1,128)} %first_ref.1, f32[1,7]{1,0:T(1,128)} %second_ref.1), custom_call_target="tpu_custom_call" | custom-call | tf_op jit(solution)/shard_map/pallas_call | solution.py:299
  2.3 8.8 %all-to-all-start = ((f32[16,136,128]{2,1,0:T(8,128)}), f32[16,136,128]{2,1,0:T(8,128)S(1)}, u32[]{:S(2)}, u32[]{:S(2)}) async-start(f32[16,136,128]{2,1,0:T(8,128)} %shard_map.56), calls=%async_computation | async-start | bytes 2228224 | tf_op jit(solution)/shard_map/all_to_all | solution.py:314
  11.1 9.2 %collective-permute-start.1 = (f32[4,24,128]{2,1,0:T(8,128)S(1)}, f32[4,24,128]{2,1,0:T(8,128)S(1)}, u32[]{:S(2)}, u32[]{:S(2)}) collective-permute-start(f32[4,24,128]{2,1,0:T(8,128)S(1)} %get-tuple-element.45), channel_id=1, source_target_pairs={{1,2},{2,1},{3,4},{4,3},{5,6},{6,5},{7,8},{8,7},{9,10},{10,9},{11,... | collective-permute-start | bytes 147464 | tf_op jit(solution)/shard_map/ppermute | solution.py:261
  20.3 1.9 %collective-permute-start = (f32[4,24,128]{2,1,0:T(8,128)S(1)}, f32[4,24,128]{2,1,0:T(8,128)S(1)}, u32[]{:S(2)}, u32[]{:S(2)}) collective-permute-start(f32[4,24,128]{2,1,0:T(8,128)S(1)} %get-tuple-element.46), channel_id=1, source_target_pairs={{0,1},{1,0},{2,3},{3,2},{4,5},{5,4},{6,7},{7,6},{8,9},{9,8},{10,11... | collective-permute-start | bytes 147464 | tf_op jit(solution)/shard_map/ppermute | solution.py:262
  22.3 22.6 %collective-permute-done.1.far_ref = f32[4,24,128]{2,1,0:T(8,128)S(1)} collective-permute-done((f32[4,24,128]{2,1,0:T(8,128)S(1)}, f32[4,24,128]{2,1,0:T(8,128)S(1)}, u32[]{:S(2)}, u32[]{:S(2)}) %collective-permute-start.1) | collective-permute-done | bytes 49184 | tf_op jit(solution)/shard_map/ppermute | solution.py:261
  45.5 3.4 %collective-permute-start.2 = (f32[12,8,128]{2,1,0:T(8,128)S(1)}, f32[12,8,128]{2,1,0:T(8,128)S(1)}, u32[]{:S(2)}, u32[]{:S(2)}) collective-permute-start(f32[12,8,128]{2,1,0:T(8,128)S(1)} %get-tuple-element.26), channel_id=1, source_target_pairs={{0,32},{32,0},{64,96},{96,64},{128,160},{160,128},{192,224},{224,1... | collective-permute-start | bytes 147464 | tf_op jit(solution)/shard_map/ppermute | solution.py:262
  48.8 1.9 %collective-permute-start.3 = (f32[12,8,128]{2,1,0:T(8,128)S(1)}, f32[12,8,128]{2,1,0:T(8,128)S(1)}, u32[]{:S(2)}, u32[]{:S(2)}) collective-permute-start(f32[12,8,128]{2,1,0:T(8,128)S(1)} %get-tuple-element.27), channel_id=1, source_target_pairs={{32,64},{64,32},{96,128},{128,96},{160,192},{192,160},{224,256},{2... | collective-permute-start | bytes 147464 | tf_op jit(solution)/shard_map/ppermute | solution.py:261
  51.5 5.5 %collective-permute-done.3.yf_ref = f32[12,8,128]{2,1,0:T(8,128)S(1)} collective-permute-done((f32[12,8,128]{2,1,0:T(8,128)S(1)}, f32[12,8,128]{2,1,0:T(8,128)S(1)}, u32[]{:S(2)}, u32[]{:S(2)}) %collective-permute-start.3) | collective-permute-done | bytes 49184 | tf_op jit(solution)/shard_map/ppermute | solution.py:261
  56.9 6.9 %shard_map.57 = (f32[12,24,128]{2,1,0:T(8,128)S(1)}, f32[12,24,128]{2,1,0:T(8,128)S(1)}, f32[4,24,128]{2,1,0:T(8,128)S(1)}, f32[4,24,128]{2,1,0:T(8,128)S(1)}, b...) custom-call(s32[2]{0:T(128)S(1)} %pad_add_fusion.flags, ...), custom_call_target="tpu_custom_call" | custom-call | tf_op jit(solution)/shard_map/pallas_call | solution.py:272
  63.9 1.9 %collective-permute-start.4 = (f32[4,24,128]{2,1,0:T(8,128)S(1)}, f32[4,24,128]{2,1,0:T(8,128)S(1)}, u32[]{:S(2)}, u32[]{:S(2)}) collective-permute-start(f32[4,24,128]{2,1,0:T(8,128)S(1)} %get-tuple-element.30), channel_id=1, source_target_pairs={{0,1},{1,0},{2,3},{3,2},{4,5},{5,4},{6,7},{7,6},{8,9},{9,8},{10,11... | collective-permute-start | bytes 147464 | tf_op jit(solution)/shard_map/ppermute | solution.py:262
  65.8 5.6 %collective-permute-start.5 = (f32[4,24,128]{2,1,0:T(8,128)S(1)}, f32[4,24,128]{2,1,0:T(8,128)S(1)}, u32[]{:S(2)}, u32[]{:S(2)}) collective-permute-start(f32[4,24,128]{2,1,0:T(8,128)S(1)} %get-tuple-element.31), channel_id=1, source_target_pairs={{1,2},{2,1},{3,4},{4,3},{5,6},{6,5},{7,8},{8,7},{9,10},{10,9},{11,... | collective-permute-start | bytes 147464 | tf_op jit(solution)/shard_map/ppermute | solution.py:261
  71.4 4.6 %collective-permute-done.5.far_ref = f32[4,24,128]{2,1,0:T(8,128)S(1)} collective-permute-done((f32[4,24,128]{2,1,0:T(8,128)S(1)}, f32[4,24,128]{2,1,0:T(8,128)S(1)}, u32[]{:S(2)}, u32[]{:S(2)}) %collective-permute-start.5) | collective-permute-done | bytes 49184 | tf_op jit(solution)/shard_map/ppermute | solution.py:261
  76.6 1.9 %collective-permute-start.6 = (f32[12,8,128]{2,1,0:T(8,128)S(1)}, f32[12,8,128]{2,1,0:T(8,128)S(1)}, u32[]{:S(2)}, u32[]{:S(2)}) collective-permute-start(f32[12,8,128]{2,1,0:T(8,128)S(1)} %get-tuple-element.33), channel_id=1, source_target_pairs={{0,32},{32,0},{64,96},{96,64},{128,160},{160,128},{192,224},{224,1... | collective-permute-start | bytes 147464 | tf_op jit(solution)/shard_map/ppermute | solution.py:262
  78.5 2.0 %collective-permute-start.7 = (f32[12,8,128]{2,1,0:T(8,128)S(1)}, f32[12,8,128]{2,1,0:T(8,128)S(1)}, u32[]{:S(2)}, u32[]{:S(2)}) collective-permute-start(f32[12,8,128]{2,1,0:T(8,128)S(1)} %get-tuple-element.34), channel_id=1, source_target_pairs={{32,64},{64,32},{96,128},{128,96},{160,192},{192,160},{224,256},{2... | collective-permute-start | bytes 147464 | tf_op jit(solution)/shard_map/ppermute | solution.py:261
  80.5 2.1 %collective-permute-done.6.yn_ref = f32[12,8,128]{2,1,0:T(8,128)S(1)} collective-permute-done((f32[12,8,128]{2,1,0:T(8,128)S(1)}, f32[12,8,128]{2,1,0:T(8,128)S(1)}, u32[]{:S(2)}, u32[]{:S(2)}) %collective-permute-start.6) | collective-permute-done | bytes 49184 | tf_op jit(solution)/shard_map/ppermute | solution.py:262
  82.6 4.0 %collective-permute-done.7.yf_ref = f32[12,8,128]{2,1,0:T(8,128)S(1)} collective-permute-done((f32[12,8,128]{2,1,0:T(8,128)S(1)}, f32[12,8,128]{2,1,0:T(8,128)S(1)}, u32[]{:S(2)}, u32[]{:S(2)}) %collective-permute-start.7) | collective-permute-done | bytes 49184 | tf_op jit(solution)/shard_map/ppermute | solution.py:261
  86.6 5.0 %shard_map.59 = (f32[12,24,128]{2,1,0:T(8,128)S(1)}, f32[12,24,128]{2,1,0:T(8,128)S(1)}, f32[2,24,128]{2,1,0:T(8,128)S(1)}, f32[2,24,128]{2,1,0:T(8,128)S(1)}) custom-call(s32[2]{0:T(128)S(1)} %pad_add_fusion.flags, f32[12,24,128]{2,1,0:T(8,128)S(1)} %get-tuple-element.28.est_ref, f32[12,24,128]{2,1,0:T(8,128)S(1)} %get-tuple-element.32.total_ref, ...), custom_call_target="tpu_custom_call" | custom-call | tf_op jit(solution)/shard_map/pallas_call | solution.py:272
  91.6 1.9 %collective-permute-start.8 = (f32[2,24,128]{2,1,0:T(8,128)S(1)}, f32[2,24,128]{2,1,0:T(8,128)S(1)}, u32[]{:S(2)}, u32[]{:S(2)}) collective-permute-start(f32[2,24,128]{2,1,0:T(8,128)S(1)} %get-tuple-element.40), channel_id=1, source_target_pairs={{0,1},{1,0},{2,3},{3,2},{4,5},{5,4},{6,7},{7,6},{8,9},{9,8},{10,11... | collective-permute-start | bytes 73736 | tf_op jit(solution)/shard_map/ppermute | solution.py:262
  93.5 4.8 %collective-permute-start.9 = (f32[2,24,128]{2,1,0:T(8,128)S(1)}, f32[2,24,128]{2,1,0:T(8,128)S(1)}, u32[]{:S(2)}, u32[]{:S(2)}) collective-permute-start(f32[2,24,128]{2,1,0:T(8,128)S(1)} %get-tuple-element.41), channel_id=1, source_target_pairs={{1,2},{2,1},{3,4},{4,3},{5,6},{6,5},{7,8},{8,7},{9,10},{10,9},{11,... | collective-permute-start | bytes 73736 | tf_op jit(solution)/shard_map/ppermute | solution.py:261
  98.3 5.2 %collective-permute-done.9.far_ref = f32[2,24,128]{2,1,0:T(8,128)S(1)} collective-permute-done((f32[2,24,128]{2,1,0:T(8,128)S(1)}, f32[2,24,128]{2,1,0:T(8,128)S(1)}, u32[]{:S(2)}, u32[]{:S(2)}) %collective-permute-start.9) | collective-permute-done | bytes 24608 | tf_op jit(solution)/shard_map/ppermute | solution.py:261
  104.0 1.9 %collective-permute-start.10 = (f32[8,8,128]{2,1,0:T(8,128)S(1)}, f32[8,8,128]{2,1,0:T(8,128)S(1)}, u32[]{:S(2)}, u32[]{:S(2)}) collective-permute-start(f32[8,8,128]{2,1,0:T(8,128)S(1)} %get-tuple-element.43), channel_id=1, source_target_pairs={{0,32},{32,0},{64,96},{96,64},{128,160},{160,128},{192,224},{224,1... | collective-permute-start | bytes 98312 | tf_op jit(solution)/shard_map/ppermute | solution.py:262
  106.0 2.0 %collective-permute-start.11 = (f32[8,8,128]{2,1,0:T(8,128)S(1)}, f32[8,8,128]{2,1,0:T(8,128)S(1)}, u32[]{:S(2)}, u32[]{:S(2)}) collective-permute-start(f32[8,8,128]{2,1,0:T(8,128)S(1)} %get-tuple-element.44), channel_id=1, source_target_pairs={{32,64},{64,32},{96,128},{128,96},{160,192},{192,160},{224,256},{2... | collective-permute-start | bytes 98312 | tf_op jit(solution)/shard_map/ppermute | solution.py:261
  107.9 1.9 %collective-permute-done.10.yn_ref = f32[8,8,128]{2,1,0:T(8,128)S(1)} collective-permute-done((f32[8,8,128]{2,1,0:T(8,128)S(1)}, f32[8,8,128]{2,1,0:T(8,128)S(1)}, u32[]{:S(2)}, u32[]{:S(2)}) %collective-permute-start.10) | collective-permute-done | bytes 32800 | tf_op jit(solution)/shard_map/ppermute | solution.py:262
  109.8 4.0 %collective-permute-done.11.yf_ref = f32[8,8,128]{2,1,0:T(8,128)S(1)} collective-permute-done((f32[8,8,128]{2,1,0:T(8,128)S(1)}, f32[8,8,128]{2,1,0:T(8,128)S(1)}, u32[]{:S(2)}, u32[]{:S(2)}) %collective-permute-start.11) | collective-permute-done | bytes 32800 | tf_op jit(solution)/shard_map/ppermute | solution.py:261
  (14 shorter events, 3.7 us)
Async XLA Ops:
  2.3 8.8 %copy-start = (f32[8,16,128]{2,1,0:T(8,128)S(1)}, f32[8,16,128]{2,1,0:T(8,128)}, u32[]{:S(2)}) copy-start(f32[8,16,128]{2,1,0:T(8,128)} %param.5) | copy-start | bytes 196612
  2.3 54.7 %all-to-all-start = ((f32[16,136,128]{2,1,0:T(8,128)}), f32[16,136,128]{2,1,0:T(8,128)S(1)}, u32[]{:S(2)}, u32[]{:S(2)}) async-start(f32[16,136,128]{2,1,0:T(8,128)} %shard_map.56), calls=%async_computation | async-start | bytes 2228224 | tf_op jit(solution)/shard_map/all_to_all | solution.py:314
  11.1 33.8 %collective-permute-start.1 = (f32[4,24,128]{2,1,0:T(8,128)S(1)}, f32[4,24,128]{2,1,0:T(8,128)S(1)}, u32[]{:S(2)}, u32[]{:S(2)}) collective-permute-start(f32[4,24,128]{2,1,0:T(8,128)S(1)} %get-tuple-element.45), channel_id=1, source_target_pairs={{1,2},{2,1},{3,4},{4,3},{5,6},{6,5},{7,8},{8,7},{9,10},{10,9},{11,... | collective-permute-start | bytes 147464 | tf_op jit(solution)/shard_map/ppermute | solution.py:261
  20.3 24.6 %collective-permute-start = (f32[4,24,128]{2,1,0:T(8,128)S(1)}, f32[4,24,128]{2,1,0:T(8,128)S(1)}, u32[]{:S(2)}, u32[]{:S(2)}) collective-permute-start(f32[4,24,128]{2,1,0:T(8,128)S(1)} %get-tuple-element.46), channel_id=1, source_target_pairs={{0,1},{1,0},{2,3},{3,2},{4,5},{5,4},{6,7},{7,6},{8,9},{9,8},{10,11... | collective-permute-start | bytes 147464 | tf_op jit(solution)/shard_map/ppermute | solution.py:262
  45.5 6.0 %collective-permute-start.2 = (f32[12,8,128]{2,1,0:T(8,128)S(1)}, f32[12,8,128]{2,1,0:T(8,128)S(1)}, u32[]{:S(2)}, u32[]{:S(2)}) collective-permute-start(f32[12,8,128]{2,1,0:T(8,128)S(1)} %get-tuple-element.26), channel_id=1, source_target_pairs={{0,32},{32,0},{64,96},{96,64},{128,160},{160,128},{192,224},{224,1... | collective-permute-start | bytes 147464 | tf_op jit(solution)/shard_map/ppermute | solution.py:262
  48.8 8.1 %collective-permute-start.3 = (f32[12,8,128]{2,1,0:T(8,128)S(1)}, f32[12,8,128]{2,1,0:T(8,128)S(1)}, u32[]{:S(2)}, u32[]{:S(2)}) collective-permute-start(f32[12,8,128]{2,1,0:T(8,128)S(1)} %get-tuple-element.27), channel_id=1, source_target_pairs={{32,64},{64,32},{96,128},{128,96},{160,192},{192,160},{224,256},{2... | collective-permute-start | bytes 147464 | tf_op jit(solution)/shard_map/ppermute | solution.py:261
  63.9 7.5 %collective-permute-start.4 = (f32[4,24,128]{2,1,0:T(8,128)S(1)}, f32[4,24,128]{2,1,0:T(8,128)S(1)}, u32[]{:S(2)}, u32[]{:S(2)}) collective-permute-start(f32[4,24,128]{2,1,0:T(8,128)S(1)} %get-tuple-element.30), channel_id=1, source_target_pairs={{0,1},{1,0},{2,3},{3,2},{4,5},{5,4},{6,7},{7,6},{8,9},{9,8},{10,11... | collective-permute-start | bytes 147464 | tf_op jit(solution)/shard_map/ppermute | solution.py:262
  65.8 10.2 %collective-permute-start.5 = (f32[4,24,128]{2,1,0:T(8,128)S(1)}, f32[4,24,128]{2,1,0:T(8,128)S(1)}, u32[]{:S(2)}, u32[]{:S(2)}) collective-permute-start(f32[4,24,128]{2,1,0:T(8,128)S(1)} %get-tuple-element.31), channel_id=1, source_target_pairs={{1,2},{2,1},{3,4},{4,3},{5,6},{6,5},{7,8},{8,7},{9,10},{10,9},{11,... | collective-permute-start | bytes 147464 | tf_op jit(solution)/shard_map/ppermute | solution.py:261
  76.6 6.0 %collective-permute-start.6 = (f32[12,8,128]{2,1,0:T(8,128)S(1)}, f32[12,8,128]{2,1,0:T(8,128)S(1)}, u32[]{:S(2)}, u32[]{:S(2)}) collective-permute-start(f32[12,8,128]{2,1,0:T(8,128)S(1)} %get-tuple-element.33), channel_id=1, source_target_pairs={{0,32},{32,0},{64,96},{96,64},{128,160},{160,128},{192,224},{224,1... | collective-permute-start | bytes 147464 | tf_op jit(solution)/shard_map/ppermute | solution.py:262
  78.5 8.1 %collective-permute-start.7 = (f32[12,8,128]{2,1,0:T(8,128)S(1)}, f32[12,8,128]{2,1,0:T(8,128)S(1)}, u32[]{:S(2)}, u32[]{:S(2)}) collective-permute-start(f32[12,8,128]{2,1,0:T(8,128)S(1)} %get-tuple-element.34), channel_id=1, source_target_pairs={{32,64},{64,32},{96,128},{128,96},{160,192},{192,160},{224,256},{2... | collective-permute-start | bytes 147464 | tf_op jit(solution)/shard_map/ppermute | solution.py:261
  91.6 6.7 %collective-permute-start.8 = (f32[2,24,128]{2,1,0:T(8,128)S(1)}, f32[2,24,128]{2,1,0:T(8,128)S(1)}, u32[]{:S(2)}, u32[]{:S(2)}) collective-permute-start(f32[2,24,128]{2,1,0:T(8,128)S(1)} %get-tuple-element.40), channel_id=1, source_target_pairs={{0,1},{1,0},{2,3},{3,2},{4,5},{5,4},{6,7},{7,6},{8,9},{9,8},{10,11... | collective-permute-start | bytes 73736 | tf_op jit(solution)/shard_map/ppermute | solution.py:262
  93.5 10.0 %collective-permute-start.9 = (f32[2,24,128]{2,1,0:T(8,128)S(1)}, f32[2,24,128]{2,1,0:T(8,128)S(1)}, u32[]{:S(2)}, u32[]{:S(2)}) collective-permute-start(f32[2,24,128]{2,1,0:T(8,128)S(1)} %get-tuple-element.41), channel_id=1, source_target_pairs={{1,2},{2,1},{3,4},{4,3},{5,6},{6,5},{7,8},{8,7},{9,10},{10,9},{11,... | collective-permute-start | bytes 73736 | tf_op jit(solution)/shard_map/ppermute | solution.py:261
  104.0 5.8 %collective-permute-start.10 = (f32[8,8,128]{2,1,0:T(8,128)S(1)}, f32[8,8,128]{2,1,0:T(8,128)S(1)}, u32[]{:S(2)}, u32[]{:S(2)}) collective-permute-start(f32[8,8,128]{2,1,0:T(8,128)S(1)} %get-tuple-element.43), channel_id=1, source_target_pairs={{0,32},{32,0},{64,96},{96,64},{128,160},{160,128},{192,224},{224,1... | collective-permute-start | bytes 98312 | tf_op jit(solution)/shard_map/ppermute | solution.py:262
  106.0 7.9 %collective-permute-start.11 = (f32[8,8,128]{2,1,0:T(8,128)S(1)}, f32[8,8,128]{2,1,0:T(8,128)S(1)}, u32[]{:S(2)}, u32[]{:S(2)}) collective-permute-start(f32[8,8,128]{2,1,0:T(8,128)S(1)} %get-tuple-element.44), channel_id=1, source_target_pairs={{32,64},{64,32},{96,128},{128,96},{160,192},{192,160},{224,256},{2... | collective-permute-start | bytes 98312 | tf_op jit(solution)/shard_map/ppermute | solution.py:261

commit v6 on v5

--- a/solution.py
+++ b/solution.py
@@ -24,6 +24,18 @@
     left = jnp.concatenate(split(x), axis=1)
     right = jnp.concatenate([matrix, matrix], axis=0)
     both = jnp.dot(left, right, preferred_element_type=jnp.float32)
+    return both[:, 0:LANES] + both[:, LANES:]
+
+
+def product_t(x, matrix):
+    left = jnp.concatenate(split(x), axis=1)
+    high, low = matrix[:, 0:LANES], matrix[:, LANES:]
+    right = jnp.concatenate(
+        [jnp.concatenate([high, high], axis=1), jnp.concatenate([low, low], axis=1)], axis=0
+    )
+    both = lax.dot_general(
+        left, right, (((1,), (1,)), ((), ())), preferred_element_type=jnp.float32
+    )
     return both[:, 0:LANES] + both[:, LANES:]
 
 
@@ -80,23 +92,12 @@
         copy.wait()
 
 
-def make_tables(sizes, data_ref, conv_ref, corr_ref, table_ref, axial):
-    _, _, nz = sizes
+def make_tables(data_ref, table_ref):
     views = data_ref.shape[0]
     lane = lax.broadcasted_iota(jnp.int32, (8, LANES), 1)
     sub = lax.broadcasted_iota(jnp.int32, (8, LANES), 0)
-    for v in range(views):
-        axial[v : v + 1, :] = data_ref[v, BLOCK : BLOCK + 1, :]
-    z = lax.broadcasted_iota(jnp.int32, (LANES, LANES), 0)
-    zz = lax.broadcasted_iota(jnp.int32, (LANES, LANES), 1)
-    reverse = jnp.where(z + zz == nz - 1, 1.0, 0.0).astype(jnp.float32)
-    axial[views:, :] = jnp.dot(
-        axial[0:views, :], reverse, precision=lax.Precision.HIGHEST, preferred_element_type=jnp.float32
-    )
 
     def one(v, carry):
-        for at, ref in ((0, conv_ref), (views, corr_ref)):
-            banded(axial[pl.ds(at + v, 1), :], nz // 2, ref.at[v])
         start = 0
         for row in (1, 2):
             taps = jnp.broadcast_to(data_ref[v, BLOCK + row : BLOCK + row + 1, :], (8, LANES))
@@ -112,7 +113,7 @@
     return jnp.broadcast_to(table_ref[v, pl.ds(k, 1), :], (8, LANES))
 
 
-def conv_part(sizes, est_ref, conv_ref, table_ref, spread, finish):
+def conv_part(sizes, est_ref, conv_ref, table_ref, spread, prepare, finish):
     nf, ns, _ = sizes
     wide, views = est_ref.shape[0], conv_ref.shape[0]
 
@@ -132,6 +133,7 @@
     lax.fori_loop(0, wide, row, 0)
 
     def one(v, carry):
+        prepare(v)
         first = [tap(table_ref, v, k) for k in range(nf)]
         out = []
         for i in range(ROWS):
@@ -146,13 +148,13 @@
     lax.fori_loop(0, views, one, 0, unroll=2)
 
 
-def corr_part(sizes, flags, ratio_of, corr_ref, table_ref, spread, part_ref, near_ref, far_ref):
+def corr_part(sizes, flags, ratio_of, conv_ref, table_ref, spread, part_ref, near_ref, far_ref):
     nf, ns, _ = sizes
     wide, views = spread.shape[1], spread.shape[0]
 
     def one(v, carry):
         first = [tap(table_ref, v, k) for k in range(nf)]
-        back = product(ratio_of(v), corr_ref[v])
+        back = product_t(ratio_of(v), conv_ref[v])
         for i in range(wide):
             for h in range(2):
                 t = None
@@ -191,42 +193,57 @@
     )
 
 
-def sides(flags, yn_ref, yf_ref):
-    even = flags[1] == 0
-    yn, yf = yn_ref[...], yf_ref[...]
-    return jnp.where(even, yf, yn), jnp.where(even, yn, yf)
-
-
-def both_parts(sizes, flags, est_ref, data_ref, conv_ref, corr_ref, table_ref, part_ref, near_ref, far_ref, spread, ratio):
+def sides(flag, near_ref, far_ref):
+    even = flag == 0
+    near, far = near_ref[...], far_ref[...]
+    return jnp.where(even, far, near), jnp.where(even, near, far)
+
+
+def both_parts(sizes, flags, est_ref, data_ref, conv_ref, table_ref, part_ref, near_ref, far_ref, spread, ratio, prepare=lambda v: None):
     def finish(v, blurred):
         ratio[v] = data_ref[v, 0:BLOCK, :] / blurred
 
-    conv_part(sizes, est_ref, conv_ref, table_ref, spread, finish)
+    conv_part(sizes, est_ref, conv_ref, table_ref, spread, prepare, finish)
     corr_part(
         sizes, flags, lambda v: ratio[v],
-        corr_ref, table_ref, spread, part_ref, near_ref, far_ref,
-    )
-
-
-def first_kernel(sizes, flags, total_ref, yn_ref, yf_ref, data_ref, est_ref, part_ref, near_ref, far_ref, conv_ref, corr_ref, table_ref, spread, ratio, axial):
-    make_tables(sizes, data_ref, conv_ref, corr_ref, table_ref, axial)
-    low, high = sides(flags, yn_ref, yf_ref)
-    est_ref[:, 0:8, :] = total_ref[:, 0:8, :] + low
-    est_ref[:, 8:16, :] = total_ref[:, 8:16, :]
-    est_ref[:, 16:24, :] = total_ref[:, 16:24, :] + high
-    both_parts(sizes, flags, est_ref, data_ref, conv_ref, corr_ref, table_ref, part_ref, near_ref, far_ref, spread, ratio)
+        conv_ref, table_ref, spread, part_ref, near_ref, far_ref,
+    )
+
+
+def columns_kernel(halo, flags, own_ref, yn_ref, yf_ref, out_ref, near_ref, far_ref):
+    low, high = sides(flags[1], yn_ref, yf_ref)
+    out_ref[:, 0:halo, :] = low[:, 8 - halo :, :]
+    out_ref[:, halo : halo + WIDTH, :] = own_ref[...]
+    out_ref[:, halo + WIDTH : WIDTH + 2 * halo, :] = high[:, 0:halo, :]
+    out_ref[:, WIDTH + 2 * halo :, :] = jnp.zeros((ROWS, COLS - WIDTH - 2 * halo, LANES), jnp.float32)
+    strip = near_ref.shape[0]
+    near_ref[...], far_ref[...] = edges(flags[0], out_ref[0:strip], out_ref[ROWS - strip :])
+
+
+def first_kernel(sizes, flags, own_ref, xn_ref, xf_ref, data_ref, est_ref, part_ref, near_ref, far_ref, conv_ref, table_ref, spread, ratio):
+    make_tables(data_ref, table_ref)
+    low, high = sides(flags[0], xn_ref, xf_ref)
+    strip = low.shape[0]
+    est_ref[0:strip] = low
+    est_ref[strip : strip + ROWS] = own_ref[...]
+    est_ref[strip + ROWS :] = high
+
+    def prepare(v):
+        banded(data_ref[v, BLOCK : BLOCK + 1, :], sizes[2] // 2, conv_ref.at[v])
+
+    both_parts(sizes, flags, est_ref, data_ref, conv_ref, table_ref, part_ref, near_ref, far_ref, spread, ratio, prepare)
 
 
 def updated(views, flags, est_ref, total_ref, yn_ref, yf_ref, new_ref):
-    low, high = sides(flags, yn_ref, yf_ref)
+    low, high = sides(flags[1], yn_ref, yf_ref)
     new_ref[:, 0:8, :] = est_ref[:, 0:8, :] * ((total_ref[:, 0:8, :] + low) / views)
     new_ref[:, 8:16, :] = est_ref[:, 8:16, :] * (total_ref[:, 8:16, :] / views)
     new_ref[:, 16:24, :] = est_ref[:, 16:24, :] * ((total_ref[:, 16:24, :] + high) / views)
 
 
-def pass_kernel(sizes, views, flags, est_ref, total_ref, yn_ref, yf_ref, data_ref, conv_ref, corr_ref, table_ref, new_ref, part_ref, near_ref, far_ref, spread, ratio):
+def pass_kernel(sizes, views, flags, est_ref, total_ref, yn_ref, yf_ref, data_ref, conv_ref, table_ref, new_ref, part_ref, near_ref, far_ref, spread, ratio):
     updated(views, flags, est_ref, total_ref, yn_ref, yf_ref, new_ref)
-    both_parts(sizes, flags, new_ref, data_ref, conv_ref, corr_ref, table_ref, part_ref, near_ref, far_ref, spread, ratio)
+    both_parts(sizes, flags, new_ref, data_ref, conv_ref, table_ref, part_ref, near_ref, far_ref, spread, ratio)
 
 
 def rows_kernel(flags, part_ref, near_ref, far_ref, out_ref, yn_ref, yf_ref):
@@ -241,7 +258,7 @@
 
 
 def final_kernel(views, lo_x, lo_y, flags, est_ref, total_ref, yn_ref, yf_ref, out_ref, total):
-    low, high = sides(flags, yn_ref, yf_ref)
+    low, high = sides(flags[1], yn_ref, yf_ref)
     total[:, 0:8, :] = total_ref[:, 0:8, :] + low
     total[:, 8:16, :] = total_ref[:, 8:16, :]
     total[:, 16:24, :] = total_ref[:, 16:24, :] + high
@@ -289,10 +306,6 @@
     flags = jnp.stack(
         [lax.axis_index("tile") % 2, lax.axis_index("view") % 2]
     ).astype(jnp.int32)
-
-    own = jnp.pad(estimate, ((nf // 2, nf // 2), (ns // 2, COLS - cols - ns // 2), (0, 0)))
-    near, far = edges(flags[0], own[0:halo], own[wide - halo :])
-    near, far = swapped(near, far, "tile")
 
     hbm = pl.BlockSpec(memory_space=pltpu.HBM)
     small = (taps_axial, taps_first, taps_second)
@@ -327,12 +340,20 @@
         yn, yf = swapped(yn, yf, "view")
         return total, yn, yf
 
-    total, yn, yf = joined(own, near, far, wide)
-    current, part, near, far, conv, corr, table = call(
+    yn, yf = edges(flags[1], estimate[:, 0:8], estimate[:, cols - 8 :])
+    yn, yf = swapped(yn, yf, "view")
+    thin = (halo // 2, COLS, lanes)
+    own, near, far = call(
+        functools.partial(columns_kernel, ns // 2),
+        (flags, estimate, yn, yf),
+        ((rows, COLS, lanes), thin, thin),
+    )
+    near, far = swapped(near, far, "tile")
+    current, part, near, far, matrix, table = call(
         functools.partial(first_kernel, sizes),
-        (flags, total, yn, yf, data),
-        (block, block, strips[0], strips[0], matrices, matrices, (views, 16, lanes)),
-        scratch + [pltpu.VMEM((2 * views, lanes), jnp.float32)],
+        (flags, own, near, far, data),
+        (block, block, strips[0], strips[0], matrices, (views, 16, lanes)),
+        scratch,
         limit=16 << 20,
     )
     for step in range(1, ITERS):
@@ -340,7 +361,7 @@
         total, yn, yf = joined(part, near, far, wide)
         current, part, near, far = call(
             functools.partial(pass_kernel, sizes, views),
-            (flags, current, total, yn, yf, data, conv, corr, table),
+            (flags, current, total, yn, yf, data, matrix, table),
             (block, block, strips[step], strips[step]),
             scratch,
             limit=12 << 20,

time: 116 us -> 113 us (0.974)
  the two profiles are of different devices: /device:TPU:38 before, /device:TPU:70 now
where the time goes in v6:
time: 113 us; the launch traced here: 112 us
  starting transfers between devices  58.4 us (52%)
  waiting for transfers between devices  36.3 us (32%)
  Pallas kernels  17.4 us (15%)
    ppermute x6, starting transfers between devices, swapped(): far = lax.ppermute(far, axis, pairs(count, 1))  38.3 us
    ppermute x6, waiting for transfers between devices, swapped(): far = lax.ppermute(far, axis, pairs(count, 1))  34.1 us
    pallas_call x6, Pallas kernels, call(): pl.pallas_call(kernel, in_specs=[SMEM] + [VMEM] * (len(ins) - 1), out_spe...  15.1 us
    ppermute x6, starting transfers between devices, swapped(): near = lax.ppermute(near, axis, pairs(count, 0))  11.8 us
    all_to_all x1, starting transfers between devices, local(): data = lax.all_to_all(data, 'view', 0, 0, tiled=True)  8.34 us
    pallas_call x1, Pallas kernels, local(): pl.pallas_call(pieces_kernel, in_specs=[hbm] * 4, out_specs=hbm, out_shap...  2.26 us
  transfers between devices with their start and end apart: 13, of which 8 were waited for; matrix products, arithmetic and copies ran while one was open for 0% of the time, Pallas kernels for 1%

profile of v6, /device:TPU:70, one launch (start us, length us, event | category | flops | bytes accessed | tf_op | source)
XLA Modules:
  0.0 112.4 jit_solution(14486171182282905070)
XLA Ops:
  0.0 2.3 %shard_map.56 = f32[16,136,128]{2,1,0:T(8,128)} custom-call(f32[8,16,16,128]{3,2,1,0:T(8,128)} %bitcast.3, f32[1,33]{1,0:T(1,128)} %axial_ref.1, f32[1,5]{1,0:T(1,128)} %first_ref.1, f32[1,7]{1,0:T(1,128)} %second_ref.1), custom_call_target="tpu_custom_call" | custom-call | tf_op jit(solution)/shard_map/pallas_call | solution.py:312
  2.3 8.3 %all-to-all-start = ((f32[16,136,128]{2,1,0:T(8,128)}), f32[16,136,128]{2,1,0:T(8,128)S(1)}, u32[]{:S(2)}, u32[]{:S(2)}) async-start(f32[16,136,128]{2,1,0:T(8,128)} %shard_map.56), calls=%async_computation | async-start | bytes 2228224 | tf_op jit(solution)/shard_map/all_to_all | solution.py:327
  10.7 4.6 %collective-permute-start.1 = (f32[8,8,128]{2,1,0:T(8,128)S(1)}, f32[8,8,128]{2,1,0:T(8,128)S(1)}, u32[]{:S(2)}, u32[]{:S(2)}) collective-permute-start(f32[8,8,128]{2,1,0:T(8,128)S(1)} %get-tuple-element.43), channel_id=1, source_target_pairs={{32,64},{64,32},{96,128},{128,96},{160,192},{192,160},{224,256},{2... | collective-permute-start | bytes 98312 | tf_op jit(solution)/shard_map/ppermute | solution.py:278
  15.2 2.2 %collective-permute-start = (f32[8,8,128]{2,1,0:T(8,128)S(1)}, f32[8,8,128]{2,1,0:T(8,128)S(1)}, u32[]{:S(2)}, u32[]{:S(2)}) collective-permute-start(f32[8,8,128]{2,1,0:T(8,128)S(1)} %get-tuple-element.44), channel_id=1, source_target_pairs={{0,32},{32,0},{64,96},{96,64},{128,160},{160,128},{192,224},{224,1... | collective-permute-start | bytes 98312 | tf_op jit(solution)/shard_map/ppermute | solution.py:279
  17.5 21.1 %collective-permute-done.1.yf_ref = f32[8,8,128]{2,1,0:T(8,128)S(1)} collective-permute-done((f32[8,8,128]{2,1,0:T(8,128)S(1)}, f32[8,8,128]{2,1,0:T(8,128)S(1)}, u32[]{:S(2)}, u32[]{:S(2)}) %collective-permute-start.1) | collective-permute-done | bytes 32800 | tf_op jit(solution)/shard_map/ppermute | solution.py:278
  39.1 1.9 %collective-permute-start.2 = (f32[2,24,128]{2,1,0:T(8,128)S(1)}, f32[2,24,128]{2,1,0:T(8,128)S(1)}, u32[]{:S(2)}, u32[]{:S(2)}) collective-permute-start(f32[2,24,128]{2,1,0:T(8,128)S(1)} %get-tuple-element.25), channel_id=1, source_target_pairs={{0,1},{1,0},{2,3},{3,2},{4,5},{5,4},{6,7},{7,6},{8,9},{9,8},{10,11... | collective-permute-start | bytes 73736 | tf_op jit(solution)/shard_map/ppermute | solution.py:279
  41.0 10.9 %collective-permute-start.3 = (f32[2,24,128]{2,1,0:T(8,128)S(1)}, f32[2,24,128]{2,1,0:T(8,128)S(1)}, u32[]{:S(2)}, u32[]{:S(2)}) collective-permute-start(f32[2,24,128]{2,1,0:T(8,128)S(1)} %get-tuple-element.26), channel_id=1, source_target_pairs={{1,2},{2,1},{3,4},{4,3},{5,6},{6,5},{7,8},{8,7},{9,10},{10,9},{11,... | collective-permute-start | bytes 73736 | tf_op jit(solution)/shard_map/ppermute | solution.py:278
  52.0 1.7 %collective-permute-done.3.xf_ref = f32[2,24,128]{2,1,0:T(8,128)S(1)} collective-permute-done((f32[2,24,128]{2,1,0:T(8,128)S(1)}, f32[2,24,128]{2,1,0:T(8,128)S(1)}, u32[]{:S(2)}, u32[]{:S(2)}) %collective-permute-start.3) | collective-permute-done | bytes 24608 | tf_op jit(solution)/shard_map/ppermute | solution.py:278
  53.7 7.0 %shard_map.57 = (f32[12,24,128]{2,1,0:T(8,128)S(1)}, f32[12,24,128]{2,1,0:T(8,128)S(1)}, f32[4,24,128]{2,1,0:T(8,128)S(1)}, f32[4,24,128]{2,1,0:T(8,128)S(1)}, b...) custom-call(s32[2]{0:T(128)S(1)} %pad_add_fusion.flags, f32[8,24,128]{2,1,0:T(8,128)S(1)} %get-tuple-element.24.own_ref, ...), custom_call_target="tpu_custom_call" | custom-call | tf_op jit(solution)/shard_map/pallas_call | solution.py:289
  60.7 1.9 %collective-permute-start.4 = (f32[4,24,128]{2,1,0:T(8,128)S(1)}, f32[4,24,128]{2,1,0:T(8,128)S(1)}, u32[]{:S(2)}, u32[]{:S(2)}) collective-permute-start(f32[4,24,128]{2,1,0:T(8,128)S(1)} %get-tuple-element.29), channel_id=1, source_target_pairs={{0,1},{1,0},{2,3},{3,2},{4,5},{5,4},{6,7},{7,6},{8,9},{9,8},{10,11... | collective-permute-start | bytes 147464 | tf_op jit(solution)/shard_map/ppermute | solution.py:279
  62.6 8.6 %collective-permute-start.5 = (f32[4,24,128]{2,1,0:T(8,128)S(1)}, f32[4,24,128]{2,1,0:T(8,128)S(1)}, u32[]{:S(2)}, u32[]{:S(2)}) collective-permute-start(f32[4,24,128]{2,1,0:T(8,128)S(1)} %get-tuple-element.30), channel_id=1, source_target_pairs={{1,2},{2,1},{3,4},{4,3},{5,6},{6,5},{7,8},{8,7},{9,10},{10,9},{11,... | collective-permute-start | bytes 147464 | tf_op jit(solution)/shard_map/ppermute | solution.py:278
  71.2 1.7 %collective-permute-done.5.far_ref = f32[4,24,128]{2,1,0:T(8,128)S(1)} collective-permute-done((f32[4,24,128]{2,1,0:T(8,128)S(1)}, f32[4,24,128]{2,1,0:T(8,128)S(1)}, u32[]{:S(2)}, u32[]{:S(2)}) %collective-permute-start.5) | collective-permute-done | bytes 49184 | tf_op jit(solution)/shard_map/ppermute | solution.py:278
  73.6 1.9 %collective-permute-start.6 = (f32[12,8,128]{2,1,0:T(8,128)S(1)}, f32[12,8,128]{2,1,0:T(8,128)S(1)}, u32[]{:S(2)}, u32[]{:S(2)}) collective-permute-start(f32[12,8,128]{2,1,0:T(8,128)S(1)} %get-tuple-element.32), channel_id=1, source_target_pairs={{0,32},{32,0},{64,96},{96,64},{128,160},{160,128},{192,224},{224,1... | collective-permute-start | bytes 147464 | tf_op jit(solution)/shard_map/ppermute | solution.py:279
  75.5 2.9 %collective-permute-start.7 = (f32[12,8,128]{2,1,0:T(8,128)S(1)}, f32[12,8,128]{2,1,0:T(8,128)S(1)}, u32[]{:S(2)}, u32[]{:S(2)}) collective-permute-start(f32[12,8,128]{2,1,0:T(8,128)S(1)} %get-tuple-element.33), channel_id=1, source_target_pairs={{32,64},{64,32},{96,128},{128,96},{160,192},{192,160},{224,256},{2... | collective-permute-start | bytes 147464 | tf_op jit(solution)/shard_map/ppermute | solution.py:278
  78.4 1.2 %collective-permute-done.6.yn_ref = f32[12,8,128]{2,1,0:T(8,128)S(1)} collective-permute-done((f32[12,8,128]{2,1,0:T(8,128)S(1)}, f32[12,8,128]{2,1,0:T(8,128)S(1)}, u32[]{:S(2)}, u32[]{:S(2)}) %collective-permute-start.6) | collective-permute-done | bytes 49184 | tf_op jit(solution)/shard_map/ppermute | solution.py:279
  79.5 4.0 %collective-permute-done.7.yf_ref = f32[12,8,128]{2,1,0:T(8,128)S(1)} collective-permute-done((f32[12,8,128]{2,1,0:T(8,128)S(1)}, f32[12,8,128]{2,1,0:T(8,128)S(1)}, u32[]{:S(2)}, u32[]{:S(2)}) %collective-permute-start.7) | collective-permute-done | bytes 49184 | tf_op jit(solution)/shard_map/ppermute | solution.py:278
  83.6 5.2 %shard_map.59 = (f32[12,24,128]{2,1,0:T(8,128)S(1)}, f32[12,24,128]{2,1,0:T(8,128)S(1)}, f32[2,24,128]{2,1,0:T(8,128)S(1)}, f32[2,24,128]{2,1,0:T(8,128)S(1)}) custom-call(s32[2]{0:T(128)S(1)} %pad_add_fusion.flags, f32[12,24,128]{2,1,0:T(8,128)S(1)} %get-tuple-element.27.est_ref, f32[12,24,128]{2,1,0:T(8,128)S(1)} %get-tuple-element.31.total_ref, ...), custom_call_target="tpu_custom_call" | custom-call | tf_op jit(solution)/shard_map/pallas_call | solution.py:289
  88.8 1.9 %collective-permute-start.8 = (f32[2,24,128]{2,1,0:T(8,128)S(1)}, f32[2,24,128]{2,1,0:T(8,128)S(1)}, u32[]{:S(2)}, u32[]{:S(2)}) collective-permute-start(f32[2,24,128]{2,1,0:T(8,128)S(1)} %get-tuple-element.38), channel_id=1, source_target_pairs={{0,1},{1,0},{2,3},{3,2},{4,5},{5,4},{6,7},{7,6},{8,9},{9,8},{10,11... | collective-permute-start | bytes 73736 | tf_op jit(solution)/shard_map/ppermute | solution.py:279
  90.8 8.5 %collective-permute-start.9 = (f32[2,24,128]{2,1,0:T(8,128)S(1)}, f32[2,24,128]{2,1,0:T(8,128)S(1)}, u32[]{:S(2)}, u32[]{:S(2)}) collective-permute-start(f32[2,24,128]{2,1,0:T(8,128)S(1)} %get-tuple-element.39), channel_id=1, source_target_pairs={{1,2},{2,1},{3,4},{4,3},{5,6},{6,5},{7,8},{8,7},{9,10},{10,9},{11,... | collective-permute-start | bytes 73736 | tf_op jit(solution)/shard_map/ppermute | solution.py:278
  99.3 1.5 %collective-permute-done.9.far_ref = f32[2,24,128]{2,1,0:T(8,128)S(1)} collective-permute-done((f32[2,24,128]{2,1,0:T(8,128)S(1)}, f32[2,24,128]{2,1,0:T(8,128)S(1)}, u32[]{:S(2)}, u32[]{:S(2)}) %collective-permute-start.9) | collective-permute-done | bytes 24608 | tf_op jit(solution)/shard_map/ppermute | solution.py:278
  101.3 1.9 %collective-permute-start.10 = (f32[8,8,128]{2,1,0:T(8,128)S(1)}, f32[8,8,128]{2,1,0:T(8,128)S(1)}, u32[]{:S(2)}, u32[]{:S(2)}) collective-permute-start(f32[8,8,128]{2,1,0:T(8,128)S(1)} %get-tuple-element.41), channel_id=1, source_target_pairs={{0,32},{32,0},{64,96},{96,64},{128,160},{160,128},{192,224},{224,1... | collective-permute-start | bytes 98312 | tf_op jit(solution)/shard_map/ppermute | solution.py:279
  103.3 2.8 %collective-permute-start.11 = (f32[8,8,128]{2,1,0:T(8,128)S(1)}, f32[8,8,128]{2,1,0:T(8,128)S(1)}, u32[]{:S(2)}, u32[]{:S(2)}) collective-permute-start(f32[8,8,128]{2,1,0:T(8,128)S(1)} %get-tuple-element.42), channel_id=1, source_target_pairs={{32,64},{64,32},{96,128},{128,96},{160,192},{192,160},{224,256},{2... | collective-permute-start | bytes 98312 | tf_op jit(solution)/shard_map/ppermute | solution.py:278
  107.2 4.0 %collective-permute-done.11.yf_ref = f32[8,8,128]{2,1,0:T(8,128)S(1)} collective-permute-done((f32[8,8,128]{2,1,0:T(8,128)S(1)}, f32[8,8,128]{2,1,0:T(8,128)S(1)}, u32[]{:S(2)}, u32[]{:S(2)}) %collective-permute-start.11) | collective-permute-done | bytes 32800 | tf_op jit(solution)/shard_map/ppermute | solution.py:278
  111.2 1.2 %shard_map.61 = f32[8,16,128]{2,1,0:T(8,128)} custom-call(s32[2]{0:T(128)S(1)} %pad_add_fusion.flags, f32[12,24,128]{2,1,0:T(8,128)S(1)} %get-tuple-element.36.est_ref, f32[8,24,128]{2,1,0:T(8,128)S(1)} %get-tuple-element.40.total_ref, f32[8,8,128]{2,1,0:T(8,128)S(1)} %collective-permute-done.10.yn_ref, f32[8,8,128]{2,1,0:T(8,128)S(1)} %collective-permute-done.11.yf_ref), custom_call_target="tpu_custom_call" | custom-call | tf_op jit(solution)/shard_map/pallas_call | solution.py:289
  (13 shorter events, 2.8 us)
Async XLA Ops:
  2.3 8.4 %copy-start = (f32[8,16,128]{2,1,0:T(8,128)S(1)}, f32[8,16,128]{2,1,0:T(8,128)}, u32[]{:S(2)}) copy-start(f32[8,16,128]{2,1,0:T(8,128)} %own_ref.1) | copy-start | bytes 196612
  2.3 51.4 %all-to-all-start = ((f32[16,136,128]{2,1,0:T(8,128)}), f32[16,136,128]{2,1,0:T(8,128)S(1)}, u32[]{:S(2)}, u32[]{:S(2)}) async-start(f32[16,136,128]{2,1,0:T(8,128)} %shard_map.56), calls=%async_computation | async-start | bytes 2228224 | tf_op jit(solution)/shard_map/all_to_all | solution.py:327
  10.7 27.9 %collective-permute-start.1 = (f32[8,8,128]{2,1,0:T(8,128)S(1)}, f32[8,8,128]{2,1,0:T(8,128)S(1)}, u32[]{:S(2)}, u32[]{:S(2)}) collective-permute-start(f32[8,8,128]{2,1,0:T(8,128)S(1)} %get-tuple-element.43), channel_id=1, source_target_pairs={{32,64},{64,32},{96,128},{128,96},{160,192},{192,160},{224,256},{2... | collective-permute-start | bytes 98312 | tf_op jit(solution)/shard_map/ppermute | solution.py:278
  15.2 23.3 %collective-permute-start = (f32[8,8,128]{2,1,0:T(8,128)S(1)}, f32[8,8,128]{2,1,0:T(8,128)S(1)}, u32[]{:S(2)}, u32[]{:S(2)}) collective-permute-start(f32[8,8,128]{2,1,0:T(8,128)S(1)} %get-tuple-element.44), channel_id=1, source_target_pairs={{0,32},{32,0},{64,96},{96,64},{128,160},{160,128},{192,224},{224,1... | collective-permute-start | bytes 98312 | tf_op jit(solution)/shard_map/ppermute | solution.py:279
  39.1 12.9 %collective-permute-start.2 = (f32[2,24,128]{2,1,0:T(8,128)S(1)}, f32[2,24,128]{2,1,0:T(8,128)S(1)}, u32[]{:S(2)}, u32[]{:S(2)}) collective-permute-start(f32[2,24,128]{2,1,0:T(8,128)S(1)} %get-tuple-element.25), channel_id=1, source_target_pairs={{0,1},{1,0},{2,3},{3,2},{4,5},{5,4},{6,7},{7,6},{8,9},{9,8},{10,11... | collective-permute-start | bytes 73736 | tf_op jit(solution)/shard_map/ppermute | solution.py:279
  41.0 12.7 %collective-permute-start.3 = (f32[2,24,128]{2,1,0:T(8,128)S(1)}, f32[2,24,128]{2,1,0:T(8,128)S(1)}, u32[]{:S(2)}, u32[]{:S(2)}) collective-permute-start(f32[2,24,128]{2,1,0:T(8,128)S(1)} %get-tuple-element.26), channel_id=1, source_target_pairs={{1,2},{2,1},{3,4},{4,3},{5,6},{6,5},{7,8},{8,7},{9,10},{10,9},{11,... | collective-permute-start | bytes 73736 | tf_op jit(solution)/shard_map/ppermute | solution.py:278
  60.7 10.5 %collective-permute-start.4 = (f32[4,24,128]{2,1,0:T(8,128)S(1)}, f32[4,24,128]{2,1,0:T(8,128)S(1)}, u32[]{:S(2)}, u32[]{:S(2)}) collective-permute-start(f32[4,24,128]{2,1,0:T(8,128)S(1)} %get-tuple-element.29), channel_id=1, source_target_pairs={{0,1},{1,0},{2,3},{3,2},{4,5},{5,4},{6,7},{7,6},{8,9},{9,8},{10,11... | collective-permute-start | bytes 147464 | tf_op jit(solution)/shard_map/ppermute | solution.py:279
  62.6 10.4 %collective-permute-start.5 = (f32[4,24,128]{2,1,0:T(8,128)S(1)}, f32[4,24,128]{2,1,0:T(8,128)S(1)}, u32[]{:S(2)}, u32[]{:S(2)}) collective-permute-start(f32[4,24,128]{2,1,0:T(8,128)S(1)} %get-tuple-element.30), channel_id=1, source_target_pairs={{1,2},{2,1},{3,4},{4,3},{5,6},{6,5},{7,8},{8,7},{9,10},{10,9},{11,... | collective-permute-start | bytes 147464 | tf_op jit(solution)/shard_map/ppermute | solution.py:278
  73.6 6.0 %collective-permute-start.6 = (f32[12,8,128]{2,1,0:T(8,128)S(1)}, f32[12,8,128]{2,1,0:T(8,128)S(1)}, u32[]{:S(2)}, u32[]{:S(2)}) collective-permute-start(f32[12,8,128]{2,1,0:T(8,128)S(1)} %get-tuple-element.32), channel_id=1, source_target_pairs={{0,32},{32,0},{64,96},{96,64},{128,160},{160,128},{192,224},{224,1... | collective-permute-start | bytes 147464 | tf_op jit(solution)/shard_map/ppermute | solution.py:279
  75.5 8.1 %collective-permute-start.7 = (f32[12,8,128]{2,1,0:T(8,128)S(1)}, f32[12,8,128]{2,1,0:T(8,128)S(1)}, u32[]{:S(2)}, u32[]{:S(2)}) collective-permute-start(f32[12,8,128]{2,1,0:T(8,128)S(1)} %get-tuple-element.33), channel_id=1, source_target_pairs={{32,64},{64,32},{96,128},{128,96},{160,192},{192,160},{224,256},{2... | collective-permute-start | bytes 147464 | tf_op jit(solution)/shard_map/ppermute | solution.py:278
  88.8 10.4 %collective-permute-start.8 = (f32[2,24,128]{2,1,0:T(8,128)S(1)}, f32[2,24,128]{2,1,0:T(8,128)S(1)}, u32[]{:S(2)}, u32[]{:S(2)}) collective-permute-start(f32[2,24,128]{2,1,0:T(8,128)S(1)} %get-tuple-element.38), channel_id=1, source_target_pairs={{0,1},{1,0},{2,3},{3,2},{4,5},{5,4},{6,7},{7,6},{8,9},{9,8},{10,11... | collective-permute-start | bytes 73736 | tf_op jit(solution)/shard_map/ppermute | solution.py:279
  90.8 10.0 %collective-permute-start.9 = (f32[2,24,128]{2,1,0:T(8,128)S(1)}, f32[2,24,128]{2,1,0:T(8,128)S(1)}, u32[]{:S(2)}, u32[]{:S(2)}) collective-permute-start(f32[2,24,128]{2,1,0:T(8,128)S(1)} %get-tuple-element.39), channel_id=1, source_target_pairs={{1,2},{2,1},{3,4},{4,3},{5,6},{6,5},{7,8},{8,7},{9,10},{10,9},{11,... | collective-permute-start | bytes 73736 | tf_op jit(solution)/shard_map/ppermute | solution.py:278
  101.3 5.8 %collective-permute-start.10 = (f32[8,8,128]{2,1,0:T(8,128)S(1)}, f32[8,8,128]{2,1,0:T(8,128)S(1)}, u32[]{:S(2)}, u32[]{:S(2)}) collective-permute-start(f32[8,8,128]{2,1,0:T(8,128)S(1)} %get-tuple-element.41), channel_id=1, source_target_pairs={{0,32},{32,0},{64,96},{96,64},{128,160},{160,128},{192,224},{224,1... | collective-permute-start | bytes 98312 | tf_op jit(solution)/shard_map/ppermute | solution.py:279
  103.3 7.9 %collective-permute-start.11 = (f32[8,8,128]{2,1,0:T(8,128)S(1)}, f32[8,8,128]{2,1,0:T(8,128)S(1)}, u32[]{:S(2)}, u32[]{:S(2)}) collective-permute-start(f32[8,8,128]{2,1,0:T(8,128)S(1)} %get-tuple-element.42), channel_id=1, source_target_pairs={{32,64},{64,32},{96,128},{128,96},{160,192},{192,160},{224,256},{2... | collective-permute-start | bytes 98312 | tf_op jit(solution)/shard_map/ppermute | solution.py:278

commit v7 on v6

--- a/solution.py
+++ b/solution.py
@@ -24,18 +24,6 @@
     left = jnp.concatenate(split(x), axis=1)
     right = jnp.concatenate([matrix, matrix], axis=0)
     both = jnp.dot(left, right, preferred_element_type=jnp.float32)
-    return both[:, 0:LANES] + both[:, LANES:]
-
-
-def product_t(x, matrix):
-    left = jnp.concatenate(split(x), axis=1)
-    high, low = matrix[:, 0:LANES], matrix[:, LANES:]
-    right = jnp.concatenate(
-        [jnp.concatenate([high, high], axis=1), jnp.concatenate([low, low], axis=1)], axis=0
-    )
-    both = lax.dot_general(
-        left, right, (((1,), (1,)), ((), ())), preferred_element_type=jnp.float32
-    )
     return both[:, 0:LANES] + both[:, LANES:]
 
 
@@ -92,10 +80,19 @@
         copy.wait()
 
 
-def make_tables(data_ref, table_ref):
+def make_tables(sizes, data_ref, table_ref, axial):
+    _, _, nz = sizes
     views = data_ref.shape[0]
     lane = lax.broadcasted_iota(jnp.int32, (8, LANES), 1)
     sub = lax.broadcasted_iota(jnp.int32, (8, LANES), 0)
+    for v in range(views):
+        axial[v : v + 1, :] = data_ref[v, BLOCK : BLOCK + 1, :]
+    z = lax.broadcasted_iota(jnp.int32, (LANES, LANES), 0)
+    zz = lax.broadcasted_iota(jnp.int32, (LANES, LANES), 1)
+    reverse = jnp.where(z + zz == nz - 1, 1.0, 0.0).astype(jnp.float32)
+    axial[views:, :] = jnp.dot(
+        axial[0:views, :], reverse, precision=lax.Precision.HIGHEST, preferred_element_type=jnp.float32
+    )
 
     def one(v, carry):
         start = 0
@@ -148,13 +145,14 @@
     lax.fori_loop(0, views, one, 0, unroll=2)
 
 
-def corr_part(sizes, flags, ratio_of, conv_ref, table_ref, spread, part_ref, near_ref, far_ref):
+def corr_part(sizes, flags, ratio_of, corr_ref, table_ref, spread, part_ref, near_ref, far_ref, prepare):
     nf, ns, _ = sizes
     wide, views = spread.shape[1], spread.shape[0]
 
     def one(v, carry):
         first = [tap(table_ref, v, k) for k in range(nf)]
-        back = product_t(ratio_of(v), conv_ref[v])
+        prepare(v)
+        back = product(ratio_of(v), corr_ref[v])
         for i in range(wide):
             for h in range(2):
                 t = None
@@ -199,14 +197,14 @@
     return jnp.where(even, far, near), jnp.where(even, near, far)
 
 
-def both_parts(sizes, flags, est_ref, data_ref, conv_ref, table_ref, part_ref, near_ref, far_ref, spread, ratio, prepare=lambda v: None):
+def both_parts(sizes, flags, est_ref, data_ref, conv_ref, corr_ref, table_ref, part_ref, near_ref, far_ref, spread, ratio, prepare=lambda v: None, prepare_corr=lambda v: None):
     def finish(v, blurred):
         ratio[v] = data_ref[v, 0:BLOCK, :] / blurred
 
     conv_part(sizes, est_ref, conv_ref, table_ref, spread, prepare, finish)
     corr_part(
         sizes, flags, lambda v: ratio[v],
-        conv_ref, table_ref, spread, part_ref, near_ref, far_ref,
+        corr_ref, table_ref, spread, part_ref, near_ref, far_ref, prepare_corr,
     )
 
 
@@ -220,8 +218,8 @@
     near_ref[...], far_ref[...] = edges(flags[0], out_ref[0:strip], out_ref[ROWS - strip :])
 
 
-def first_kernel(sizes, flags, own_ref, xn_ref, xf_ref, data_ref, est_ref, part_ref, near_ref, far_ref, conv_ref, table_ref, spread, ratio):
-    make_tables(data_ref, table_ref)
+def first_kernel(sizes, flags, own_ref, xn_ref, xf_ref, data_ref, est_ref, part_ref, near_ref, far_ref, conv_ref, corr_ref, table_ref, spread, ratio, axial):
+    make_tables(sizes, data_ref, table_ref, axial)
     low, high = sides(flags[0], xn_ref, xf_ref)
     strip = low.shape[0]
     est_ref[0:strip] = low
@@ -229,9 +227,12 @@
     est_ref[strip + ROWS :] = high
 
     def prepare(v):
-        banded(data_ref[v, BLOCK : BLOCK + 1, :], sizes[2] // 2, conv_ref.at[v])
-
-    both_parts(sizes, flags, est_ref, data_ref, conv_ref, table_ref, part_ref, near_ref, far_ref, spread, ratio, prepare)
+        banded(axial[pl.ds(v, 1), :], sizes[2] // 2, conv_ref.at[v])
+
+    def prepare_corr(v):
+        banded(axial[pl.ds(data_ref.shape[0] + v, 1), :], sizes[2] // 2, corr_ref.at[v])
+
+    both_parts(sizes, flags, est_ref, data_ref, conv_ref, corr_ref, table_ref, part_ref, near_ref, far_ref, spread, ratio, prepare, prepare_corr)
 
 
 def updated(views, flags, est_ref, total_ref, yn_ref, yf_ref, new_ref):
@@ -241,9 +242,9 @@
     new_ref[:, 16:24, :] = est_ref[:, 16:24, :] * ((total_ref[:, 16:24, :] + high) / views)
 
 
-def pass_kernel(sizes, views, flags, est_ref, total_ref, yn_ref, yf_ref, data_ref, conv_ref, table_ref, new_ref, part_ref, near_ref, far_ref, spread, ratio):
+def pass_kernel(sizes, views, flags, est_ref, total_ref, yn_ref, yf_ref, data_ref, conv_ref, corr_ref, table_ref, new_ref, part_ref, near_ref, far_ref, spread, ratio):
     updated(views, flags, est_ref, total_ref, yn_ref, yf_ref, new_ref)
-    both_parts(sizes, flags, new_ref, data_ref, conv_ref, table_ref, part_ref, near_ref, far_ref, spread, ratio)
+    both_parts(sizes, flags, new_ref, data_ref, conv_ref, corr_ref, table_ref, part_ref, near_ref, far_ref, spread, ratio)
 
 
 def rows_kernel(flags, part_ref, near_ref, far_ref, out_ref, yn_ref, yf_ref):
@@ -349,11 +350,11 @@
         ((rows, COLS, lanes), thin, thin),
     )
     near, far = swapped(near, far, "tile")
-    current, part, near, far, matrix, table = call(
+    current, part, near, far, conv, corr, table = call(
         functools.partial(first_kernel, sizes),
         (flags, own, near, far, data),
-        (block, block, strips[0], strips[0], matrices, (views, 16, lanes)),
-        scratch,
+        (block, block, strips[0], strips[0], matrices, matrices, (views, 16, lanes)),
+        scratch + [pltpu.VMEM((2 * views, lanes), jnp.float32)],
         limit=16 << 20,
     )
     for step in range(1, ITERS):
@@ -361,7 +362,7 @@
         total, yn, yf = joined(part, near, far, wide)
         current, part, near, far = call(
             functools.partial(pass_kernel, sizes, views),
-            (flags, current, total, yn, yf, data, matrix, table),
+            (flags, current, total, yn, yf, data, conv, corr, table),
             (block, block, strips[step], strips[step]),
             scratch,
             limit=12 << 20,

time: 113 us -> 113 us (level)
  no operation moved by 1% of the time
where the time goes in v7:
time: 113 us; the launch traced here: 112 us
  starting transfers between devices  59 us (52%)
  waiting for transfers between devices  35.4 us (31%)
  Pallas kernels  17.6 us (16%)
    ppermute x6, starting transfers between devices, swapped(): far = lax.ppermute(far, axis, pairs(count, 1))  38.8 us
    ppermute x6, waiting for transfers between devices, swapped(): far = lax.ppermute(far, axis, pairs(count, 1))  33.9 us
    pallas_call x6, Pallas kernels, call(): pl.pallas_call(kernel, in_specs=[SMEM] + [VMEM] * (len(ins) - 1), out_spe...  15.4 us
    ppermute x6, starting transfers between devices, swapped(): near = lax.ppermute(near, axis, pairs(count, 0))  11.8 us
    all_to_all x1, starting transfers between devices, local(): data = lax.all_to_all(data, 'view', 0, 0, tiled=True)  8.34 us
    pallas_call x1, Pallas kernels, local(): pl.pallas_call(pieces_kernel, in_specs=[hbm] * 4, out_specs=hbm, out_shap...  2.26 us
  transfers between devices with their start and end apart: 13, of which 8 were waited for; matrix products, arithmetic and copies ran while one was open for 0% of the time, Pallas kernels for 1%

profile of v7, /device:TPU:70, one launch (start us, length us, event | category | flops | bytes accessed | tf_op | source)
XLA Modules:
  0.0 112.3 jit_solution(9567740517757198525)
XLA Ops:
  0.0 2.3 %shard_map.56 = f32[16,136,128]{2,1,0:T(8,128)} custom-call(f32[8,16,16,128]{3,2,1,0:T(8,128)} %bitcast.3, f32[1,33]{1,0:T(1,128)} %axial_ref.1, f32[1,5]{1,0:T(1,128)} %first_ref.1, f32[1,7]{1,0:T(1,128)} %second_ref.1), custom_call_target="tpu_custom_call" | custom-call | tf_op jit(solution)/shard_map/pallas_call | solution.py:313
  2.3 8.3 %all-to-all-start = ((f32[16,136,128]{2,1,0:T(8,128)}), f32[16,136,128]{2,1,0:T(8,128)S(1)}, u32[]{:S(2)}, u32[]{:S(2)}) async-start(f32[16,136,128]{2,1,0:T(8,128)} %shard_map.56), calls=%async_computation | async-start | bytes 2228224 | tf_op jit(solution)/shard_map/all_to_all | solution.py:328
  10.7 4.6 %collective-permute-start.1 = (f32[8,8,128]{2,1,0:T(8,128)S(1)}, f32[8,8,128]{2,1,0:T(8,128)S(1)}, u32[]{:S(2)}, u32[]{:S(2)}) collective-permute-start(f32[8,8,128]{2,1,0:T(8,128)S(1)} %get-tuple-element.45), channel_id=1, source_target_pairs={{32,64},{64,32},{96,128},{128,96},{160,192},{192,160},{224,256},{2... | collective-permute-start | bytes 98312 | tf_op jit(solution)/shard_map/ppermute | solution.py:279
  15.2 2.2 %collective-permute-start = (f32[8,8,128]{2,1,0:T(8,128)S(1)}, f32[8,8,128]{2,1,0:T(8,128)S(1)}, u32[]{:S(2)}, u32[]{:S(2)}) collective-permute-start(f32[8,8,128]{2,1,0:T(8,128)S(1)} %get-tuple-element.46), channel_id=1, source_target_pairs={{0,32},{32,0},{64,96},{96,64},{128,160},{160,128},{192,224},{224,1... | collective-permute-start | bytes 98312 | tf_op jit(solution)/shard_map/ppermute | solution.py:280
  17.5 21.1 %collective-permute-done.1.yf_ref = f32[8,8,128]{2,1,0:T(8,128)S(1)} collective-permute-done((f32[8,8,128]{2,1,0:T(8,128)S(1)}, f32[8,8,128]{2,1,0:T(8,128)S(1)}, u32[]{:S(2)}, u32[]{:S(2)}) %collective-permute-start.1) | collective-permute-done | bytes 32800 | tf_op jit(solution)/shard_map/ppermute | solution.py:279
  39.1 1.9 %collective-permute-start.2 = (f32[2,24,128]{2,1,0:T(8,128)S(1)}, f32[2,24,128]{2,1,0:T(8,128)S(1)}, u32[]{:S(2)}, u32[]{:S(2)}) collective-permute-start(f32[2,24,128]{2,1,0:T(8,128)S(1)} %get-tuple-element.26), channel_id=1, source_target_pairs={{0,1},{1,0},{2,3},{3,2},{4,5},{5,4},{6,7},{7,6},{8,9},{9,8},{10,11... | collective-permute-start | bytes 73736 | tf_op jit(solution)/shard_map/ppermute | solution.py:280
  41.0 10.9 %collective-permute-start.3 = (f32[2,24,128]{2,1,0:T(8,128)S(1)}, f32[2,24,128]{2,1,0:T(8,128)S(1)}, u32[]{:S(2)}, u32[]{:S(2)}) collective-permute-start(f32[2,24,128]{2,1,0:T(8,128)S(1)} %get-tuple-element.27), channel_id=1, source_target_pairs={{1,2},{2,1},{3,4},{4,3},{5,6},{6,5},{7,8},{8,7},{9,10},{10,9},{11,... | collective-permute-start | bytes 73736 | tf_op jit(solution)/shard_map/ppermute | solution.py:279
  52.0 1.5 %collective-permute-done.3.xf_ref = f32[2,24,128]{2,1,0:T(8,128)S(1)} collective-permute-done((f32[2,24,128]{2,1,0:T(8,128)S(1)}, f32[2,24,128]{2,1,0:T(8,128)S(1)}, u32[]{:S(2)}, u32[]{:S(2)}) %collective-permute-start.3) | collective-permute-done | bytes 24608 | tf_op jit(solution)/shard_map/ppermute | solution.py:279
  53.5 7.5 %shard_map.57 = (f32[12,24,128]{2,1,0:T(8,128)S(1)}, f32[12,24,128]{2,1,0:T(8,128)S(1)}, f32[4,24,128]{2,1,0:T(8,128)S(1)}, f32[4,24,128]{2,1,0:T(8,128)S(1)}, b...) custom-call(s32[2]{0:T(128)S(1)} %pad_add_fusion.flags, ...), custom_call_target="tpu_custom_call" | custom-call | tf_op jit(solution)/shard_map/pallas_call | solution.py:290
  61.0 1.9 %collective-permute-start.4 = (f32[4,24,128]{2,1,0:T(8,128)S(1)}, f32[4,24,128]{2,1,0:T(8,128)S(1)}, u32[]{:S(2)}, u32[]{:S(2)}) collective-permute-start(f32[4,24,128]{2,1,0:T(8,128)S(1)} %get-tuple-element.30), channel_id=1, source_target_pairs={{0,1},{1,0},{2,3},{3,2},{4,5},{5,4},{6,7},{7,6},{8,9},{9,8},{10,11... | collective-permute-start | bytes 147464 | tf_op jit(solution)/shard_map/ppermute | solution.py:280
  62.9 8.4 %collective-permute-start.5 = (f32[4,24,128]{2,1,0:T(8,128)S(1)}, f32[4,24,128]{2,1,0:T(8,128)S(1)}, u32[]{:S(2)}, u32[]{:S(2)}) collective-permute-start(f32[4,24,128]{2,1,0:T(8,128)S(1)} %get-tuple-element.31), channel_id=1, source_target_pairs={{1,2},{2,1},{3,4},{4,3},{5,6},{6,5},{7,8},{8,7},{9,10},{10,9},{11,... | collective-permute-start | bytes 147464 | tf_op jit(solution)/shard_map/ppermute | solution.py:279
  71.4 1.8 %collective-permute-done.5.far_ref = f32[4,24,128]{2,1,0:T(8,128)S(1)} collective-permute-done((f32[4,24,128]{2,1,0:T(8,128)S(1)}, f32[4,24,128]{2,1,0:T(8,128)S(1)}, u32[]{:S(2)}, u32[]{:S(2)}) %collective-permute-start.5) | collective-permute-done | bytes 49184 | tf_op jit(solution)/shard_map/ppermute | solution.py:279
  73.7 1.9 %collective-permute-start.6 = (f32[12,8,128]{2,1,0:T(8,128)S(1)}, f32[12,8,128]{2,1,0:T(8,128)S(1)}, u32[]{:S(2)}, u32[]{:S(2)}) collective-permute-start(f32[12,8,128]{2,1,0:T(8,128)S(1)} %get-tuple-element.33), channel_id=1, source_target_pairs={{0,32},{32,0},{64,96},{96,64},{128,160},{160,128},{192,224},{224,1... | collective-permute-start | bytes 147464 | tf_op jit(solution)/shard_map/ppermute | solution.py:280
  75.6 3.2 %collective-permute-start.7 = (f32[12,8,128]{2,1,0:T(8,128)S(1)}, f32[12,8,128]{2,1,0:T(8,128)S(1)}, u32[]{:S(2)}, u32[]{:S(2)}) collective-permute-start(f32[12,8,128]{2,1,0:T(8,128)S(1)} %get-tuple-element.34), channel_id=1, source_target_pairs={{32,64},{64,32},{96,128},{128,96},{160,192},{192,160},{224,256},{2... | collective-permute-start | bytes 147464 | tf_op jit(solution)/shard_map/ppermute | solution.py:279
  78.9 0.8 collective-permute-done.6.yn_ref
  79.7 4.0 %collective-permute-done.7.yf_ref = f32[12,8,128]{2,1,0:T(8,128)S(1)} collective-permute-done((f32[12,8,128]{2,1,0:T(8,128)S(1)}, f32[12,8,128]{2,1,0:T(8,128)S(1)}, u32[]{:S(2)}, u32[]{:S(2)}) %collective-permute-start.7) | collective-permute-done | bytes 49184 | tf_op jit(solution)/shard_map/ppermute | solution.py:279
  83.7 5.0 %shard_map.59 = (f32[12,24,128]{2,1,0:T(8,128)S(1)}, f32[12,24,128]{2,1,0:T(8,128)S(1)}, f32[2,24,128]{2,1,0:T(8,128)S(1)}, f32[2,24,128]{2,1,0:T(8,128)S(1)}) custom-call(s32[2]{0:T(128)S(1)} %pad_add_fusion.flags, f32[12,24,128]{2,1,0:T(8,128)S(1)} %get-tuple-element.28.est_ref, f32[12,24,128]{2,1,0:T(8,128)S(1)} %get-tuple-element.32.total_ref, ...), custom_call_target="tpu_custom_call" | custom-call | tf_op jit(solution)/shard_map/pallas_call | solution.py:290
  88.7 1.9 %collective-permute-start.8 = (f32[2,24,128]{2,1,0:T(8,128)S(1)}, f32[2,24,128]{2,1,0:T(8,128)S(1)}, u32[]{:S(2)}, u32[]{:S(2)}) collective-permute-start(f32[2,24,128]{2,1,0:T(8,128)S(1)} %get-tuple-element.40), channel_id=1, source_target_pairs={{0,1},{1,0},{2,3},{3,2},{4,5},{5,4},{6,7},{7,6},{8,9},{9,8},{10,11... | collective-permute-start | bytes 73736 | tf_op jit(solution)/shard_map/ppermute | solution.py:280
  90.6 8.5 %collective-permute-start.9 = (f32[2,24,128]{2,1,0:T(8,128)S(1)}, f32[2,24,128]{2,1,0:T(8,128)S(1)}, u32[]{:S(2)}, u32[]{:S(2)}) collective-permute-start(f32[2,24,128]{2,1,0:T(8,128)S(1)} %get-tuple-element.41), channel_id=1, source_target_pairs={{1,2},{2,1},{3,4},{4,3},{5,6},{6,5},{7,8},{8,7},{9,10},{10,9},{11,... | collective-permute-start | bytes 73736 | tf_op jit(solution)/shard_map/ppermute | solution.py:279
  99.2 1.5 %collective-permute-done.9.far_ref = f32[2,24,128]{2,1,0:T(8,128)S(1)} collective-permute-done((f32[2,24,128]{2,1,0:T(8,128)S(1)}, f32[2,24,128]{2,1,0:T(8,128)S(1)}, u32[]{:S(2)}, u32[]{:S(2)}) %collective-permute-start.9) | collective-permute-done | bytes 24608 | tf_op jit(solution)/shard_map/ppermute | solution.py:279
  101.2 1.9 %collective-permute-start.10 = (f32[8,8,128]{2,1,0:T(8,128)S(1)}, f32[8,8,128]{2,1,0:T(8,128)S(1)}, u32[]{:S(2)}, u32[]{:S(2)}) collective-permute-start(f32[8,8,128]{2,1,0:T(8,128)S(1)} %get-tuple-element.43), channel_id=1, source_target_pairs={{0,32},{32,0},{64,96},{96,64},{128,160},{160,128},{192,224},{224,1... | collective-permute-start | bytes 98312 | tf_op jit(solution)/shard_map/ppermute | solution.py:280
  103.1 3.2 %collective-permute-start.11 = (f32[8,8,128]{2,1,0:T(8,128)S(1)}, f32[8,8,128]{2,1,0:T(8,128)S(1)}, u32[]{:S(2)}, u32[]{:S(2)}) collective-permute-start(f32[8,8,128]{2,1,0:T(8,128)S(1)} %get-tuple-element.44), channel_id=1, source_target_pairs={{32,64},{64,32},{96,128},{128,96},{160,192},{192,160},{224,256},{2... | collective-permute-start | bytes 98312 | tf_op jit(solution)/shard_map/ppermute | solution.py:279
  107.0 4.0 %collective-permute-done.11.yf_ref = f32[8,8,128]{2,1,0:T(8,128)S(1)} collective-permute-done((f32[8,8,128]{2,1,0:T(8,128)S(1)}, f32[8,8,128]{2,1,0:T(8,128)S(1)}, u32[]{:S(2)}, u32[]{:S(2)}) %collective-permute-start.11) | collective-permute-done | bytes 32800 | tf_op jit(solution)/shard_map/ppermute | solution.py:279
  111.1 1.2 %shard_map.61 = f32[8,16,128]{2,1,0:T(8,128)} custom-call(s32[2]{0:T(128)S(1)} %pad_add_fusion.flags, f32[12,24,128]{2,1,0:T(8,128)S(1)} %get-tuple-element.38.est_ref, f32[8,24,128]{2,1,0:T(8,128)S(1)} %get-tuple-element.42.total_ref, f32[8,8,128]{2,1,0:T(8,128)S(1)} %collective-permute-done.10.yn_ref, f32[8,8,128]{2,1,0:T(8,128)S(1)} %collective-permute-done.11.yf_ref), custom_call_target="tpu_custom_call" | custom-call | tf_op jit(solution)/shard_map/pallas_call | solution.py:290
  (13 shorter events, 2.5 us)
Async XLA Ops:
  2.3 8.4 %copy-start = (f32[8,16,128]{2,1,0:T(8,128)S(1)}, f32[8,16,128]{2,1,0:T(8,128)}, u32[]{:S(2)}) copy-start(f32[8,16,128]{2,1,0:T(8,128)} %own_ref.1) | copy-start | bytes 196612
  2.3 51.2 %all-to-all-start = ((f32[16,136,128]{2,1,0:T(8,128)}), f32[16,136,128]{2,1,0:T(8,128)S(1)}, u32[]{:S(2)}, u32[]{:S(2)}) async-start(f32[16,136,128]{2,1,0:T(8,128)} %shard_map.56), calls=%async_computation | async-start | bytes 2228224 | tf_op jit(solution)/shard_map/all_to_all | solution.py:328
  10.7 27.9 %collective-permute-start.1 = (f32[8,8,128]{2,1,0:T(8,128)S(1)}, f32[8,8,128]{2,1,0:T(8,128)S(1)}, u32[]{:S(2)}, u32[]{:S(2)}) collective-permute-start(f32[8,8,128]{2,1,0:T(8,128)S(1)} %get-tuple-element.45), channel_id=1, source_target_pairs={{32,64},{64,32},{96,128},{128,96},{160,192},{192,160},{224,256},{2... | collective-permute-start | bytes 98312 | tf_op jit(solution)/shard_map/ppermute | solution.py:279
  15.2 23.3 %collective-permute-start = (f32[8,8,128]{2,1,0:T(8,128)S(1)}, f32[8,8,128]{2,1,0:T(8,128)S(1)}, u32[]{:S(2)}, u32[]{:S(2)}) collective-permute-start(f32[8,8,128]{2,1,0:T(8,128)S(1)} %get-tuple-element.46), channel_id=1, source_target_pairs={{0,32},{32,0},{64,96},{96,64},{128,160},{160,128},{192,224},{224,1... | collective-permute-start | bytes 98312 | tf_op jit(solution)/shard_map/ppermute | solution.py:280
  39.1 12.9 %collective-permute-start.2 = (f32[2,24,128]{2,1,0:T(8,128)S(1)}, f32[2,24,128]{2,1,0:T(8,128)S(1)}, u32[]{:S(2)}, u32[]{:S(2)}) collective-permute-start(f32[2,24,128]{2,1,0:T(8,128)S(1)} %get-tuple-element.26), channel_id=1, source_target_pairs={{0,1},{1,0},{2,3},{3,2},{4,5},{5,4},{6,7},{7,6},{8,9},{9,8},{10,11... | collective-permute-start | bytes 73736 | tf_op jit(solution)/shard_map/ppermute | solution.py:280
  41.0 12.4 %collective-permute-start.3 = (f32[2,24,128]{2,1,0:T(8,128)S(1)}, f32[2,24,128]{2,1,0:T(8,128)S(1)}, u32[]{:S(2)}, u32[]{:S(2)}) collective-permute-start(f32[2,24,128]{2,1,0:T(8,128)S(1)} %get-tuple-element.27), channel_id=1, source_target_pairs={{1,2},{2,1},{3,4},{4,3},{5,6},{6,5},{7,8},{8,7},{9,10},{10,9},{11,... | collective-permute-start | bytes 73736 | tf_op jit(solution)/shard_map/ppermute | solution.py:279
  61.0 10.4 %collective-permute-start.4 = (f32[4,24,128]{2,1,0:T(8,128)S(1)}, f32[4,24,128]{2,1,0:T(8,128)S(1)}, u32[]{:S(2)}, u32[]{:S(2)}) collective-permute-start(f32[4,24,128]{2,1,0:T(8,128)S(1)} %get-tuple-element.30), channel_id=1, source_target_pairs={{0,1},{1,0},{2,3},{3,2},{4,5},{5,4},{6,7},{7,6},{8,9},{9,8},{10,11... | collective-permute-start | bytes 147464 | tf_op jit(solution)/shard_map/ppermute | solution.py:280
  62.9 10.2 %collective-permute-start.5 = (f32[4,24,128]{2,1,0:T(8,128)S(1)}, f32[4,24,128]{2,1,0:T(8,128)S(1)}, u32[]{:S(2)}, u32[]{:S(2)}) collective-permute-start(f32[4,24,128]{2,1,0:T(8,128)S(1)} %get-tuple-element.31), channel_id=1, source_target_pairs={{1,2},{2,1},{3,4},{4,3},{5,6},{6,5},{7,8},{8,7},{9,10},{10,9},{11,... | collective-permute-start | bytes 147464 | tf_op jit(solution)/shard_map/ppermute | solution.py:279
  73.7 6.0 %collective-permute-start.6 = (f32[12,8,128]{2,1,0:T(8,128)S(1)}, f32[12,8,128]{2,1,0:T(8,128)S(1)}, u32[]{:S(2)}, u32[]{:S(2)}) collective-permute-start(f32[12,8,128]{2,1,0:T(8,128)S(1)} %get-tuple-element.33), channel_id=1, source_target_pairs={{0,32},{32,0},{64,96},{96,64},{128,160},{160,128},{192,224},{224,1... | collective-permute-start | bytes 147464 | tf_op jit(solution)/shard_map/ppermute | solution.py:280
  75.6 8.1 %collective-permute-start.7 = (f32[12,8,128]{2,1,0:T(8,128)S(1)}, f32[12,8,128]{2,1,0:T(8,128)S(1)}, u32[]{:S(2)}, u32[]{:S(2)}) collective-permute-start(f32[12,8,128]{2,1,0:T(8,128)S(1)} %get-tuple-element.34), channel_id=1, source_target_pairs={{32,64},{64,32},{96,128},{128,96},{160,192},{192,160},{224,256},{2... | collective-permute-start | bytes 147464 | tf_op jit(solution)/shard_map/ppermute | solution.py:279
  88.7 10.4 %collective-permute-start.8 = (f32[2,24,128]{2,1,0:T(8,128)S(1)}, f32[2,24,128]{2,1,0:T(8,128)S(1)}, u32[]{:S(2)}, u32[]{:S(2)}) collective-permute-start(f32[2,24,128]{2,1,0:T(8,128)S(1)} %get-tuple-element.40), channel_id=1, source_target_pairs={{0,1},{1,0},{2,3},{3,2},{4,5},{5,4},{6,7},{7,6},{8,9},{9,8},{10,11... | collective-permute-start | bytes 73736 | tf_op jit(solution)/shard_map/ppermute | solution.py:280
  90.6 10.0 %collective-permute-start.9 = (f32[2,24,128]{2,1,0:T(8,128)S(1)}, f32[2,24,128]{2,1,0:T(8,128)S(1)}, u32[]{:S(2)}, u32[]{:S(2)}) collective-permute-start(f32[2,24,128]{2,1,0:T(8,128)S(1)} %get-tuple-element.41), channel_id=1, source_target_pairs={{1,2},{2,1},{3,4},{4,3},{5,6},{6,5},{7,8},{8,7},{9,10},{10,9},{11,... | collective-permute-start | bytes 73736 | tf_op jit(solution)/shard_map/ppermute | solution.py:279
  101.2 5.8 %collective-permute-start.10 = (f32[8,8,128]{2,1,0:T(8,128)S(1)}, f32[8,8,128]{2,1,0:T(8,128)S(1)}, u32[]{:S(2)}, u32[]{:S(2)}) collective-permute-start(f32[8,8,128]{2,1,0:T(8,128)S(1)} %get-tuple-element.43), channel_id=1, source_target_pairs={{0,32},{32,0},{64,96},{96,64},{128,160},{160,128},{192,224},{224,1... | collective-permute-start | bytes 98312 | tf_op jit(solution)/shard_map/ppermute | solution.py:280
  103.1 7.9 %collective-permute-start.11 = (f32[8,8,128]{2,1,0:T(8,128)S(1)}, f32[8,8,128]{2,1,0:T(8,128)S(1)}, u32[]{:S(2)}, u32[]{:S(2)}) collective-permute-start(f32[8,8,128]{2,1,0:T(8,128)S(1)} %get-tuple-element.44), channel_id=1, source_target_pairs={{32,64},{64,32},{96,128},{128,96},{160,192},{192,160},{224,256},{2... | collective-permute-start | bytes 98312 | tf_op jit(solution)/shard_map/ppermute | solution.py:279

commit v8 on v7

--- a/solution.py
+++ b/solution.py
@@ -210,7 +210,7 @@
 
 def columns_kernel(halo, flags, own_ref, yn_ref, yf_ref, out_ref, near_ref, far_ref):
     low, high = sides(flags[1], yn_ref, yf_ref)
-    out_ref[:, 0:halo, :] = low[:, 8 - halo :, :]
+    out_ref[:, 0:halo, :] = low[:, WIDTH - halo :, :]
     out_ref[:, halo : halo + WIDTH, :] = own_ref[...]
     out_ref[:, halo + WIDTH : WIDTH + 2 * halo, :] = high[:, 0:halo, :]
     out_ref[:, WIDTH + 2 * halo :, :] = jnp.zeros((ROWS, COLS - WIDTH - 2 * halo, LANES), jnp.float32)
@@ -341,8 +341,7 @@
         yn, yf = swapped(yn, yf, "view")
         return total, yn, yf
 
-    yn, yf = edges(flags[1], estimate[:, 0:8], estimate[:, cols - 8 :])
-    yn, yf = swapped(yn, yf, "view")
+    yn, yf = swapped(estimate, estimate, "view")
     thin = (halo // 2, COLS, lanes)
     own, near, far = call(
         functools.partial(columns_kernel, ns // 2),

time: 113 us -> 114 us (level)
    ppermute x6, starting transfers between devices: 11.8 us -> 13 us  [swapped(): near = lax.ppermute(near, axis, pairs(count, 0))]
  transfers between devices with their start and end apart: 13 -> 13, of which waited for: 8 -> 9; matrix products, arithmetic and copies ran while one was open for 0% -> 0% of each run, Pallas kernels for 1% -> 0%
where the time goes in v8:
time: 114 us; the launch traced here: 113 us
  starting transfers between devices  59.3 us (52%)
  waiting for transfers between devices  36 us (32%)
  Pallas kernels  17.7 us (16%)
    ppermute x6, starting transfers between devices, swapped(): far = lax.ppermute(far, axis, pairs(count, 1))  38 us
    ppermute x6, waiting for transfers between devices, swapped(): far = lax.ppermute(far, axis, pairs(count, 1))  33.8 us
    pallas_call x6, Pallas kernels, call(): pl.pallas_call(kernel, in_specs=[SMEM] + [VMEM] * (len(ins) - 1), out_spe...  15.4 us
    ppermute x6, starting transfers between devices, swapped(): near = lax.ppermute(near, axis, pairs(count, 0))  13 us
    all_to_all x1, starting transfers between devices, local(): data = lax.all_to_all(data, 'view', 0, 0, tiled=True)  8.34 us
  transfers between devices with their start and end apart: 13, of which 9 were waited for; matrix products, arithmetic and copies ran while one was open for 0% of the time, Pallas kernels for 0%

profile of v8, /device:TPU:70, one launch (start us, length us, event | category | flops | bytes accessed | tf_op | source)
XLA Modules:
  0.0 113.2 jit_solution(3612128197447616113)
XLA Ops:
  0.0 2.3 %shard_map.56 = f32[16,136,128]{2,1,0:T(8,128)} custom-call(f32[8,16,16,128]{3,2,1,0:T(8,128)} %bitcast.3, f32[1,33]{1,0:T(1,128)} %axial_ref.1, f32[1,5]{1,0:T(1,128)} %first_ref.1, f32[1,7]{1,0:T(1,128)} %second_ref.1), custom_call_target="tpu_custom_call" | custom-call | tf_op jit(solution)/shard_map/pallas_call | solution.py:313
  2.3 8.3 %all-to-all-start = ((f32[16,136,128]{2,1,0:T(8,128)}), f32[16,136,128]{2,1,0:T(8,128)S(1)}, u32[]{:S(2)}, u32[]{:S(2)}) async-start(f32[16,136,128]{2,1,0:T(8,128)} %shard_map.56), calls=%async_computation | async-start | bytes 2228224 | tf_op jit(solution)/shard_map/all_to_all | solution.py:328
  10.6 3.4 %collective-permute-start = (f32[8,16,128]{2,1,0:T(8,128)S(1)}, f32[8,16,128]{2,1,0:T(8,128)S(1)}, u32[]{:S(2)}, u32[]{:S(2)}) collective-permute-start(f32[8,16,128]{2,1,0:T(8,128)S(1)} %copy-done), channel_id=1, source_target_pairs={{0,32},{32,0},{64,96},{96,64},{128,160},{160,128},{192,224},{224,1... | collective-permute-start | bytes 196616 | tf_op jit(solution)/shard_map/ppermute | solution.py:280
  14.0 4.0 %collective-permute-start.1 = (f32[8,16,128]{2,1,0:T(8,128)S(1)}, f32[8,16,128]{2,1,0:T(8,128)S(1)}, u32[]{:S(2)}, u32[]{:S(2)}) collective-permute-start(f32[8,16,128]{2,1,0:T(8,128)S(1)} %copy-done), channel_id=1, source_target_pairs={{32,64},{64,32},{96,128},{128,96},{160,192},{192,160},{224,256},{2... | collective-permute-start | bytes 196616 | tf_op jit(solution)/shard_map/ppermute | solution.py:279
  18.4 20.8 %collective-permute-done.1.yf_ref = f32[8,16,128]{2,1,0:T(8,128)S(1)} collective-permute-done((f32[8,16,128]{2,1,0:T(8,128)S(1)}, f32[8,16,128]{2,1,0:T(8,128)S(1)}, u32[]{:S(2)}, u32[]{:S(2)}) %collective-permute-start.1) | collective-permute-done | bytes 65568 | tf_op jit(solution)/shard_map/ppermute | solution.py:279
  39.8 1.9 %collective-permute-start.2 = (f32[2,24,128]{2,1,0:T(8,128)S(1)}, f32[2,24,128]{2,1,0:T(8,128)S(1)}, u32[]{:S(2)}, u32[]{:S(2)}) collective-permute-start(f32[2,24,128]{2,1,0:T(8,128)S(1)} %get-tuple-element.26), channel_id=1, source_target_pairs={{0,1},{1,0},{2,3},{3,2},{4,5},{5,4},{6,7},{7,6},{8,9},{9,8},{10,11... | collective-permute-start | bytes 73736 | tf_op jit(solution)/shard_map/ppermute | solution.py:280
  41.7 10.8 %collective-permute-start.3 = (f32[2,24,128]{2,1,0:T(8,128)S(1)}, f32[2,24,128]{2,1,0:T(8,128)S(1)}, u32[]{:S(2)}, u32[]{:S(2)}) collective-permute-start(f32[2,24,128]{2,1,0:T(8,128)S(1)} %get-tuple-element.27), channel_id=1, source_target_pairs={{1,2},{2,1},{3,4},{4,3},{5,6},{6,5},{7,8},{8,7},{9,10},{10,9},{11,... | collective-permute-start | bytes 73736 | tf_op jit(solution)/shard_map/ppermute | solution.py:279
  52.5 1.7 %collective-permute-done.3.xf_ref = f32[2,24,128]{2,1,0:T(8,128)S(1)} collective-permute-done((f32[2,24,128]{2,1,0:T(8,128)S(1)}, f32[2,24,128]{2,1,0:T(8,128)S(1)}, u32[]{:S(2)}, u32[]{:S(2)}) %collective-permute-start.3) | collective-permute-done | bytes 24608 | tf_op jit(solution)/shard_map/ppermute | solution.py:279
  54.2 7.5 %shard_map.57 = (f32[12,24,128]{2,1,0:T(8,128)S(1)}, f32[12,24,128]{2,1,0:T(8,128)S(1)}, f32[4,24,128]{2,1,0:T(8,128)S(1)}, f32[4,24,128]{2,1,0:T(8,128)S(1)}, b...) custom-call(s32[2]{0:T(128)S(1)} %pad_add_fusion.flags, ...), custom_call_target="tpu_custom_call" | custom-call | tf_op jit(solution)/shard_map/pallas_call | solution.py:290
  61.8 1.9 %collective-permute-start.4 = (f32[4,24,128]{2,1,0:T(8,128)S(1)}, f32[4,24,128]{2,1,0:T(8,128)S(1)}, u32[]{:S(2)}, u32[]{:S(2)}) collective-permute-start(f32[4,24,128]{2,1,0:T(8,128)S(1)} %get-tuple-element.30), channel_id=1, source_target_pairs={{0,1},{1,0},{2,3},{3,2},{4,5},{5,4},{6,7},{7,6},{8,9},{9,8},{10,11... | collective-permute-start | bytes 147464 | tf_op jit(solution)/shard_map/ppermute | solution.py:280
  63.7 8.6 %collective-permute-start.5 = (f32[4,24,128]{2,1,0:T(8,128)S(1)}, f32[4,24,128]{2,1,0:T(8,128)S(1)}, u32[]{:S(2)}, u32[]{:S(2)}) collective-permute-start(f32[4,24,128]{2,1,0:T(8,128)S(1)} %get-tuple-element.31), channel_id=1, source_target_pairs={{1,2},{2,1},{3,4},{4,3},{5,6},{6,5},{7,8},{8,7},{9,10},{10,9},{11,... | collective-permute-start | bytes 147464 | tf_op jit(solution)/shard_map/ppermute | solution.py:279
  72.3 1.7 %collective-permute-done.5.far_ref = f32[4,24,128]{2,1,0:T(8,128)S(1)} collective-permute-done((f32[4,24,128]{2,1,0:T(8,128)S(1)}, f32[4,24,128]{2,1,0:T(8,128)S(1)}, u32[]{:S(2)}, u32[]{:S(2)}) %collective-permute-start.5) | collective-permute-done | bytes 49184 | tf_op jit(solution)/shard_map/ppermute | solution.py:279
  74.6 1.9 %collective-permute-start.6 = (f32[12,8,128]{2,1,0:T(8,128)S(1)}, f32[12,8,128]{2,1,0:T(8,128)S(1)}, u32[]{:S(2)}, u32[]{:S(2)}) collective-permute-start(f32[12,8,128]{2,1,0:T(8,128)S(1)} %get-tuple-element.33), channel_id=1, source_target_pairs={{0,32},{32,0},{64,96},{96,64},{128,160},{160,128},{192,224},{224,1... | collective-permute-start | bytes 147464 | tf_op jit(solution)/shard_map/ppermute | solution.py:280
  76.6 3.1 %collective-permute-start.7 = (f32[12,8,128]{2,1,0:T(8,128)S(1)}, f32[12,8,128]{2,1,0:T(8,128)S(1)}, u32[]{:S(2)}, u32[]{:S(2)}) collective-permute-start(f32[12,8,128]{2,1,0:T(8,128)S(1)} %get-tuple-element.34), channel_id=1, source_target_pairs={{32,64},{64,32},{96,128},{128,96},{160,192},{192,160},{224,256},{2... | collective-permute-start | bytes 147464 | tf_op jit(solution)/shard_map/ppermute | solution.py:279
  79.6 1.0 collective-permute-done.6.yn_ref
  80.6 4.0 %collective-permute-done.7.yf_ref = f32[12,8,128]{2,1,0:T(8,128)S(1)} collective-permute-done((f32[12,8,128]{2,1,0:T(8,128)S(1)}, f32[12,8,128]{2,1,0:T(8,128)S(1)}, u32[]{:S(2)}, u32[]{:S(2)}) %collective-permute-start.7) | collective-permute-done | bytes 49184 | tf_op jit(solution)/shard_map/ppermute | solution.py:279
  84.7 5.0 %shard_map.59 = (f32[12,24,128]{2,1,0:T(8,128)S(1)}, f32[12,24,128]{2,1,0:T(8,128)S(1)}, f32[2,24,128]{2,1,0:T(8,128)S(1)}, f32[2,24,128]{2,1,0:T(8,128)S(1)}) custom-call(s32[2]{0:T(128)S(1)} %pad_add_fusion.flags, f32[12,24,128]{2,1,0:T(8,128)S(1)} %get-tuple-element.28.est_ref, f32[12,24,128]{2,1,0:T(8,128)S(1)} %get-tuple-element.32.total_ref, ...), custom_call_target="tpu_custom_call" | custom-call | tf_op jit(solution)/shard_map/pallas_call | solution.py:290
  89.6 1.9 %collective-permute-start.8 = (f32[2,24,128]{2,1,0:T(8,128)S(1)}, f32[2,24,128]{2,1,0:T(8,128)S(1)}, u32[]{:S(2)}, u32[]{:S(2)}) collective-permute-start(f32[2,24,128]{2,1,0:T(8,128)S(1)} %get-tuple-element.40), channel_id=1, source_target_pairs={{0,1},{1,0},{2,3},{3,2},{4,5},{5,4},{6,7},{7,6},{8,9},{9,8},{10,11... | collective-permute-start | bytes 73736 | tf_op jit(solution)/shard_map/ppermute | solution.py:280
  91.6 8.5 %collective-permute-start.9 = (f32[2,24,128]{2,1,0:T(8,128)S(1)}, f32[2,24,128]{2,1,0:T(8,128)S(1)}, u32[]{:S(2)}, u32[]{:S(2)}) collective-permute-start(f32[2,24,128]{2,1,0:T(8,128)S(1)} %get-tuple-element.41), channel_id=1, source_target_pairs={{1,2},{2,1},{3,4},{4,3},{5,6},{6,5},{7,8},{8,7},{9,10},{10,9},{11,... | collective-permute-start | bytes 73736 | tf_op jit(solution)/shard_map/ppermute | solution.py:279
  100.1 1.5 %collective-permute-done.9.far_ref = f32[2,24,128]{2,1,0:T(8,128)S(1)} collective-permute-done((f32[2,24,128]{2,1,0:T(8,128)S(1)}, f32[2,24,128]{2,1,0:T(8,128)S(1)}, u32[]{:S(2)}, u32[]{:S(2)}) %collective-permute-start.9) | collective-permute-done | bytes 24608 | tf_op jit(solution)/shard_map/ppermute | solution.py:279
  102.1 1.9 %collective-permute-start.10 = (f32[8,8,128]{2,1,0:T(8,128)S(1)}, f32[8,8,128]{2,1,0:T(8,128)S(1)}, u32[]{:S(2)}, u32[]{:S(2)}) collective-permute-start(f32[8,8,128]{2,1,0:T(8,128)S(1)} %get-tuple-element.43), channel_id=1, source_target_pairs={{0,32},{32,0},{64,96},{96,64},{128,160},{160,128},{192,224},{224,1... | collective-permute-start | bytes 98312 | tf_op jit(solution)/shard_map/ppermute | solution.py:280
  104.1 3.0 %collective-permute-start.11 = (f32[8,8,128]{2,1,0:T(8,128)S(1)}, f32[8,8,128]{2,1,0:T(8,128)S(1)}, u32[]{:S(2)}, u32[]{:S(2)}) collective-permute-start(f32[8,8,128]{2,1,0:T(8,128)S(1)} %get-tuple-element.44), channel_id=1, source_target_pairs={{32,64},{64,32},{96,128},{128,96},{160,192},{192,160},{224,256},{2... | collective-permute-start | bytes 98312 | tf_op jit(solution)/shard_map/ppermute | solution.py:279
  108.0 4.0 %collective-permute-done.11.yf_ref = f32[8,8,128]{2,1,0:T(8,128)S(1)} collective-permute-done((f32[8,8,128]{2,1,0:T(8,128)S(1)}, f32[8,8,128]{2,1,0:T(8,128)S(1)}, u32[]{:S(2)}, u32[]{:S(2)}) %collective-permute-start.11) | collective-permute-done | bytes 32800 | tf_op jit(solution)/shard_map/ppermute | solution.py:279
  112.0 1.2 %shard_map.61 = f32[8,16,128]{2,1,0:T(8,128)} custom-call(s32[2]{0:T(128)S(1)} %pad_add_fusion.flags, f32[12,24,128]{2,1,0:T(8,128)S(1)} %get-tuple-element.38.est_ref, f32[8,24,128]{2,1,0:T(8,128)S(1)} %get-tuple-element.42.total_ref, f32[8,8,128]{2,1,0:T(8,128)S(1)} %collective-permute-done.10.yn_ref, f32[8,8,128]{2,1,0:T(8,128)S(1)} %collective-permute-done.11.yf_ref), custom_call_target="tpu_custom_call" | custom-call | tf_op jit(solution)/shard_map/pallas_call | solution.py:290
  (12 shorter events, 2.9 us)
Async XLA Ops:
  2.3 8.4 %copy-start = (f32[8,16,128]{2,1,0:T(8,128)S(1)}, f32[8,16,128]{2,1,0:T(8,128)}, u32[]{:S(2)}) copy-start(f32[8,16,128]{2,1,0:T(8,128)} %own_ref.1) | copy-start | bytes 196612
  2.3 52.0 %all-to-all-start = ((f32[16,136,128]{2,1,0:T(8,128)}), f32[16,136,128]{2,1,0:T(8,128)S(1)}, u32[]{:S(2)}, u32[]{:S(2)}) async-start(f32[16,136,128]{2,1,0:T(8,128)} %shard_map.56), calls=%async_computation | async-start | bytes 2228224 | tf_op jit(solution)/shard_map/all_to_all | solution.py:328
  10.6 7.8 %collective-permute-start = (f32[8,16,128]{2,1,0:T(8,128)S(1)}, f32[8,16,128]{2,1,0:T(8,128)S(1)}, u32[]{:S(2)}, u32[]{:S(2)}) collective-permute-start(f32[8,16,128]{2,1,0:T(8,128)S(1)} %copy-done), channel_id=1, source_target_pairs={{0,32},{32,0},{64,96},{96,64},{128,160},{160,128},{192,224},{224,1... | collective-permute-start | bytes 196616 | tf_op jit(solution)/shard_map/ppermute | solution.py:280
  14.0 25.2 %collective-permute-start.1 = (f32[8,16,128]{2,1,0:T(8,128)S(1)}, f32[8,16,128]{2,1,0:T(8,128)S(1)}, u32[]{:S(2)}, u32[]{:S(2)}) collective-permute-start(f32[8,16,128]{2,1,0:T(8,128)S(1)} %copy-done), channel_id=1, source_target_pairs={{32,64},{64,32},{96,128},{128,96},{160,192},{192,160},{224,256},{2... | collective-permute-start | bytes 196616 | tf_op jit(solution)/shard_map/ppermute | solution.py:279
  39.8 12.7 %collective-permute-start.2 = (f32[2,24,128]{2,1,0:T(8,128)S(1)}, f32[2,24,128]{2,1,0:T(8,128)S(1)}, u32[]{:S(2)}, u32[]{:S(2)}) collective-permute-start(f32[2,24,128]{2,1,0:T(8,128)S(1)} %get-tuple-element.26), channel_id=1, source_target_pairs={{0,1},{1,0},{2,3},{3,2},{4,5},{5,4},{6,7},{7,6},{8,9},{9,8},{10,11... | collective-permute-start | bytes 73736 | tf_op jit(solution)/shard_map/ppermute | solution.py:280
  41.7 12.6 %collective-permute-start.3 = (f32[2,24,128]{2,1,0:T(8,128)S(1)}, f32[2,24,128]{2,1,0:T(8,128)S(1)}, u32[]{:S(2)}, u32[]{:S(2)}) collective-permute-start(f32[2,24,128]{2,1,0:T(8,128)S(1)} %get-tuple-element.27), channel_id=1, source_target_pairs={{1,2},{2,1},{3,4},{4,3},{5,6},{6,5},{7,8},{8,7},{9,10},{10,9},{11,... | collective-permute-start | bytes 73736 | tf_op jit(solution)/shard_map/ppermute | solution.py:279
  61.8 10.5 %collective-permute-start.4 = (f32[4,24,128]{2,1,0:T(8,128)S(1)}, f32[4,24,128]{2,1,0:T(8,128)S(1)}, u32[]{:S(2)}, u32[]{:S(2)}) collective-permute-start(f32[4,24,128]{2,1,0:T(8,128)S(1)} %get-tuple-element.30), channel_id=1, source_target_pairs={{0,1},{1,0},{2,3},{3,2},{4,5},{5,4},{6,7},{7,6},{8,9},{9,8},{10,11... | collective-permute-start | bytes 147464 | tf_op jit(solution)/shard_map/ppermute | solution.py:280
  63.7 10.4 %collective-permute-start.5 = (f32[4,24,128]{2,1,0:T(8,128)S(1)}, f32[4,24,128]{2,1,0:T(8,128)S(1)}, u32[]{:S(2)}, u32[]{:S(2)}) collective-permute-start(f32[4,24,128]{2,1,0:T(8,128)S(1)} %get-tuple-element.31), channel_id=1, source_target_pairs={{1,2},{2,1},{3,4},{4,3},{5,6},{6,5},{7,8},{8,7},{9,10},{10,9},{11,... | collective-permute-start | bytes 147464 | tf_op jit(solution)/shard_map/ppermute | solution.py:279
  74.6 6.0 %collective-permute-start.6 = (f32[12,8,128]{2,1,0:T(8,128)S(1)}, f32[12,8,128]{2,1,0:T(8,128)S(1)}, u32[]{:S(2)}, u32[]{:S(2)}) collective-permute-start(f32[12,8,128]{2,1,0:T(8,128)S(1)} %get-tuple-element.33), channel_id=1, source_target_pairs={{0,32},{32,0},{64,96},{96,64},{128,160},{160,128},{192,224},{224,1... | collective-permute-start | bytes 147464 | tf_op jit(solution)/shard_map/ppermute | solution.py:280
  76.6 8.1 %collective-permute-start.7 = (f32[12,8,128]{2,1,0:T(8,128)S(1)}, f32[12,8,128]{2,1,0:T(8,128)S(1)}, u32[]{:S(2)}, u32[]{:S(2)}) collective-permute-start(f32[12,8,128]{2,1,0:T(8,128)S(1)} %get-tuple-element.34), channel_id=1, source_target_pairs={{32,64},{64,32},{96,128},{128,96},{160,192},{192,160},{224,256},{2... | collective-permute-start | bytes 147464 | tf_op jit(solution)/shard_map/ppermute | solution.py:279
  89.6 10.4 %collective-permute-start.8 = (f32[2,24,128]{2,1,0:T(8,128)S(1)}, f32[2,24,128]{2,1,0:T(8,128)S(1)}, u32[]{:S(2)}, u32[]{:S(2)}) collective-permute-start(f32[2,24,128]{2,1,0:T(8,128)S(1)} %get-tuple-element.40), channel_id=1, source_target_pairs={{0,1},{1,0},{2,3},{3,2},{4,5},{5,4},{6,7},{7,6},{8,9},{9,8},{10,11... | collective-permute-start | bytes 73736 | tf_op jit(solution)/shard_map/ppermute | solution.py:280
  91.6 10.0 %collective-permute-start.9 = (f32[2,24,128]{2,1,0:T(8,128)S(1)}, f32[2,24,128]{2,1,0:T(8,128)S(1)}, u32[]{:S(2)}, u32[]{:S(2)}) collective-permute-start(f32[2,24,128]{2,1,0:T(8,128)S(1)} %get-tuple-element.41), channel_id=1, source_target_pairs={{1,2},{2,1},{3,4},{4,3},{5,6},{6,5},{7,8},{8,7},{9,10},{10,9},{11,... | collective-permute-start | bytes 73736 | tf_op jit(solution)/shard_map/ppermute | solution.py:279
  102.1 5.8 %collective-permute-start.10 = (f32[8,8,128]{2,1,0:T(8,128)S(1)}, f32[8,8,128]{2,1,0:T(8,128)S(1)}, u32[]{:S(2)}, u32[]{:S(2)}) collective-permute-start(f32[8,8,128]{2,1,0:T(8,128)S(1)} %get-tuple-element.43), channel_id=1, source_target_pairs={{0,32},{32,0},{64,96},{96,64},{128,160},{160,128},{192,224},{224,1... | collective-permute-start | bytes 98312 | tf_op jit(solution)/shard_map/ppermute | solution.py:280
  104.1 7.9 %collective-permute-start.11 = (f32[8,8,128]{2,1,0:T(8,128)S(1)}, f32[8,8,128]{2,1,0:T(8,128)S(1)}, u32[]{:S(2)}, u32[]{:S(2)}) collective-permute-start(f32[8,8,128]{2,1,0:T(8,128)S(1)} %get-tuple-element.44), channel_id=1, source_target_pairs={{32,64},{64,32},{96,128},{128,96},{160,192},{192,160},{224,256},{2... | collective-permute-start | bytes 98312 | tf_op jit(solution)/shard_map/ppermute | solution.py:279

commit v9 on v8

--- a/solution.py
+++ b/solution.py
@@ -80,7 +80,7 @@
         copy.wait()
 
 
-def make_tables(sizes, data_ref, table_ref, axial):
+def make_tables(sizes, data_ref, conv_ref, corr_ref, table_ref, axial):
     _, _, nz = sizes
     views = data_ref.shape[0]
     lane = lax.broadcasted_iota(jnp.int32, (8, LANES), 1)
@@ -95,6 +95,8 @@
     )
 
     def one(v, carry):
+        for at, ref in ((0, conv_ref), (views, corr_ref)):
+            banded(axial[pl.ds(at + v, 1), :], nz // 2, ref.at[v])
         start = 0
         for row in (1, 2):
             taps = jnp.broadcast_to(data_ref[v, BLOCK + row : BLOCK + row + 1, :], (8, LANES))
@@ -110,7 +112,7 @@
     return jnp.broadcast_to(table_ref[v, pl.ds(k, 1), :], (8, LANES))
 
 
-def conv_part(sizes, est_ref, conv_ref, table_ref, spread, prepare, finish):
+def conv_part(sizes, est_ref, conv_ref, table_ref, spread, finish):
     nf, ns, _ = sizes
     wide, views = est_ref.shape[0], conv_ref.shape[0]
 
@@ -130,7 +132,6 @@
     lax.fori_loop(0, wide, row, 0)
 
     def one(v, carry):
-        prepare(v)
         first = [tap(table_ref, v, k) for k in range(nf)]
         out = []
         for i in range(ROWS):
@@ -145,13 +146,12 @@
     lax.fori_loop(0, views, one, 0, unroll=2)
 
 
-def corr_part(sizes, flags, ratio_of, corr_ref, table_ref, spread, part_ref, near_ref, far_ref, prepare):
+def corr_part(sizes, flags, ratio_of, corr_ref, table_ref, spread, part_ref, near_ref, far_ref):
     nf, ns, _ = sizes
     wide, views = spread.shape[1], spread.shape[0]
 
     def one(v, carry):
         first = [tap(table_ref, v, k) for k in range(nf)]
-        prepare(v)
         back = product(ratio_of(v), corr_ref[v])
         for i in range(wide):
             for h in range(2):
@@ -197,14 +197,14 @@
     return jnp.where(even, far, near), jnp.where(even, near, far)
 
 
-def both_parts(sizes, flags, est_ref, data_ref, conv_ref, corr_ref, table_ref, part_ref, near_ref, far_ref, spread, ratio, prepare=lambda v: None, prepare_corr=lambda v: None):
+def both_parts(sizes, flags, est_ref, data_ref, conv_ref, corr_ref, table_ref, part_ref, near_ref, far_ref, spread, ratio):
     def finish(v, blurred):
         ratio[v] = data_ref[v, 0:BLOCK, :] / blurred
 
-    conv_part(sizes, est_ref, conv_ref, table_ref, spread, prepare, finish)
+    conv_part(sizes, est_ref, conv_ref, table_ref, spread, finish)
     corr_part(
         sizes, flags, lambda v: ratio[v],
-        corr_ref, table_ref, spread, part_ref, near_ref, far_ref, prepare_corr,
+        corr_ref, table_ref, spread, part_ref, near_ref, far_ref,
     )
 
 
@@ -219,20 +219,13 @@
 
 
 def first_kernel(sizes, flags, own_ref, xn_ref, xf_ref, data_ref, est_ref, part_ref, near_ref, far_ref, conv_ref, corr_ref, table_ref, spread, ratio, axial):
-    make_tables(sizes, data_ref, table_ref, axial)
+    make_tables(sizes, data_ref, conv_ref, corr_ref, table_ref, axial)
     low, high = sides(flags[0], xn_ref, xf_ref)
     strip = low.shape[0]
     est_ref[0:strip] = low
     est_ref[strip : strip + ROWS] = own_ref[...]
     est_ref[strip + ROWS :] = high
-
-    def prepare(v):
-        banded(axial[pl.ds(v, 1), :], sizes[2] // 2, conv_ref.at[v])
-
-    def prepare_corr(v):
-        banded(axial[pl.ds(data_ref.shape[0] + v, 1), :], sizes[2] // 2, corr_ref.at[v])
-
-    both_parts(sizes, flags, est_ref, data_ref, conv_ref, corr_ref, table_ref, part_ref, near_ref, far_ref, spread, ratio, prepare, prepare_corr)
+    both_parts(sizes, flags, est_ref, data_ref, conv_ref, corr_ref, table_ref, part_ref, near_ref, far_ref, spread, ratio)
 
 
 def updated(views, flags, est_ref, total_ref, yn_ref, yf_ref, new_ref):

time: 114 us -> 113 us (level)
  transfers between devices with their start and end apart: 13 -> 13, of which waited for: 9 -> 9; matrix products, arithmetic and copies ran while one was open for 0% -> 0% of each run, Pallas kernels for 0% -> 1%
where the time goes in v9:
time: 113 us; the launch traced here: 112 us
  starting transfers between devices  59.9 us (53%)
  waiting for transfers between devices  35 us (31%)
  Pallas kernels  17 us (15%)
    ppermute x6, starting transfers between devices, swapped(): far = lax.ppermute(far, axis, pairs(count, 1))  38.6 us
    ppermute x6, waiting for transfers between devices, swapped(): far = lax.ppermute(far, axis, pairs(count, 1))  33.6 us
    pallas_call x6, Pallas kernels, call(): pl.pallas_call(kernel, in_specs=[SMEM] + [VMEM] * (len(ins) - 1), out_spe...  14.8 us
    ppermute x6, starting transfers between devices, swapped(): near = lax.ppermute(near, axis, pairs(count, 0))  13 us
    all_to_all x1, starting transfers between devices, local(): data = lax.all_to_all(data, 'view', 0, 0, tiled=True)  8.34 us
    pallas_call x1, Pallas kernels, local(): pl.pallas_call(pieces_kernel, in_specs=[hbm] * 4, out_specs=hbm, out_shap...  2.27 us
  transfers between devices with their start and end apart: 13, of which 9 were waited for; matrix products, arithmetic and copies ran while one was open for 0% of the time, Pallas kernels for 1%

profile of v9, /device:TPU:70, one launch (start us, length us, event | category | flops | bytes accessed | tf_op | source)
XLA Modules:
  0.0 112.2 jit_solution(5650543784640098297)
XLA Ops:
  0.0 2.3 %shard_map.56 = f32[16,136,128]{2,1,0:T(8,128)} custom-call(f32[8,16,16,128]{3,2,1,0:T(8,128)} %bitcast.3, f32[1,33]{1,0:T(1,128)} %axial_ref.1, f32[1,5]{1,0:T(1,128)} %first_ref.1, f32[1,7]{1,0:T(1,128)} %second_ref.1), custom_call_target="tpu_custom_call" | custom-call | tf_op jit(solution)/shard_map/pallas_call | solution.py:306
  2.3 8.3 %all-to-all-start = ((f32[16,136,128]{2,1,0:T(8,128)}), f32[16,136,128]{2,1,0:T(8,128)S(1)}, u32[]{:S(2)}, u32[]{:S(2)}) async-start(f32[16,136,128]{2,1,0:T(8,128)} %shard_map.56), calls=%async_computation | async-start | bytes 2228224 | tf_op jit(solution)/shard_map/all_to_all | solution.py:321
  10.6 3.4 %collective-permute-start = (f32[8,16,128]{2,1,0:T(8,128)S(1)}, f32[8,16,128]{2,1,0:T(8,128)S(1)}, u32[]{:S(2)}, u32[]{:S(2)}) collective-permute-start(f32[8,16,128]{2,1,0:T(8,128)S(1)} %copy-done), channel_id=1, source_target_pairs={{0,32},{32,0},{64,96},{96,64},{128,160},{160,128},{192,224},{224,1... | collective-permute-start | bytes 196616 | tf_op jit(solution)/shard_map/ppermute | solution.py:273
  14.0 4.0 %collective-permute-start.1 = (f32[8,16,128]{2,1,0:T(8,128)S(1)}, f32[8,16,128]{2,1,0:T(8,128)S(1)}, u32[]{:S(2)}, u32[]{:S(2)}) collective-permute-start(f32[8,16,128]{2,1,0:T(8,128)S(1)} %copy-done), channel_id=1, source_target_pairs={{32,64},{64,32},{96,128},{128,96},{160,192},{192,160},{224,256},{2... | collective-permute-start | bytes 196616 | tf_op jit(solution)/shard_map/ppermute | solution.py:272
  18.4 20.8 %collective-permute-done.1.yf_ref = f32[8,16,128]{2,1,0:T(8,128)S(1)} collective-permute-done((f32[8,16,128]{2,1,0:T(8,128)S(1)}, f32[8,16,128]{2,1,0:T(8,128)S(1)}, u32[]{:S(2)}, u32[]{:S(2)}) %collective-permute-start.1) | collective-permute-done | bytes 65568 | tf_op jit(solution)/shard_map/ppermute | solution.py:272
  39.8 1.9 %collective-permute-start.2 = (f32[2,24,128]{2,1,0:T(8,128)S(1)}, f32[2,24,128]{2,1,0:T(8,128)S(1)}, u32[]{:S(2)}, u32[]{:S(2)}) collective-permute-start(f32[2,24,128]{2,1,0:T(8,128)S(1)} %get-tuple-element.26), channel_id=1, source_target_pairs={{0,1},{1,0},{2,3},{3,2},{4,5},{5,4},{6,7},{7,6},{8,9},{9,8},{10,11... | collective-permute-start | bytes 73736 | tf_op jit(solution)/shard_map/ppermute | solution.py:273
  41.7 10.8 %collective-permute-start.3 = (f32[2,24,128]{2,1,0:T(8,128)S(1)}, f32[2,24,128]{2,1,0:T(8,128)S(1)}, u32[]{:S(2)}, u32[]{:S(2)}) collective-permute-start(f32[2,24,128]{2,1,0:T(8,128)S(1)} %get-tuple-element.27), channel_id=1, source_target_pairs={{1,2},{2,1},{3,4},{4,3},{5,6},{6,5},{7,8},{8,7},{9,10},{10,9},{11,... | collective-permute-start | bytes 73736 | tf_op jit(solution)/shard_map/ppermute | solution.py:272
  52.5 1.5 %collective-permute-done.3.xf_ref = f32[2,24,128]{2,1,0:T(8,128)S(1)} collective-permute-done((f32[2,24,128]{2,1,0:T(8,128)S(1)}, f32[2,24,128]{2,1,0:T(8,128)S(1)}, u32[]{:S(2)}, u32[]{:S(2)}) %collective-permute-start.3) | collective-permute-done | bytes 24608 | tf_op jit(solution)/shard_map/ppermute | solution.py:272
  54.0 6.9 %shard_map.57 = (f32[12,24,128]{2,1,0:T(8,128)S(1)}, f32[12,24,128]{2,1,0:T(8,128)S(1)}, f32[4,24,128]{2,1,0:T(8,128)S(1)}, f32[4,24,128]{2,1,0:T(8,128)S(1)}, b...) custom-call(s32[2]{0:T(128)S(1)} %pad_add_fusion.flags, ...), custom_call_target="tpu_custom_call" | custom-call | tf_op jit(solution)/shard_map/pallas_call | solution.py:283
  60.9 1.9 %collective-permute-start.4 = (f32[4,24,128]{2,1,0:T(8,128)S(1)}, f32[4,24,128]{2,1,0:T(8,128)S(1)}, u32[]{:S(2)}, u32[]{:S(2)}) collective-permute-start(f32[4,24,128]{2,1,0:T(8,128)S(1)} %get-tuple-element.30), channel_id=1, source_target_pairs={{0,1},{1,0},{2,3},{3,2},{4,5},{5,4},{6,7},{7,6},{8,9},{9,8},{10,11... | collective-permute-start | bytes 147464 | tf_op jit(solution)/shard_map/ppermute | solution.py:273
  62.8 8.4 %collective-permute-start.5 = (f32[4,24,128]{2,1,0:T(8,128)S(1)}, f32[4,24,128]{2,1,0:T(8,128)S(1)}, u32[]{:S(2)}, u32[]{:S(2)}) collective-permute-start(f32[4,24,128]{2,1,0:T(8,128)S(1)} %get-tuple-element.31), channel_id=1, source_target_pairs={{1,2},{2,1},{3,4},{4,3},{5,6},{6,5},{7,8},{8,7},{9,10},{10,9},{11,... | collective-permute-start | bytes 147464 | tf_op jit(solution)/shard_map/ppermute | solution.py:272
  71.3 1.7 %collective-permute-done.5.far_ref = f32[4,24,128]{2,1,0:T(8,128)S(1)} collective-permute-done((f32[4,24,128]{2,1,0:T(8,128)S(1)}, f32[4,24,128]{2,1,0:T(8,128)S(1)}, u32[]{:S(2)}, u32[]{:S(2)}) %collective-permute-start.5) | collective-permute-done | bytes 49184 | tf_op jit(solution)/shard_map/ppermute | solution.py:272
  73.6 1.9 %collective-permute-start.6 = (f32[12,8,128]{2,1,0:T(8,128)S(1)}, f32[12,8,128]{2,1,0:T(8,128)S(1)}, u32[]{:S(2)}, u32[]{:S(2)}) collective-permute-start(f32[12,8,128]{2,1,0:T(8,128)S(1)} %get-tuple-element.33), channel_id=1, source_target_pairs={{0,32},{32,0},{64,96},{96,64},{128,160},{160,128},{192,224},{224,1... | collective-permute-start | bytes 147464 | tf_op jit(solution)/shard_map/ppermute | solution.py:273
  75.6 3.4 %collective-permute-start.7 = (f32[12,8,128]{2,1,0:T(8,128)S(1)}, f32[12,8,128]{2,1,0:T(8,128)S(1)}, u32[]{:S(2)}, u32[]{:S(2)}) collective-permute-start(f32[12,8,128]{2,1,0:T(8,128)S(1)} %get-tuple-element.34), channel_id=1, source_target_pairs={{32,64},{64,32},{96,128},{128,96},{160,192},{192,160},{224,256},{2... | collective-permute-start | bytes 147464 | tf_op jit(solution)/shard_map/ppermute | solution.py:272
  79.0 0.6 collective-permute-done.6.yn_ref
  79.6 4.0 %collective-permute-done.7.yf_ref = f32[12,8,128]{2,1,0:T(8,128)S(1)} collective-permute-done((f32[12,8,128]{2,1,0:T(8,128)S(1)}, f32[12,8,128]{2,1,0:T(8,128)S(1)}, u32[]{:S(2)}, u32[]{:S(2)}) %collective-permute-start.7) | collective-permute-done | bytes 49184 | tf_op jit(solution)/shard_map/ppermute | solution.py:272
  83.7 5.0 %shard_map.59 = (f32[12,24,128]{2,1,0:T(8,128)S(1)}, f32[12,24,128]{2,1,0:T(8,128)S(1)}, f32[2,24,128]{2,1,0:T(8,128)S(1)}, f32[2,24,128]{2,1,0:T(8,128)S(1)}) custom-call(s32[2]{0:T(128)S(1)} %pad_add_fusion.flags, f32[12,24,128]{2,1,0:T(8,128)S(1)} %get-tuple-element.28.est_ref, f32[12,24,128]{2,1,0:T(8,128)S(1)} %get-tuple-element.32.total_ref, ...), custom_call_target="tpu_custom_call" | custom-call | tf_op jit(solution)/shard_map/pallas_call | solution.py:283
  88.7 1.9 %collective-permute-start.8 = (f32[2,24,128]{2,1,0:T(8,128)S(1)}, f32[2,24,128]{2,1,0:T(8,128)S(1)}, u32[]{:S(2)}, u32[]{:S(2)}) collective-permute-start(f32[2,24,128]{2,1,0:T(8,128)S(1)} %get-tuple-element.40), channel_id=1, source_target_pairs={{0,1},{1,0},{2,3},{3,2},{4,5},{5,4},{6,7},{7,6},{8,9},{9,8},{10,11... | collective-permute-start | bytes 73736 | tf_op jit(solution)/shard_map/ppermute | solution.py:273
  90.6 8.5 %collective-permute-start.9 = (f32[2,24,128]{2,1,0:T(8,128)S(1)}, f32[2,24,128]{2,1,0:T(8,128)S(1)}, u32[]{:S(2)}, u32[]{:S(2)}) collective-permute-start(f32[2,24,128]{2,1,0:T(8,128)S(1)} %get-tuple-element.41), channel_id=1, source_target_pairs={{1,2},{2,1},{3,4},{4,3},{5,6},{6,5},{7,8},{8,7},{9,10},{10,9},{11,... | collective-permute-start | bytes 73736 | tf_op jit(solution)/shard_map/ppermute | solution.py:272
  99.1 1.5 %collective-permute-done.9.far_ref = f32[2,24,128]{2,1,0:T(8,128)S(1)} collective-permute-done((f32[2,24,128]{2,1,0:T(8,128)S(1)}, f32[2,24,128]{2,1,0:T(8,128)S(1)}, u32[]{:S(2)}, u32[]{:S(2)}) %collective-permute-start.9) | collective-permute-done | bytes 24608 | tf_op jit(solution)/shard_map/ppermute | solution.py:272
  101.2 1.9 %collective-permute-start.10 = (f32[8,8,128]{2,1,0:T(8,128)S(1)}, f32[8,8,128]{2,1,0:T(8,128)S(1)}, u32[]{:S(2)}, u32[]{:S(2)}) collective-permute-start(f32[8,8,128]{2,1,0:T(8,128)S(1)} %get-tuple-element.43), channel_id=1, source_target_pairs={{0,32},{32,0},{64,96},{96,64},{128,160},{160,128},{192,224},{224,1... | collective-permute-start | bytes 98312 | tf_op jit(solution)/shard_map/ppermute | solution.py:273
  103.1 3.4 %collective-permute-start.11 = (f32[8,8,128]{2,1,0:T(8,128)S(1)}, f32[8,8,128]{2,1,0:T(8,128)S(1)}, u32[]{:S(2)}, u32[]{:S(2)}) collective-permute-start(f32[8,8,128]{2,1,0:T(8,128)S(1)} %get-tuple-element.44), channel_id=1, source_target_pairs={{32,64},{64,32},{96,128},{128,96},{160,192},{192,160},{224,256},{2... | collective-permute-start | bytes 98312 | tf_op jit(solution)/shard_map/ppermute | solution.py:272
  107.0 4.0 %collective-permute-done.11.yf_ref = f32[8,8,128]{2,1,0:T(8,128)S(1)} collective-permute-done((f32[8,8,128]{2,1,0:T(8,128)S(1)}, f32[8,8,128]{2,1,0:T(8,128)S(1)}, u32[]{:S(2)}, u32[]{:S(2)}) %collective-permute-start.11) | collective-permute-done | bytes 32800 | tf_op jit(solution)/shard_map/ppermute | solution.py:272
  111.0 1.2 %shard_map.61 = f32[8,16,128]{2,1,0:T(8,128)} custom-call(s32[2]{0:T(128)S(1)} %pad_add_fusion.flags, f32[12,24,128]{2,1,0:T(8,128)S(1)} %get-tuple-element.38.est_ref, f32[8,24,128]{2,1,0:T(8,128)S(1)} %get-tuple-element.42.total_ref, f32[8,8,128]{2,1,0:T(8,128)S(1)} %collective-permute-done.10.yn_ref, f32[8,8,128]{2,1,0:T(8,128)S(1)} %collective-permute-done.11.yf_ref), custom_call_target="tpu_custom_call" | custom-call | tf_op jit(solution)/shard_map/pallas_call | solution.py:283
  (12 shorter events, 2.6 us)
Async XLA Ops:
  2.3 8.4 %copy-start = (f32[8,16,128]{2,1,0:T(8,128)S(1)}, f32[8,16,128]{2,1,0:T(8,128)}, u32[]{:S(2)}) copy-start(f32[8,16,128]{2,1,0:T(8,128)} %own_ref.1) | copy-start | bytes 196612
  2.3 51.7 %all-to-all-start = ((f32[16,136,128]{2,1,0:T(8,128)}), f32[16,136,128]{2,1,0:T(8,128)S(1)}, u32[]{:S(2)}, u32[]{:S(2)}) async-start(f32[16,136,128]{2,1,0:T(8,128)} %shard_map.56), calls=%async_computation | async-start | bytes 2228224 | tf_op jit(solution)/shard_map/all_to_all | solution.py:321
  10.6 7.8 %collective-permute-start = (f32[8,16,128]{2,1,0:T(8,128)S(1)}, f32[8,16,128]{2,1,0:T(8,128)S(1)}, u32[]{:S(2)}, u32[]{:S(2)}) collective-permute-start(f32[8,16,128]{2,1,0:T(8,128)S(1)} %copy-done), channel_id=1, source_target_pairs={{0,32},{32,0},{64,96},{96,64},{128,160},{160,128},{192,224},{224,1... | collective-permute-start | bytes 196616 | tf_op jit(solution)/shard_map/ppermute | solution.py:273
  14.0 25.2 %collective-permute-start.1 = (f32[8,16,128]{2,1,0:T(8,128)S(1)}, f32[8,16,128]{2,1,0:T(8,128)S(1)}, u32[]{:S(2)}, u32[]{:S(2)}) collective-permute-start(f32[8,16,128]{2,1,0:T(8,128)S(1)} %copy-done), channel_id=1, source_target_pairs={{32,64},{64,32},{96,128},{128,96},{160,192},{192,160},{224,256},{2... | collective-permute-start | bytes 196616 | tf_op jit(solution)/shard_map/ppermute | solution.py:272
  39.8 12.7 %collective-permute-start.2 = (f32[2,24,128]{2,1,0:T(8,128)S(1)}, f32[2,24,128]{2,1,0:T(8,128)S(1)}, u32[]{:S(2)}, u32[]{:S(2)}) collective-permute-start(f32[2,24,128]{2,1,0:T(8,128)S(1)} %get-tuple-element.26), channel_id=1, source_target_pairs={{0,1},{1,0},{2,3},{3,2},{4,5},{5,4},{6,7},{7,6},{8,9},{9,8},{10,11... | collective-permute-start | bytes 73736 | tf_op jit(solution)/shard_map/ppermute | solution.py:273
  41.7 12.3 %collective-permute-start.3 = (f32[2,24,128]{2,1,0:T(8,128)S(1)}, f32[2,24,128]{2,1,0:T(8,128)S(1)}, u32[]{:S(2)}, u32[]{:S(2)}) collective-permute-start(f32[2,24,128]{2,1,0:T(8,128)S(1)} %get-tuple-element.27), channel_id=1, source_target_pairs={{1,2},{2,1},{3,4},{4,3},{5,6},{6,5},{7,8},{8,7},{9,10},{10,9},{11,... | collective-permute-start | bytes 73736 | tf_op jit(solution)/shard_map/ppermute | solution.py:272
  60.9 10.4 %collective-permute-start.4 = (f32[4,24,128]{2,1,0:T(8,128)S(1)}, f32[4,24,128]{2,1,0:T(8,128)S(1)}, u32[]{:S(2)}, u32[]{:S(2)}) collective-permute-start(f32[4,24,128]{2,1,0:T(8,128)S(1)} %get-tuple-element.30), channel_id=1, source_target_pairs={{0,1},{1,0},{2,3},{3,2},{4,5},{5,4},{6,7},{7,6},{8,9},{9,8},{10,11... | collective-permute-start | bytes 147464 | tf_op jit(solution)/shard_map/ppermute | solution.py:273
  62.8 10.2 %collective-permute-start.5 = (f32[4,24,128]{2,1,0:T(8,128)S(1)}, f32[4,24,128]{2,1,0:T(8,128)S(1)}, u32[]{:S(2)}, u32[]{:S(2)}) collective-permute-start(f32[4,24,128]{2,1,0:T(8,128)S(1)} %get-tuple-element.31), channel_id=1, source_target_pairs={{1,2},{2,1},{3,4},{4,3},{5,6},{6,5},{7,8},{8,7},{9,10},{10,9},{11,... | collective-permute-start | bytes 147464 | tf_op jit(solution)/shard_map/ppermute | solution.py:272
  73.6 6.0 %collective-permute-start.6 = (f32[12,8,128]{2,1,0:T(8,128)S(1)}, f32[12,8,128]{2,1,0:T(8,128)S(1)}, u32[]{:S(2)}, u32[]{:S(2)}) collective-permute-start(f32[12,8,128]{2,1,0:T(8,128)S(1)} %get-tuple-element.33), channel_id=1, source_target_pairs={{0,32},{32,0},{64,96},{96,64},{128,160},{160,128},{192,224},{224,1... | collective-permute-start | bytes 147464 | tf_op jit(solution)/shard_map/ppermute | solution.py:273
  75.6 8.1 %collective-permute-start.7 = (f32[12,8,128]{2,1,0:T(8,128)S(1)}, f32[12,8,128]{2,1,0:T(8,128)S(1)}, u32[]{:S(2)}, u32[]{:S(2)}) collective-permute-start(f32[12,8,128]{2,1,0:T(8,128)S(1)} %get-tuple-element.34), channel_id=1, source_target_pairs={{32,64},{64,32},{96,128},{128,96},{160,192},{192,160},{224,256},{2... | collective-permute-start | bytes 147464 | tf_op jit(solution)/shard_map/ppermute | solution.py:272
  88.7 10.4 %collective-permute-start.8 = (f32[2,24,128]{2,1,0:T(8,128)S(1)}, f32[2,24,128]{2,1,0:T(8,128)S(1)}, u32[]{:S(2)}, u32[]{:S(2)}) collective-permute-start(f32[2,24,128]{2,1,0:T(8,128)S(1)} %get-tuple-element.40), channel_id=1, source_target_pairs={{0,1},{1,0},{2,3},{3,2},{4,5},{5,4},{6,7},{7,6},{8,9},{9,8},{10,11... | collective-permute-start | bytes 73736 | tf_op jit(solution)/shard_map/ppermute | solution.py:273
  90.6 10.0 %collective-permute-start.9 = (f32[2,24,128]{2,1,0:T(8,128)S(1)}, f32[2,24,128]{2,1,0:T(8,128)S(1)}, u32[]{:S(2)}, u32[]{:S(2)}) collective-permute-start(f32[2,24,128]{2,1,0:T(8,128)S(1)} %get-tuple-element.41), channel_id=1, source_target_pairs={{1,2},{2,1},{3,4},{4,3},{5,6},{6,5},{7,8},{8,7},{9,10},{10,9},{11,... | collective-permute-start | bytes 73736 | tf_op jit(solution)/shard_map/ppermute | solution.py:272
  101.2 5.8 %collective-permute-start.10 = (f32[8,8,128]{2,1,0:T(8,128)S(1)}, f32[8,8,128]{2,1,0:T(8,128)S(1)}, u32[]{:S(2)}, u32[]{:S(2)}) collective-permute-start(f32[8,8,128]{2,1,0:T(8,128)S(1)} %get-tuple-element.43), channel_id=1, source_target_pairs={{0,32},{32,0},{64,96},{96,64},{128,160},{160,128},{192,224},{224,1... | collective-permute-start | bytes 98312 | tf_op jit(solution)/shard_map/ppermute | solution.py:273
  103.1 7.9 %collective-permute-start.11 = (f32[8,8,128]{2,1,0:T(8,128)S(1)}, f32[8,8,128]{2,1,0:T(8,128)S(1)}, u32[]{:S(2)}, u32[]{:S(2)}) collective-permute-start(f32[8,8,128]{2,1,0:T(8,128)S(1)} %get-tuple-element.44), channel_id=1, source_target_pairs={{32,64},{64,32},{96,128},{128,96},{160,192},{192,160},{224,256},{2... | collective-permute-start | bytes 98312 | tf_op jit(solution)/shard_map/ppermute | solution.py:272
